TPU v7x, 128 devices: a whole 4x4x4 slice. The times are simulated.
128 devices in a mesh: dp: 16 (over y, x), tensor: 8 (over z, core).
Axes of the slice: x: 4, y: 4, z: 4, core: 2. Of those that a mesh axis runs over, the one named last changes fastest.
Arguments:
- tokens: bfloat16 [16384, 1536], P('dp'), may hold values from -6 to 6
- teacher_feats: bfloat16 [16384, 256], P('dp'), may hold values from -12 to 12
- masks: int32 [64, 256], P('dp'), may hold values from 0 to 1, as said below
- w_in: bfloat16 [1536, 2048], P('dp'), may hold values from -0.15625 to 0.15625
- w_out: bfloat16 [2048, 256], P('dp'), may hold values from -0.125 to 0.125
- proto_student: bfloat16 [256, 131072], P(None, ('dp', 'tensor')), may hold values from -0.375 to 0.375
- proto_teacher: bfloat16 [256, 131072], P(None, ('dp', 'tensor')), may hold values from -1 to 1
Outputs:
- d_tokens: bfloat16 [16384, 1536], P('dp')
- grad_in: float32 [1536, 2048], P('dp')
- grad_out: float32 [2048, 256], P('dp')
- grad_proto: float32 [256, 131072], P(None, ('dp', 'tensor'))
- crop_loss: float32 [64], P('dp')
Inputs may be any that keep to these rules, and one draw needn't show every extreme that they name: `masks`: the crops of one index of dp hold 256 or fewer masked patches together, exactly 256 on some index; a crop holds at most 129.
All inputs are finite; a program needn't handle non-finite values.
Results may differ from a plain program's by a relative error of at most 0.02.
Values may be sent and summed in bfloat16 or wider, within the bound.
No kernel may reach another device: no remote copies, remote signals or barrier semaphores. Data moves between devices by JAX's collectives and lax.ppermute only.
A program may use at most 192 MiB of HBM per device.

v0:
```python
import jax
import jax.numpy as jnp
from jax import lax
from jax.experimental import pallas as pl
from jax.experimental.pallas import tpu as pltpu
from jax.sharding import PartitionSpec as P

CAP = 256
TEACHER_TEMP = 0.07
STUDENT_TEMP = 0.1
EPS = 1e-06
GRAD_SCALE = 65536.0
INTERPRET = False
f32, bf16 = (jnp.float32, jnp.bfloat16)
VMEM = pl.BlockSpec(memory_space=pltpu.VMEM)
HBM = pl.BlockSpec(memory_space=pl.ANY)
SMEM = pl.BlockSpec(memory_space=pltpu.SMEM)
NT = (((1,), (1,)), ((), ()))
TN = (((0,), (0,)), ((), ()))
EXTRA = 16
HALF = CAP // 2
LINES = CAP + EXTRA


def mm(a, b, dims=None):
    if dims is None:
        return jnp.dot(a, b, preferred_element_type=f32)
    return lax.dot_general(a, b, dims, preferred_element_type=f32)


def call(body, outs, ins, out_specs=None, in_specs=None, scratch=()):
    outs = tuple(jax.ShapeDtypeStruct(s, d) for s, d in outs)
    return pl.pallas_call(
        body,
        out_shape=outs,
        in_specs=in_specs or [VMEM] * len(ins),
        out_specs=tuple(out_specs or [VMEM] * len(outs)),
        scratch_shapes=list(scratch),
        interpret=INTERPRET,
        compiler_params=pltpu.CompilerParams(vmem_limit_bytes=48 << 20),
    )(*ins)


def iota(shape, dim):
    return lax.broadcasted_iota(jnp.int32, shape, dim)


def copies(pairs, sems):
    return [pltpu.make_async_copy(a, b, sems.at[i]) for i, (a, b) in enumerate(pairs)]


GROUP = 4
UNROLL = 4


def group(ref, q):
    return ref.at[pl.ds(q * GROUP, GROUP)]


def start_all(number, make):
    def go(i, _):
        make(i).start()
        return 0

    lax.fori_loop(0, number, go, 0)


def wait_all(number, make):
    def go(i, _):
        make(i).wait()
        return 0

    lax.fori_loop(0, number, go, 0)


def over_groups(peers, step, loads=(), stores=(), unroll=1):
    def go(q, _):
        for make in loads:
            make(q).wait()
        lax.fori_loop(0, GROUP, lambda i, _: step(q * GROUP + i), 0, unroll=unroll)
        for make in stores:
            make(q).start()
        return 0

    lax.fori_loop(0, peers // GROUP, go, 0)


def select_body(at_ref, mask_ref, feats_ref, sel_ref, send_hbm, member_ref, mine_ref, unit_ref, pack_ref, sems):
    crops, patches = mask_ref.shape
    mask = mask_ref[...].astype(f32)
    upto = (iota((patches, patches), 0) <= iota((patches, patches), 1)).astype(f32).astype(bf16)
    rank = mm(mask.astype(bf16), upto)
    count = jnp.sum(mask, axis=1, keepdims=True)
    total = jnp.sum(count, axis=0, keepdims=True)
    slot = iota((CAP, patches), 0).astype(f32)
    lane = iota((1, CAP), 1).astype(f32)
    start = jnp.zeros((1, 1), f32)
    weight = jnp.zeros((1, CAP), f32)
    first = iota((CAP, patches), 1) == 0
    member_ref[...] = jnp.zeros_like(member_ref)
    for c in range(crops):
        hit = jnp.where((rank[c : c + 1] + start == slot + 1.0) & (mask[c : c + 1] > 0.0), 1.0, 0.0)
        if c == 0:
            hit = jnp.where(first & (slot >= total), 1.0, hit)
        sel_ref[:, c * patches : (c + 1) * patches] = hit.astype(bf16)
        own = count[c : c + 1]
        inside = jnp.where((lane >= start) & (lane < start + own), 1.0, 0.0)
        part = inside * (1.0 / jnp.maximum(own, 1.0))
        member_ref[c : c + 1, :] = part
        weight = weight + part
        start = start + own
    live = jnp.where(lane < total, 1.0, 0.0)
    picked = mm(sel_ref[...], feats_ref[...])
    scale = lax.rsqrt(jnp.sum(picked * picked, axis=1, keepdims=True) + EPS)
    unit_ref[...] = (picked * scale).astype(bf16)
    at = iota((EXTRA, CAP), 0)
    tail = jnp.where(at == 0, live, jnp.where(at == 1, weight * GRAD_SCALE, 0.0)).astype(bf16)
    mine_ref[...] = tail
    pack_ref[0:HALF, :] = unit_ref[pl.ds(pl.multiple_of(at_ref[0] * HALF, HALF), HALF), :]
    pack_ref[HALF : HALF + EXTRA, :] = tail
    peers = send_hbm.shape[0]
    make = lambda g: pltpu.make_async_copy(pack_ref, send_hbm.at[g], sems.at[g])
    start_all(peers, make)
    wait_all(peers, make)


def columns_body(student_ref, teacher_ref, cols_ref, student_t_ref, teacher_t_ref, norm_ref):
    for part in chunks_of(student_ref.shape[1]):
        wide = student_ref[:, part].astype(f32)
        norm = jnp.sqrt(jnp.sum(wide * wide, axis=0, keepdims=True) + EPS)
        norm_ref[:, part] = norm
        unit = wide / norm
        cols_ref[:, part] = unit.astype(bf16)
        student_t_ref[part, :] = unit.T.astype(bf16)
        wide = teacher_ref[:, part].astype(f32)
        norm = jnp.sqrt(jnp.sum(wide * wide, axis=0, keepdims=True) + EPS)
        teacher_t_ref[part, :] = (wide / norm).T.astype(bf16)


def weights_body(at_ref, w_in_ref, w_out_ref, pack_ref):
    rows, hid = w_in_ref.shape
    half = hid // 2
    bot = w_out_ref.shape[1]
    lines = w_out_ref.shape[0] * bot // half
    pack_ref[0:rows, :] = w_in_ref[:, pl.ds(pl.multiple_of(at_ref[0] * half, half), half)]
    for q in range(half // bot):
        pack_ref[rows : rows + lines, q * bot : (q + 1) * bot] = w_out_ref[q * lines : (q + 1) * lines, :]


def weight_loads(at_ref, w_hbm, w_in_ref, w_out_ref, sems):
    peers = w_hbm.shape[0]
    rows = w_in_ref.shape[0] // peers
    lines = w_hbm.shape[1] - rows
    bot = w_out_ref.shape[1]
    quarters = w_hbm.shape[2] // bot
    pairs = [(w_hbm.at[g, 0:rows, :], w_in_ref.at[g * rows : (g + 1) * rows, :]) for g in range(peers)]
    for i in range(peers // 2):
        for q in range(quarters):
            source = w_hbm.at[at_ref[0] * (peers // 2) + i, rows : rows + lines, q * bot : (q + 1) * bot]
            at = (i * quarters + q) * lines
            pairs.append((source, w_out_ref.at[at : at + lines, :]))
    return copies(pairs, sems)


def forward_body(
    at_ref, sel_ref, tokens_hbm, w_hbm, rows_ref, hidden_ref, slope_ref, feats_ref, tokens_ref, w_in_ref, w_out_ref, sems, tsem
):
    tokens = pltpu.make_async_copy(tokens_hbm, tokens_ref, tsem)
    tokens.start()
    loads = weight_loads(at_ref, w_hbm, w_in_ref, w_out_ref, sems)
    for load in loads:
        load.start()
    tokens.wait()
    rows = mm(sel_ref[...], tokens_ref[...]).astype(bf16)
    rows_ref[...] = rows
    for load in loads:
        load.wait()
    feats = jnp.zeros(feats_ref.shape, f32)
    for part in chunks_of(hidden_ref.shape[1]):
        pre = mm(rows, w_in_ref[:, part])
        cdf = 0.5 * (1.0 + lax.erf(pre * 0.7071067811865476))
        slope_ref[:, part] = cdf + pre * (jnp.exp(-0.5 * pre * pre) * 0.3989422804014327)
        hidden = (pre * cdf).astype(bf16)
        hidden_ref[:, part] = hidden
        feats = feats + mm(hidden, w_out_ref[part, :])
    feats_ref[...] = feats


def unit_body(feats_ref, other_ref, unit_ref, inv_ref, rows_ref):
    feats = feats_ref[...] + other_ref[...]
    inv = lax.rsqrt(jnp.sum(feats * feats, axis=1, keepdims=True) + EPS)
    unit = feats * inv
    unit_ref[...] = unit.T
    inv_ref[...] = jnp.broadcast_to(inv, feats.shape).T[0:8]
    rows_ref[...] = unit.astype(bf16)


def chunks_of(width):
    step = min(256, width)
    return [slice(at, at + step) for at in range(0, width, step)]


def row_of(ref, g):
    return ref[pl.ds(g, 1), :]


def fold(x):
    return x.reshape(x.shape[0] // 8, 8, x.shape[1]).sum(axis=0)


def expo_body(
    at_ref, cols_ref, own_hbm, other_hbm, expo_hbm, part_ref, live_ref, weight_ref,
    rows_ref, tail_ref, expo_ref, total_ref, sums_ref, sems, own_sems, other_sems, tail_sems,
):
    peers = own_hbm.shape[0]
    width = cols_ref.shape[0]
    core = at_ref[0]
    number = peers // GROUP
    rows_of = lambda ref, q: ref.at[pl.ds(q * GROUP, GROUP), 0:HALF, :]
    rows_at = lambda q, c: rows_ref.at[pl.ds(q * GROUP, GROUP), c]
    load_own = lambda q: pltpu.make_async_copy(rows_of(own_hbm, q), rows_at(q, core), own_sems.at[q])
    load_other = lambda q: pltpu.make_async_copy(rows_of(other_hbm, q), rows_at(q, 1 - core), other_sems.at[q])
    load_tail = pltpu.make_async_copy(own_hbm.at[:, HALF : HALF + EXTRA, :], tail_ref, tail_sems.at[0])
    store = lambda q: pltpu.make_async_copy(group(expo_ref, q), group(expo_hbm, q), sems.at[q])
    load_tail.start()
    start_all(number, load_own)
    start_all(number, load_other)
    total_ref[...] = jnp.zeros_like(total_ref)
    load_tail.wait()

    def first(g):
        rows = rows_ref[g].reshape(CAP, rows_ref.shape[3])
        tail = tail_ref[g].astype(f32)
        live = tail[0:1]
        live_ref[pl.ds(g, 1), :] = live
        weight_ref[pl.ds(g, 1), :] = tail[1:2]
        for part in chunks_of(width):
            cos = mm(cols_ref[part, :], rows, NT)
            expo = jnp.exp(cos * (1.0 / TEACHER_TEMP)) * live
            expo_ref[g, part, :] = expo.astype(bf16)
            total_ref[part, :] += expo[:, 0:128] + expo[:, 128:256]
        return 0

    over_groups(peers, first, (load_own, load_other), (store,), UNROLL)
    spread_scale(total_ref)
    row_parts(expo_ref, total_ref, sums_ref, part_ref)
    wait_all(number, store)


def spread_scale(total_ref):
    for part in chunks_of(total_ref.shape[0]):
        sums = jnp.sum(total_ref[part, :], axis=1, keepdims=True)
        total_ref[part, :] = jnp.broadcast_to(1.0 / sums, sums.shape[:1] + (128,))


def scaled(expo, scale):
    return jnp.concatenate([expo[:, 0:128] * scale, expo[:, 128:256] * scale], axis=1)


def row_parts(expo_ref, scale_ref, sums_ref, part_ref):
    def step(g):
        acc = jnp.zeros((8, CAP), f32)
        for part in chunks_of(scale_ref.shape[0]):
            acc = acc + fold(scaled(expo_ref[g, part, :].astype(f32), scale_ref[part, :]))
        sums_ref[pl.ds(g, 1), :] = jnp.sum(acc, axis=0, keepdims=True)
        return 0

    over_groups(expo_ref.shape[0], step, unroll=UNROLL)
    sums = sums_ref[...].astype(bf16)
    for t in range(part_ref.shape[0]):
        part_ref[t] = sums


def relay_body(parts_ref, out_ref):
    sums = parts_ref[0].astype(f32)
    for t in range(1, parts_ref.shape[0]):
        sums = sums + parts_ref[t].astype(f32)
    sums = sums.astype(bf16)
    for g in range(out_ref.shape[0]):
        out_ref[g] = sums


def scales_from(parts_ref, live_ref, scale_ref):
    sums = parts_ref[0].astype(f32)
    for g in range(1, parts_ref.shape[0]):
        sums = sums + parts_ref[g].astype(f32)
    live = live_ref[...]
    scale_ref[...] = live / (sums + 1.0 - live)


def column_sums(load, expo_ref, scale_ref, total_ref):
    total_ref[...] = jnp.zeros_like(total_ref)

    def step(g):
        row = row_of(scale_ref, g)
        for part in chunks_of(total_ref.shape[0]):
            expo = expo_ref[g, part, :].astype(f32)
            total_ref[part, :] += expo[:, 0:128] * row[:, 0:128] + expo[:, 128:256] * row[:, 128:256]
        return 0

    over_groups(expo_ref.shape[0], step, (load,), unroll=UNROLL)
    spread_scale(total_ref)


def balance_body(expo_hbm, parts_ref, live_ref, part_ref, expo_ref, total_ref, sums_ref, scale_ref, sems):
    load = lambda q: pltpu.make_async_copy(group(expo_hbm, q), group(expo_ref, q), sems.at[q])
    start_all(expo_ref.shape[0] // GROUP, load)
    scales_from(parts_ref, live_ref, scale_ref)
    column_sums(load, expo_ref, scale_ref, total_ref)
    row_parts(expo_ref, total_ref, sums_ref, part_ref)


def divide_up(g, acc, pull, halves_ref):
    rows = jnp.sum(acc, axis=0, keepdims=True)
    rows = jnp.where(iota((EXTRA, CAP), 0) == 0, rows, 0.0).astype(bf16)
    pull = pull.astype(bf16)
    for at, block in ((slice(0, CAP), pull), (slice(CAP, LINES), rows)):
        halves_ref[0, g, at, :] = block[:, 0:HALF]
        halves_ref[1, g, at, :] = block[:, HALF:CAP]


def last_body(
    at_ref, expo_hbm, parts_ref, live_ref, cols_ref, keep_hbm, give_hbm, total_ref,
    expo_ref, scale_ref, halves_ref, sems, keep_sems, give_sems,
):
    peers = expo_ref.shape[0]
    core = at_ref[0]
    load = lambda q: pltpu.make_async_copy(group(expo_hbm, q), group(expo_ref, q), sems.at[q])
    half_at = lambda c, q: halves_ref.at[c, pl.ds(q * GROUP, GROUP)]
    keep = lambda q: pltpu.make_async_copy(half_at(core, q), group(keep_hbm, q), keep_sems.at[q])
    give = lambda q: pltpu.make_async_copy(half_at(1 - core, q), group(give_hbm, q), give_sems.at[q])
    number = peers // GROUP
    start_all(number, load)
    scales_from(parts_ref, live_ref, scale_ref)
    column_sums(load, expo_ref, scale_ref, total_ref)

    def step(g):
        acc = jnp.zeros((8, CAP), f32)
        pull = jnp.zeros((cols_ref.shape[0], CAP), f32)
        for part in chunks_of(total_ref.shape[0]):
            balanced = scaled(expo_ref[g, part, :].astype(f32), total_ref[part, :])
            acc = acc + fold(balanced)
            pull = pull + mm(cols_ref[:, part], balanced.astype(bf16))
        divide_up(g, acc, pull, halves_ref)
        return 0

    over_groups(peers, step, (), (give, keep), UNROLL)
    wait_all(number, give)
    wait_all(number, keep)


def student_body(
    at_ref, cols_t_ref, cols_ref, rows_hbm, raised_hbm, keep_hbm, give_hbm,
    rows_ref, raised_ref, halves_ref, row_sems, sems, keep_sems, give_sems,
):
    peers = rows_ref.shape[0]
    load = lambda q: pltpu.make_async_copy(group(rows_hbm, q), group(rows_ref, q), row_sems.at[q])
    start_all(peers // GROUP, load)
    core = at_ref[0]
    width = cols_t_ref.shape[0]
    store = lambda q: pltpu.make_async_copy(group(raised_ref, q), group(raised_hbm, q), sems.at[q])
    half_at = lambda c, q: halves_ref.at[c, pl.ds(q * GROUP, GROUP)]
    keep = lambda q: pltpu.make_async_copy(half_at(core, q), group(keep_hbm, q), keep_sems.at[q])
    give = lambda q: pltpu.make_async_copy(half_at(1 - core, q), group(give_hbm, q), give_sems.at[q])
    number = peers // GROUP

    def step(g):
        rows = rows_ref[g]
        acc = jnp.zeros((8, CAP), f32)
        pull = jnp.zeros((cols_ref.shape[0], CAP), f32)
        for part in chunks_of(width):
            raised = jnp.exp(mm(cols_t_ref[part, :], rows, NT) * (1.0 / STUDENT_TEMP))
            acc = acc + fold(raised)
            raised = raised.astype(bf16)
            raised_ref[g, part, :] = raised
            pull = pull + mm(cols_ref[:, part], raised)
        divide_up(g, acc, pull, halves_ref)
        return 0

    over_groups(peers, step, (load,), (store, give, keep), UNROLL)
    for make in (give, keep, store):
        wait_all(number, make)


def columns_grad_body(
    expo_hbm, raised_hbm, scale_ref, got_hbm, rows_hbm, proto_ref, norm_ref,
    grad_ref, expo_ref, raised_ref, acc_ref, tail_ref, rows_ref, esems, rsems, tail_sems, row_sems,
):
    peers = expo_ref.shape[0]
    load = lambda q: pltpu.make_async_copy(group(expo_hbm, q), group(expo_ref, q), esems.at[q])
    load_raised = lambda q: pltpu.make_async_copy(group(raised_hbm, q), group(raised_ref, q), rsems.at[q])
    load_rows = lambda q: pltpu.make_async_copy(group(rows_hbm, q), group(rows_ref, q), row_sems.at[q])
    lines = got_hbm.shape[1] - EXTRA
    load_tail = pltpu.make_async_copy(got_hbm.at[:, lines : lines + EXTRA, :], tail_ref, tail_sems.at[0])
    load_tail.start()

    def begin(q, _):
        for make in (load_rows, load, load_raised):
            make(q).start()
        return 0

    lax.fori_loop(0, peers // GROUP, begin, 0)
    acc_ref[...] = jnp.zeros_like(acc_ref)
    load_tail.wait()

    def step(g):
        tail = tail_ref[g].astype(f32)
        alpha = tail[0:1] + tail[1:2]
        beta = tail[2:3] + tail[3:4]
        rows = rows_ref[g]
        for part in chunks_of(acc_ref.shape[0]):
            balanced = scaled(expo_ref[g, part, :].astype(f32), scale_ref[part, :])
            score = raised_ref[g, part, :].astype(f32) * alpha - balanced * beta
            acc_ref[part, :] += mm(score.astype(bf16), rows)
        return 0

    over_groups(peers, step, (load_rows, load, load_raised), (), UNROLL)
    for part in chunks_of(acc_ref.shape[0]):
        grad = acc_ref[part, :].T
        norm = norm_ref[:, part]
        unit = proto_ref[:, part].astype(f32) / norm
        grad_ref[:, part] = (grad - unit * jnp.sum(unit * grad, axis=0, keepdims=True)) / norm


def join(core, both_ref, other_ref, at):
    own, other = (both_ref[at], other_ref[at])
    low = core == 0
    return jnp.concatenate([jnp.where(low, own, other), jnp.where(low, other, own)], axis=1)


def two_parts(x):
    high = x.astype(bf16)
    return (high.astype(f32), x - high.astype(f32))


def backward_body(
    at_ref, both_ref, other_ref, mine_ref, member_ref, unit_ref, inv_ref, rows_ref, hidden_ref, slope_ref, w_hbm,
    send_hbm, grad_rows_ref, loss_ref, w_in_ref, w_out_ref, send_ref, pre_ref, out_ref, sems, send_sems,
):
    peers = w_hbm.shape[0]
    loads = weight_loads(at_ref, w_hbm, w_in_ref, w_out_ref, sems)
    for load in loads:
        load.start()
    tail = mine_ref[...].astype(f32)
    live, weight = (tail[0:1], tail[1:2] * (1.0 / STUDENT_TEMP))
    pull = join(at_ref[0], both_ref, other_ref, 0)
    push = join(at_ref[0], both_ref, other_ref, 1)
    norm_sum = push[CAP : CAP + 1]
    push = push[0:CAP]
    scale = live / (pull[CAP : CAP + 1] + 1.0 - live)
    pull = pull[0:CAP]
    unit = unit_ref[...]
    cross = jnp.sum(unit.astype(bf16).astype(f32) * pull, axis=0, keepdims=True) * (1.0 / STUDENT_TEMP)
    row_loss = jnp.log(norm_sum) - scale * cross
    loss = jnp.sum(member_ref[...] * row_loss, axis=1, keepdims=True)
    loss_ref[...] = jnp.broadcast_to(loss, loss_ref.shape)
    alpha = weight / norm_sum
    beta = weight * scale
    grad_unit = push * alpha - pull * beta
    inner = jnp.sum(unit * grad_unit, axis=0, keepdims=True)
    grad_feats = (inv_ref[0:1] * (grad_unit - unit * inner)).T.astype(bf16)
    for load in loads:
        load.wait()
    width = send_ref.shape[2]
    grad_rows = jnp.zeros(grad_rows_ref.shape, f32)
    for part in chunks_of(hidden_ref.shape[1]):
        grad_pre = (mm(grad_feats, w_out_ref[part, :], NT) * slope_ref[:, part]).astype(bf16)
        pre_ref[:, part] = grad_pre
        grad_rows = grad_rows + mm(grad_pre, w_in_ref[:, part], NT)
        out_ref[part, :] = mm(hidden_ref[:, part], grad_feats, TN).astype(bf16)
    grad_rows_ref[...] = grad_rows.astype(bf16)
    core, level = (at_ref[0], at_ref[1])
    own = pre_ref[:, pl.ds(pl.multiple_of(level * width, width), width)]
    grad_in = mm(rows_ref[...], own, TN).astype(bf16)
    per = grad_in.shape[0] // peers
    block = out_ref.shape[0] // (peers // 2)
    share = block // 4
    at = iota((EXTRA, CAP), 0)
    rows = jnp.zeros((EXTRA, CAP), f32)
    for i, x in enumerate(two_parts(alpha) + two_parts(beta)):
        rows = jnp.where(at == i, x, rows)
    rows = rows.astype(bf16)
    store = lambda g: pltpu.make_async_copy(send_ref.at[g], send_hbm.at[g], send_sems.at[g])
    for g in range(peers):
        send_ref[g, 0:per, :] = grad_in[g * per : (g + 1) * per, :]
        start = pl.multiple_of((g % (peers // 2)) * block + level * share, share)
        out = out_ref[pl.ds(start, share), :]
        send_ref[g, per : per + share, :] = jnp.where(core == g // (peers // 2), out, jnp.zeros_like(out))
        send_ref[g, per + share : per + share + EXTRA, :] = rows
        store(g).start()
    wait_all(peers, store)


def place_body(sel_ref, rows_ref, other_ref, out_hbm, out_ref, sems):
    rows = (rows_ref[...].astype(f32) + other_ref[...].astype(f32)).astype(bf16)
    pieces = out_ref.shape[0]
    size = out_ref.shape[1]
    store = lambda i: pltpu.make_async_copy(out_ref.at[i], out_hbm.at[i], sems.at[i])
    for i in range(pieces):
        out_ref[i] = mm(sel_ref[:, i * size : (i + 1) * size], rows, TN).astype(bf16)
        store(i).start()
    wait_all(pieces, store)


def gather_grads_body(got_ref, send_ref):
    peers = got_ref.shape[0]
    lines = send_ref.shape[1]
    acc = got_ref[0, 0:lines, :].astype(f32)
    for g in range(1, peers):
        acc = acc + got_ref[g, 0:lines, :].astype(f32)
    acc = acc.astype(bf16)
    for t in range(send_ref.shape[0]):
        send_ref[t] = acc


def weight_grads_body(at_ref, parts_ref, grad_in_ref, grad_out_ref):
    peers, lines, width = parts_ref.shape
    per = grad_in_ref.shape[0]
    share = lines - per
    for t in range(peers):
        to = ((t % 2) * (peers // 2) + t // 2) * width
        grad_in_ref[:, to : to + width] = parts_ref[t, 0:per, :].astype(f32)
    for z in range(peers // 2):
        grad_out_ref[z * share : (z + 1) * share, :] = parts_ref[2 * z + at_ref[2], per:lines, :].astype(f32)


def sem(number):
    return pltpu.SemaphoreType.DMA((number,))


def run_expo(at, cols_t, own, other, tensor):
    dp, (width, bot) = (own.shape[0], cols_t.shape)
    big, small = ((dp, width, CAP), (dp, CAP))
    return call(
        expo_body,
        [(big, bf16), ((tensor, *small), bf16), (small, f32), (small, f32)],
        (at, cols_t, own, other),
        in_specs=[SMEM, VMEM, HBM, HBM],
        out_specs=[HBM, VMEM, VMEM, VMEM],
        scratch=[
            pltpu.VMEM((dp, 2, HALF, bot), bf16),
            pltpu.VMEM((dp, EXTRA, bot), bf16),
            pltpu.VMEM(big, bf16),
            pltpu.VMEM((width, 128), f32),
            pltpu.VMEM(small, f32),
            *[sem(dp // GROUP)] * 4,
        ],
    )


def run_balance(expo, got, live, tensor):
    dp, width, _ = expo.shape
    small = pltpu.VMEM(live.shape, f32)
    return call(
        balance_body,
        [((tensor, *live.shape), bf16)],
        (expo, got, live),
        in_specs=[HBM, VMEM, VMEM],
        scratch=[pltpu.VMEM(expo.shape, bf16), pltpu.VMEM((width, 128), f32), small, small, sem(dp // GROUP)],
    )[0]


def run_last(at, expo, got, live, cols):
    dp, width, _ = expo.shape
    halves = (dp, LINES, HALF)
    return call(
        last_body,
        [(halves, bf16), (halves, bf16), ((width, 128), f32)],
        (at, expo, got, live, cols),
        in_specs=[SMEM, HBM, VMEM, VMEM, VMEM],
        out_specs=[HBM, HBM, VMEM],
        scratch=[
            pltpu.VMEM(expo.shape, bf16),
            pltpu.VMEM(live.shape, f32),
            pltpu.VMEM((2, *halves), bf16),
            *[sem(dp // GROUP)] * 3,
        ],
    )


def run_student(at, cols_t, cols, rows):
    dp = rows.shape[0]
    big, halves = ((dp, cols.shape[1], CAP), (dp, LINES, HALF))
    return call(
        student_body,
        [(big, bf16), (halves, bf16), (halves, bf16)],
        (at, cols_t, cols, rows),
        in_specs=[SMEM, VMEM, VMEM, HBM],
        out_specs=[HBM, HBM, HBM],
        scratch=[
            pltpu.VMEM(rows.shape, bf16),
            pltpu.VMEM(big, bf16),
            pltpu.VMEM((2, *halves), bf16),
            *[sem(dp // GROUP)] * 4,
        ],
    )


def run_columns_grad(expo, raised, scale, got, rows, proto, norm):
    dp, held = (expo.shape[0], pltpu.VMEM(expo.shape, bf16))
    return call(
        columns_grad_body,
        [(proto.shape, f32)],
        (expo, raised, scale, got, rows, proto, norm),
        in_specs=[HBM, HBM, VMEM, HBM, HBM, VMEM, VMEM],
        scratch=[
            held,
            held,
            pltpu.VMEM(proto.shape[::-1], f32),
            pltpu.VMEM((dp, EXTRA, CAP), bf16),
            pltpu.VMEM(rows.shape, bf16),
            *[sem(dp // GROUP)] * 4,
        ],
    )[0]


def exchange(x, axis):
    return lax.all_to_all(x, axis, split_axis=0, concat_axis=0, tiled=True)


def sibling(x):
    peers = lax.axis_size("tensor")
    return lax.ppermute(x, "tensor", [(i, i ^ 1) for i in range(peers)])


def everywhere(part, small):
    got = exchange(part, "tensor")
    (sums,) = call(relay_body, [((small[0], *small), bf16)], (got,))
    return exchange(sums, "dp")


def levels(x, by):
    peers = lax.axis_size("tensor")
    return lax.ppermute(x, "tensor", [(i, i ^ (2 * by)) for i in range(peers)])


def paired(keep, give):
    return (keep.astype(f32) + sibling(give).astype(f32)).astype(bf16)


def slot_sums_body(parts_hbm, out_ref, parts_ref, sems):
    peers = parts_hbm.shape[0]
    load = lambda g: pltpu.make_async_copy(parts_hbm.at[g], parts_ref.at[g], sems.at[g])
    start_all(peers, load)
    load(0).wait()
    acc = parts_ref[0].astype(f32)
    for g in range(1, peers):
        load(g).wait()
        acc = acc + parts_ref[g].astype(f32)
    out_ref[...] = acc.astype(bf16)


def slot_sums(parts):
    out = parts.shape[1:]
    scratch = [pltpu.VMEM(parts.shape, bf16), pltpu.SemaphoreType.DMA((parts.shape[0],))]
    return call(slot_sums_body, [(out, bf16)], (parts,), in_specs=[HBM], scratch=scratch)[0]


def after(x, earlier):
    return lax.optimization_barrier((x, earlier))[0]


def parts_of(tokens, teacher_feats, masks, w_in, w_out, proto_student, proto_teacher):
    dim = tokens.shape[1]
    hid = w_in.shape[1]
    bot, width = proto_student.shape
    dp, tensor = (lax.axis_size("dp"), lax.axis_size("tensor"))
    per = w_in.shape[0]
    half = hid // 2
    share = w_out.shape[0] // 4
    t = lax.axis_index("tensor").astype(jnp.int32)
    g = lax.axis_index("dp").astype(jnp.int32)
    at = jnp.stack([t % 2, t // 2, g // (dp // 2)])

    lines = per + w_out.shape[0] * bot // half
    (w_pack,) = call(weights_body, [((lines, half), bf16)], (at, w_in, w_out), in_specs=[SMEM, VMEM, VMEM])
    w_all = lax.all_gather(w_pack, "dp", axis=0, tiled=True).reshape(dp, lines, half)
    dma = pltpu.SemaphoreType.DMA
    sems = dma((dp,))
    sel, send, member, mine = call(
        select_body,
        [((CAP, tokens.shape[0]), bf16), ((dp, HALF + EXTRA, bot), bf16), ((8, CAP), f32), ((EXTRA, CAP), bf16)],
        (at, masks, teacher_feats),
        in_specs=[SMEM, VMEM, VMEM],
        out_specs=[VMEM, HBM, VMEM, VMEM],
        scratch=[pltpu.VMEM((CAP, bot), bf16), pltpu.VMEM((HALF + EXTRA, bot), bf16), sems],
    )
    packs = exchange(send, "dp")
    others = sibling(packs)
    cols, student_t, teacher_t, norm = call(
        columns_body,
        [((bot, width), bf16), ((width, bot), bf16), ((width, bot), bf16), ((1, width), f32)],
        (proto_student, proto_teacher),
    )
    expo, part, live, _ = run_expo(at, teacher_t, packs, others, tensor)
    loads = dma((dp + 2 * dp,))
    w_held = [pltpu.VMEM((dim, half), bf16), pltpu.VMEM((half, bot), bf16)]
    rows, hidden, slope, feats = call(
        forward_body,
        [((CAP, dim), bf16), ((CAP, half), bf16), ((CAP, half), f32), ((CAP, bot), f32)],
        (at, sel, tokens, after(w_all, part)),
        in_specs=[SMEM, VMEM, HBM, HBM],
        scratch=[pltpu.VMEM(tokens.shape, bf16), *w_held, loads, dma(())],
    )
    unit, inv, student_rows = call(
        unit_body, [((bot, CAP), f32), ((8, CAP), f32), ((CAP, bot), bf16)], (feats, sibling(feats))
    )
    all_rows = lax.all_gather(student_rows, "dp", axis=0, tiled=True).reshape(dp, CAP, bot)
    got = everywhere(part, live.shape)
    part = run_balance(expo, got, live, tensor)
    got = everywhere(part, live.shape)
    keep, give, scale = run_last(at, expo, got, live, cols)
    pull = paired(keep, give)
    pull_got = exchange(pull, "dp")
    all_rows = after(all_rows, pull)
    raised, keep, give = run_student(at, student_t, cols, all_rows)
    push_got = exchange(paired(keep, give), "dp")
    both = jnp.stack([slot_sums(pull_got), slot_sums(push_got)])
    near, far, last = (levels(both, by) for by in (1, 2, 3))
    wide = lambda x: x.astype(f32)
    both = (wide(both) + wide(near)) + (wide(far) + wide(last))
    back_lines = per + share + EXTRA
    send, grad_rows, loss = call(
        backward_body,
        [((dp, back_lines, bot), bf16), ((CAP, dim), bf16), ((8, 128), f32)],
        (at, both, sibling(both), mine, member, unit, inv, rows, hidden, slope, w_all),
        in_specs=[SMEM] + [VMEM] * 9 + [HBM],
        out_specs=[HBM, VMEM, VMEM],
        scratch=[
            *w_held,
            pltpu.VMEM((dp, back_lines, bot), bf16),
            pltpu.VMEM((CAP, half), bf16),
            pltpu.VMEM((half, bot), bf16),
            loads,
            sems,
        ],
    )
    got = exchange(send, "dp")
    pieces = 4
    d_shape = (pieces, tokens.shape[0] // pieces, dim)
    (d_tokens,) = call(
        place_body,
        [(d_shape, bf16)],
        (sel, grad_rows, sibling(grad_rows)),
        out_specs=[HBM],
        scratch=[pltpu.VMEM(d_shape, bf16), dma((pieces,))],
    )
    got, d_tokens = lax.optimization_barrier((got, d_tokens))
    (sent,) = call(gather_grads_body, [((tensor, per + share, bot), bf16)], (got,))
    parts = exchange(sent, "tensor")
    grad_proto = run_columns_grad(expo, raised, scale, got, all_rows, proto_student, norm)
    grad_in, grad_out = call(
        weight_grads_body, [((per, hid), f32), ((w_out.shape[0], bot), f32)], (at, parts), in_specs=[SMEM, VMEM]
    )
    return (d_tokens.reshape(tokens.shape), grad_in, grad_out, grad_proto, loss[: masks.shape[0], 0])


def solution(mesh):
    placed = (
        P("dp", None),
        P("dp", None),
        P("dp", None),
        P("dp", None),
        P("dp", None),
        P(None, ("dp", "tensor")),
        P(None, ("dp", "tensor")),
    )
    return jax.shard_map(
        parts_of,
        mesh=mesh,
        in_specs=placed,
        out_specs=(P("dp", None), P("dp", None), P("dp", None), P(None, ("dp", "tensor")), P("dp")),
        check_vma=False,
    )
```

profile of v0, /device:TPU:1, one launch (start us, length us, event | category | flops | bytes accessed | tf_op | source)
XLA Modules:
  0.0 273.3 jit_solution(11296004076679124828)
XLA Ops:
  11.2 3.1 %shard_map.111 = (bf16[256,1024]{1,0:T(8,128)(2,1)S(1)}, bf16[16,144,256]{2,1,0:T(8,128)(2,1)S(1)}, f32[8,256]{1,0:T(8,128)S(1)}, bf16[16,256]{1,0:T(8,128)(2,1)S(1)}) custom-call(s32[3]{0:T(128)S(1)} %pad_add_fusion.at_ref, s32[4,256]{1,0:T(4,128)S(1)} %copy-done.26, bf16[1024,256]{1,0:T(8,128)(2,1)S(1)} %copy-done.14), custom_call_target="tpu_custom_call" | custom-call | tf_op jit(solution)/shard_map/pallas_call | solution.py:33
  14.9 29.0 %all_to_all.45.own_hbm = bf16[16,144,256]{2,1,0:T(8,128)(2,1)S(1)} all-to-all(bf16[16,144,256]{2,1,0:T(8,128)(2,1)S(1)} %get-tuple-element.39), channel_id=1, replica_groups=mesh['dp'=16,'tensor'=8] {'dp'}, dimensions={0} | all-to-all | bytes 2359296 | tf_op jit(solution)/shard_map/all_to_all | solution.py:618
  43.9 2.2 collective-permute-start
  48.6 7.6 %shard_map.112 = (bf16[16,1024,256]{2,1,0:T(8,128)(2,1)}, bf16[8,16,256]{2,1,0:T(8,128)(2,1)S(1)}, f32[16,256]{1,0:T(8,128)S(1)}, f32[16,256]{1,0:T(8,128)}) custom-call(s32[3]{0:T(128)S(1)} %pad_add_fusion.at_ref, bf16[1024,256]{1,0:T(8,128)(2,1)S(1)} %get-tuple-element.38.cols_ref, bf16[16,144,256]{2,1,0:T(8,128)(2,1)S(1)} %all_to_all.45.own_hbm, ...), custom_call_target="tpu_custom_call" | custom-call | tf_op jit(solution)/shard_map/pallas_call | solution.py:33
  56.2 17.3 %all-gather.3.cloned.1.call-done = bf16[2048,1024]{1,0:T(8,128)(2,1)} async-done(((bf16[128,1024]{1,0:T(8,128)(2,1)}), bf16[2048,1024]{1,0:T(8,128)(2,1)}) %all-gather.3.cloned.1.call-update) | async-done | bytes 4194320 | tf_op jit(solution)/shard_map/all_gather | solution.py:677
  73.5 7.2 %shard_map.119 = (bf16[256,1536]{1,0:T(8,128)(2,1)S(1)}, bf16[256,1024]{1,0:T(8,128)(2,1)S(1)}, f32[256,1024]{1,0:T(8,128)S(1)}, f32[256,256]{1,0:T(8,128)S(1)}) custom-call(s32[3]{0:T(128)S(1)} %pad_add_fusion.at_ref, bf16[256,1024]{1,0:T(8,128)(2,1)S(1)} %get-tuple-element.47.sel_ref, bf16[1024,1536]{1,0:T(8,128)(2,1)} %tokens_hbm.1, ...), custom_call_target="tpu_custom_call" | custom-call | tf_op jit(solution)/shard_map/pallas_call | solution.py:33
  85.8 9.4 %all_to_all.46.parts_ref = bf16[8,16,256]{2,1,0:T(8,128)(2,1)S(1)} all-to-all(bf16[8,16,256]{2,1,0:T(8,128)(2,1)S(1)} %get-tuple-element.41), channel_id=1, replica_groups=mesh['dp'=16,'tensor'=8] {'tensor'}, dimensions={0} | all-to-all | bytes 131072 | tf_op jit(solution)/shard_map/all_to_all | solution.py:618
  95.2 11.7 %all_to_all.47.parts_ref = bf16[16,16,256]{2,1,0:T(8,128)(2,1)S(1)} all-to-all(bf16[16,16,256]{2,1,0:T(8,128)(2,1)S(1)} %shard_map.113), channel_id=1, replica_groups=mesh['dp'=16,'tensor'=8] {'dp'}, dimensions={0} | all-to-all | bytes 262144 | tf_op jit(solution)/shard_map/all_to_all | solution.py:618
  106.9 5.9 %shard_map.114 = bf16[8,16,256]{2,1,0:T(8,128)(2,1)S(1)} custom-call(bf16[16,1024,256]{2,1,0:T(8,128)(2,1)} %get-tuple-element.40.expo_hbm, bf16[16,16,256]{2,1,0:T(8,128)(2,1)S(1)} %all_to_all.47.parts_ref, f32[16,256]{1,0:T(8,128)S(1)} %get-tuple-element.42.live_ref), custom_call_target="tpu_custom_call" | custom-call | tf_op jit(solution)/shard_map/pallas_call | solution.py:33
  112.9 9.4 %all_to_all.48.parts_ref = bf16[8,16,256]{2,1,0:T(8,128)(2,1)S(1)} all-to-all(bf16[8,16,256]{2,1,0:T(8,128)(2,1)S(1)} %shard_map.114), channel_id=1, replica_groups=mesh['dp'=16,'tensor'=8] {'tensor'}, dimensions={0} | all-to-all | bytes 131072 | tf_op jit(solution)/shard_map/all_to_all | solution.py:618
  122.3 10.1 %all_to_all.49.parts_ref = bf16[16,16,256]{2,1,0:T(8,128)(2,1)S(1)} all-to-all(bf16[16,16,256]{2,1,0:T(8,128)(2,1)S(1)} %shard_map.115), channel_id=1, replica_groups=mesh['dp'=16,'tensor'=8] {'dp'}, dimensions={0} | all-to-all | bytes 262144 | tf_op jit(solution)/shard_map/all_to_all | solution.py:618
  132.4 8.3 %shard_map.116 = (bf16[16,272,128]{2,1,0:T(8,128)(2,1)S(1)}, bf16[16,272,128]{2,1,0:T(8,128)(2,1)S(1)}, f32[1024,128]{1,0:T(8,128)S(1)}) custom-call(s32[3]{0:T(128)S(1)} %pad_add_fusion.at_ref, bf16[16,1024,256]{2,1,0:T(8,128)(2,1)} %get-tuple-element.40.expo_hbm, bf16[16,16,256]{2,1,0:T(8,128)(2,1)S(1)} %all_to_all.49.parts_ref, ...), custom_call_target="tpu_custom_call" | custom-call | tf_op jit(solution)/shard_map/pallas_call | solution.py:33
  143.2 2.4 collective-permute-done.1
  148.5 8.3 %shard_map.121 = (bf16[16,1024,256]{2,1,0:T(8,128)(2,1)}, bf16[16,272,128]{2,1,0:T(8,128)(2,1)S(1)}, bf16[16,272,128]{2,1,0:T(8,128)(2,1)}) custom-call(s32[3]{0:T(128)S(1)} %pad_add_fusion.at_ref, bf16[1024,256]{1,0:T(8,128)(2,1)S(1)} %copy-done.17, bf16[256,1024]{1,0:T(8,128)(2,1)S(1)} %get-tuple-element.43.cols_ref, bf16[16,256,256]{2,1,0:T(8,128)(2,1)S(1)} %bitcast.8), custom_call_target="tpu_custom_call" | custom-call | tf_op jit(solution)/shard_map/pallas_call | solution.py:33
  157.2 3.7 %all-to-all-start.5 = ((bf16[16,272,128]{2,1,0:T(8,128)(2,1)}), bf16[16,272,128]{2,1,0:T(8,128)(2,1)S(1)}, u32[]{:S(2)}, u32[]{:S(2)}) async-start(bf16[16,272,128]{2,1,0:T(8,128)(2,1)} %add_convert_fusion.1), calls=%async_computation.5 | async-start | bytes 2228224 | tf_op jit(solution)/shard_map/all_to_all | solution.py:618
  161.0 2.5 add_convert_fusion
  163.5 16.7 %all-to-all-done.5.parts_hbm = bf16[16,272,128]{2,1,0:T(8,128)(2,1)S(1)} async-done(((bf16[16,272,128]{2,1,0:T(8,128)(2,1)}), bf16[16,272,128]{2,1,0:T(8,128)(2,1)S(1)}, u32[]{:S(2)}, u32[]{:S(2)}) %all-to-all-start.5) | async-done | bytes 1114144 | tf_op jit(solution)/shard_map/all_to_all | solution.py:618
  180.2 3.7 %all-to-all-start.6 = ((bf16[16,272,128]{2,1,0:T(8,128)(2,1)}), bf16[16,272,128]{2,1,0:T(8,128)(2,1)S(1)}, u32[]{:S(2)}, u32[]{:S(2)}) async-start(bf16[16,272,128]{2,1,0:T(8,128)(2,1)} %add_convert_fusion), calls=%async_computation.6 | async-start | bytes 2228224 | tf_op jit(solution)/shard_map/all_to_all | solution.py:618
  183.9 1.9 shard_map.117
  186.5 14.1 %all-to-all-done.6.parts_hbm = bf16[16,272,128]{2,1,0:T(8,128)(2,1)S(1)} async-done(((bf16[16,272,128]{2,1,0:T(8,128)(2,1)}), bf16[16,272,128]{2,1,0:T(8,128)(2,1)S(1)}, u32[]{:S(2)}, u32[]{:S(2)}) %all-to-all-start.6) | async-done | bytes 1114144 | tf_op jit(solution)/shard_map/all_to_all | solution.py:618
  200.6 1.9 shard_map.122
  205.9 2.2 collective-permute-done.5
  208.7 2.8 %collective-permute-done.6 = bf16[2,272,128]{2,1,0:T(8,128)(2,1)S(1)} collective-permute-done((bf16[2,272,128]{2,1,0:T(8,128)(2,1)S(1)}, bf16[2,272,128]{2,1,0:T(8,128)(2,1)S(1)}, u32[]{:S(2)}, u32[]{:S(2)}) %collective-permute-start.6) | collective-permute-done | bytes 139296 | tf_op jit(solution)/shard_map/ppermute | solution.py:634
  211.6 2.9 %collective-permute-start.7 = (f32[2,272,128]{2,1,0:T(8,128)S(1)}, f32[2,272,128]{2,1,0:T(8,128)S(1)}, u32[]{:S(2)}, u32[]{:S(2)}) collective-permute-start(f32[2,272,128]{2,1,0:T(8,128)S(1)} %add_add_fusion.both_ref), channel_id=1, source_target_pairs={{0,1},{1,0},{2,3},{3,2},{4,5},{5,4},{6,7},{7,6},{8,9},{9,8},{10,11... | collective-permute-start | bytes 835592 | tf_op jit(solution)/shard_map/ppermute | solution.py:623
  215.7 6.7 %shard_map.123 = (bf16[16,144,256]{2,1,0:T(8,128)(2,1)S(1)}, bf16[256,1536]{1,0:T(8,128)(2,1)S(1)}, f32[8,128]{1,0:T(8,128)S(1)}) custom-call(s32[3]{0:T(128)S(1)} %pad_add_fusion.at_ref, f32[2,272,128]{2,1,0:T(8,128)S(1)} %add_add_fusion.both_ref, f32[2,272,128]{2,1,0:T(8,128)S(1)} %collective-permute-done.7.other_ref, bf16[16,256]{1,0:T(8,128)(2,1)S(1)} %copy-done.23, ...), custom_call_target="tpu_custom_call" | custom-call | tf_op jit(solution)/shard_map/pallas_call | solution.py:33
  224.1 3.7 %all-to-all-start.7 = ((bf16[16,144,256]{2,1,0:T(8,128)(2,1)}), bf16[16,144,256]{2,1,0:T(8,128)(2,1)S(1)}, u32[]{:S(2)}, u32[]{:S(2)}) async-start(bf16[16,144,256]{2,1,0:T(8,128)(2,1)} %copy-done.5), calls=%async_computation.7 | async-start | bytes 2359296 | tf_op jit(solution)/shard_map/all_to_all | solution.py:618
  228.5 1.9 collective-permute-done.8.other_ref
  230.4 2.1 shard_map.124
  232.5 13.4 %all-to-all-done.7.got_ref.got_hbm = bf16[16,144,256]{2,1,0:T(8,128)(2,1)S(1)} async-done(((bf16[16,144,256]{2,1,0:T(8,128)(2,1)}), bf16[16,144,256]{2,1,0:T(8,128)(2,1)S(1)}, u32[]{:S(2)}, u32[]{:S(2)}) %all-to-all-start.7) | async-done | bytes 1179680 | tf_op jit(solution)/shard_map/all_to_all | solution.py:618
  246.9 6.3 %all-to-all-start.8 = ((bf16[8,128,256]{2,1,0:T(8,128)(2,1)}), bf16[8,128,256]{2,1,0:T(8,128)(2,1)}, u32[]{:S(2)}, u32[]{:S(2)}) async-start(bf16[8,128,256]{2,1,0:T(8,128)(2,1)} %copy-done.4), calls=%async_computation.8 | async-start | bytes 1048576 | tf_op jit(solution)/shard_map/all_to_all | solution.py:618
  255.8 8.6 %shard_map.127 = f32[256,1024]{1,0:T(8,128)} custom-call(bf16[16,1024,256]{2,1,0:T(8,128)(2,1)} %get-tuple-element.40.expo_hbm, bf16[16,1024,256]{2,1,0:T(8,128)(2,1)} %get-tuple-element.67.raised_hbm, f32[1024,128]{1,0:T(8,128)S(1)} %copy-done.11, bf16[16,144,256]{2,1,0:T(8,128)(2,1)S(1)} %all-to-all-done.7.got_ref.got_hbm, ...), custom_call_target="tpu_custom_call" | custom-call | tf_op jit(solution)/shard_map/pallas_call | solution.py:33
  264.5 2.0 shard_map.126
  (87 shorter events, 30.0 us)
Async XLA Ops:
  7.2 3.3 %copy-start.14 = (bf16[1024,256]{1,0:T(8,128)(2,1)S(1)}, bf16[1024,256]{1,0:T(8,128)(2,1)}, u32[]{:S(2)}) copy-start(bf16[1024,256]{1,0:T(8,128)(2,1)} %feats_ref.1) | copy-start | bytes 1572868
  7.2 66.3 %all-gather.3.cloned.1.call-start = ((), (), s32[]{:S(2)}) async-start(), calls=%async_computation.9 | async-start | bytes 4456448 | tf_op jit(solution)/shard_map/all_gather | solution.py:677
  10.4 136.4 %all-gather.5.cloned.1.call-start = ((), (), s32[]{:S(2)}) async-start(), calls=%async_computation.10 | async-start | bytes 2228224 | tf_op jit(solution)/shard_map/all_gather | solution.py:708
  14.9 31.2 %copy-start.2 = (bf16[256,1024]{1,0:T(8,128)(2,1)S(1)}, bf16[256,1024]{1,0:T(8,128)(2,1)}, u32[]{:S(2)}) copy-start(bf16[256,1024]{1,0:T(8,128)(2,1)} %proto_ref.1) | copy-start | bytes 1572868
  14.9 31.2 %copy-start.15 = (bf16[256,1024]{1,0:T(8,128)(2,1)S(1)}, bf16[256,1024]{1,0:T(8,128)(2,1)}, u32[]{:S(2)}) copy-start(bf16[256,1024]{1,0:T(8,128)(2,1)} %teacher_ref.1) | copy-start | bytes 1572868
  43.9 4.7 %collective-permute-start = (bf16[16,144,256]{2,1,0:T(8,128)(2,1)S(1)}, bf16[16,144,256]{2,1,0:T(8,128)(2,1)S(1)}, u32[]{:S(2)}, u32[]{:S(2)}) collective-permute-start(bf16[16,144,256]{2,1,0:T(8,128)(2,1)S(1)} %all_to_all.45.own_hbm), channel_id=1, source_target_pairs={{0,1},{1,0},{2,3},{3,2},{4,5},{5,4},{6,7},{7,6},{8,9},{9,8},{10,11... | collective-permute-start | bytes 3538952 | tf_op jit(solution)/shard_map/ppermute | solution.py:623
  81.6 31.2 %copy-start.12 = (bf16[256,1024]{1,0:T(8,128)(2,1)}, bf16[256,1024]{1,0:T(8,128)(2,1)S(1)}, u32[]{:S(2)}) copy-start(bf16[256,1024]{1,0:T(8,128)(2,1)S(1)} %get-tuple-element.59.hidden_ref) | copy-start | bytes 1572868
  81.6 2.0 collective-permute-start.2
  141.4 4.1 %collective-permute-start.1 = (bf16[16,272,128]{2,1,0:T(8,128)(2,1)S(1)}, bf16[16,272,128]{2,1,0:T(8,128)(2,1)S(1)}, u32[]{:S(2)}, u32[]{:S(2)}) collective-permute-start(bf16[16,272,128]{2,1,0:T(8,128)(2,1)S(1)} %get-tuple-element.45), channel_id=1, source_target_pairs={{0,1},{1,0},{2,3},{3,2},{4,5},{5,4},{6,7},{7,6},{8,9},{9,8},{10,11... | collective-permute-start | bytes 3342344 | tf_op jit(solution)/shard_map/ppermute | solution.py:623
  145.6 1.3 copy-start.17
  146.9 1.6 copy-start
  156.8 4.2 %collective-permute-start.3 = (bf16[16,272,128]{2,1,0:T(8,128)(2,1)}, bf16[16,272,128]{2,1,0:T(8,128)(2,1)}, u32[]{:S(2)}, u32[]{:S(2)}) collective-permute-start(bf16[16,272,128]{2,1,0:T(8,128)(2,1)} %get-tuple-element.53), channel_id=1, source_target_pairs={{0,1},{1,0},{2,3},{3,2},{4,5},{5,4},{6,7},{7,6},{8,9},{9,8},{10,11... | collective-permute-start | bytes 3342344 | tf_op jit(solution)/shard_map/ppermute | solution.py:623
  157.2 23.0 %all-to-all-start.5 = ((bf16[16,272,128]{2,1,0:T(8,128)(2,1)}), bf16[16,272,128]{2,1,0:T(8,128)(2,1)S(1)}, u32[]{:S(2)}, u32[]{:S(2)}) async-start(bf16[16,272,128]{2,1,0:T(8,128)(2,1)} %add_convert_fusion.1), calls=%async_computation.5 | async-start | bytes 2228224 | tf_op jit(solution)/shard_map/all_to_all | solution.py:618
  180.2 20.4 %all-to-all-start.6 = ((bf16[16,272,128]{2,1,0:T(8,128)(2,1)}), bf16[16,272,128]{2,1,0:T(8,128)(2,1)S(1)}, u32[]{:S(2)}, u32[]{:S(2)}) async-start(bf16[16,272,128]{2,1,0:T(8,128)(2,1)} %add_convert_fusion), calls=%async_computation.6 | async-start | bytes 2228224 | tf_op jit(solution)/shard_map/all_to_all | solution.py:618
  186.5 29.2 %copy-start.7 = (f32[256,1024]{1,0:T(8,128)S(1)}, f32[256,1024]{1,0:T(8,128)}, u32[]{:S(2)}) copy-start(f32[256,1024]{1,0:T(8,128)} %copy-done.6) | copy-start | bytes 3145732
  186.5 29.2 %copy-start.23 = (bf16[16,256]{1,0:T(8,128)(2,1)S(1)}, bf16[16,256]{1,0:T(8,128)(2,1)}, u32[]{:S(2)}) copy-start(bf16[16,256]{1,0:T(8,128)(2,1)} %copy-done.22) | copy-start | bytes 24580
  186.5 29.2 %copy-start.25 = (f32[8,256]{1,0:T(8,128)S(1)}, f32[8,256]{1,0:T(8,128)}, u32[]{:S(2)}) copy-start(f32[8,256]{1,0:T(8,128)} %copy-done.24) | copy-start | bytes 24580
  200.6 1.9 copy-start.9
  200.6 15.1 %copy-start.13 = (bf16[256,1024]{1,0:T(8,128)(2,1)S(1)}, bf16[256,1024]{1,0:T(8,128)(2,1)}, u32[]{:S(2)}) copy-start(bf16[256,1024]{1,0:T(8,128)(2,1)} %copy-done.12) | copy-start | bytes 1572868
  200.6 15.1 %copy-start.20 = (f32[256,256]{1,0:T(8,128)S(1)}, f32[256,256]{1,0:T(8,128)}, u32[]{:S(2)}) copy-start(f32[256,256]{1,0:T(8,128)} %copy-done.19) | copy-start | bytes 786436
  202.5 5.5 %collective-permute-start.5 = (bf16[2,272,128]{2,1,0:T(8,128)(2,1)S(1)}, bf16[2,272,128]{2,1,0:T(8,128)(2,1)S(1)}, u32[]{:S(2)}, u32[]{:S(2)}) collective-permute-start(bf16[2,272,128]{2,1,0:T(8,128)(2,1)S(1)} %pad_maximum_fusion), channel_id=1, source_target_pairs={{0,4},{1,5},{2,6},{3,7},{4,0},{5,1},{6,2},{7,3},{8,12},{9,13},{10,... | collective-permute-start | bytes 417800 | tf_op jit(solution)/shard_map/ppermute | solution.py:634
  204.2 4.5 %collective-permute-start.4 = (bf16[2,272,128]{2,1,0:T(8,128)(2,1)S(1)}, bf16[2,272,128]{2,1,0:T(8,128)(2,1)S(1)}, u32[]{:S(2)}, u32[]{:S(2)}) collective-permute-start(bf16[2,272,128]{2,1,0:T(8,128)(2,1)S(1)} %pad_maximum_fusion), channel_id=1, source_target_pairs={{0,2},{1,3},{2,0},{3,1},{4,6},{5,7},{6,4},{7,5},{8,10},{9,11},{10,... | collective-permute-start | bytes 417800 | tf_op jit(solution)/shard_map/ppermute | solution.py:634
  204.8 6.7 %collective-permute-start.6 = (bf16[2,272,128]{2,1,0:T(8,128)(2,1)S(1)}, bf16[2,272,128]{2,1,0:T(8,128)(2,1)S(1)}, u32[]{:S(2)}, u32[]{:S(2)}) collective-permute-start(bf16[2,272,128]{2,1,0:T(8,128)(2,1)S(1)} %pad_maximum_fusion), channel_id=1, source_target_pairs={{0,6},{1,7},{2,4},{3,5},{4,2},{5,3},{6,0},{7,1},{8,14},{9,15},{10,... | collective-permute-start | bytes 417800 | tf_op jit(solution)/shard_map/ppermute | solution.py:634
  211.6 4.1 %collective-permute-start.7 = (f32[2,272,128]{2,1,0:T(8,128)S(1)}, f32[2,272,128]{2,1,0:T(8,128)S(1)}, u32[]{:S(2)}, u32[]{:S(2)}) collective-permute-start(f32[2,272,128]{2,1,0:T(8,128)S(1)} %add_add_fusion.both_ref), channel_id=1, source_target_pairs={{0,1},{1,0},{2,3},{3,2},{4,5},{5,4},{6,7},{7,6},{8,9},{9,8},{10,11... | collective-permute-start | bytes 835592 | tf_op jit(solution)/shard_map/ppermute | solution.py:623
  222.5 1.1 copy-start.5
  224.1 21.8 %all-to-all-start.7 = ((bf16[16,144,256]{2,1,0:T(8,128)(2,1)}), bf16[16,144,256]{2,1,0:T(8,128)(2,1)S(1)}, u32[]{:S(2)}, u32[]{:S(2)}) async-start(bf16[16,144,256]{2,1,0:T(8,128)(2,1)} %copy-done.5), calls=%async_computation.7 | async-start | bytes 2359296 | tf_op jit(solution)/shard_map/all_to_all | solution.py:618
  227.8 2.6 collective-permute-start.8
  232.5 20.6 %copy-start.28 = (f32[8,128]{1,0:T(8,128)S(1)}, f32[8,128]{1,0:T(8,128)}, u32[]{:S(2)}) copy-start(f32[8,128]{1,0:T(8,128)} %copy-done.27) | copy-start | bytes 12292
  232.5 21.2 %copy-start.1 = (bf16[4096,256]{1,0:T(8,128)(2,1)S(1)}, bf16[4096,256]{1,0:T(8,128)(2,1)}, u32[]{:S(2)}) copy-start(bf16[4096,256]{1,0:T(8,128)(2,1)} %all-gather.5.cloned.1.call-done) | copy-start | bytes 6291460
  246.9 17.6 %all-to-all-start.8 = ((bf16[8,128,256]{2,1,0:T(8,128)(2,1)}), bf16[8,128,256]{2,1,0:T(8,128)(2,1)}, u32[]{:S(2)}, u32[]{:S(2)}) async-start(bf16[8,128,256]{2,1,0:T(8,128)(2,1)} %copy-done.4), calls=%async_computation.8 | async-start | bytes 1048576 | tf_op jit(solution)/shard_map/all_to_all | solution.py:618
  253.8 1.0 copy-start.3
  254.8 1.0 copy-start.11
  (12 other events, 9.0 us)
Sparse Core Ops, SparseCore 0:
  10.7 62.7 all-gather.2
  85.9 42.8 all-gather.4
where the time goes:
time: 274 us; the launch traced here: 273 us
  waiting for transfers between devices  75.1 us (27%)
  blocking collectives  69.6 us (25%)
  Pallas kernels  66.3 us (24%)
  starting transfers between devices  29.6 us (11%)
  local copies, waits for them, and re-layouts  14.4 us (5%)
  between operations  14.4 us (5%)
  other arithmetic  4 us (1%)
    all_to_all x5, blocking collectives, exchange(): return lax.all_to_all(x, axis, split_axis=0, concat_axis=0, tiled=True)  69.6 us
    pallas_call x18, Pallas kernels, call(): pl.pallas_call(body, out_shape=outs, in_specs=in_specs or [VMEM] * len(in...  66.3 us
    all_to_all x4, waiting for transfers between devices, exchange(): return lax.all_to_all(x, axis, split_axis=0, concat_axis=0, tiled=True)  44.3 us
    all_to_all x4, starting transfers between devices, exchange(): return lax.all_to_all(x, axis, split_axis=0, concat_axis=0, tiled=True)  17.3 us
    all_gather x1, waiting for transfers between devices, parts_of(): lax.all_gather(w_pack, 'dp', axis=0, tiled=True).reshape(dp, lines, half)  17.3 us
    unnamed x58, local copies, waits for them, and re-layouts  13.8 us
    ppermute x6, starting transfers between devices, sibling(): return lax.ppermute(x, 'tensor', [(i, i ^ 1) for i in range(peers)])  8.82 us
    ppermute x6, waiting for transfers between devices, sibling(): return lax.ppermute(x, 'tensor', [(i, i ^ 1) for i in range(peers)])  7.84 us
  transfers between devices with their start and end apart: 15, of which 12 were waited for; matrix products, arithmetic and copies ran while one was open for 2% of the time, Pallas kernels for 14%

commit v1 on v0

--- a/solution.py
+++ b/solution.py
@@ -13,7 +13,8 @@
 INTERPRET = False
 f32, bf16 = (jnp.float32, jnp.bfloat16)
 VMEM = pl.BlockSpec(memory_space=pltpu.VMEM)
-HBM = pl.BlockSpec(memory_space=pl.ANY)
+HBM = pl.BlockSpec(memory_space=pltpu.HBM)
+ANY = pl.BlockSpec(memory_space=pl.ANY)
 SMEM = pl.BlockSpec(memory_space=pltpu.SMEM)
 NT = (((1,), (1,)), ((), ()))
 TN = (((0,), (0,)), ((), ()))
@@ -29,12 +30,15 @@
 
 
 def call(body, outs, ins, out_specs=None, in_specs=None, scratch=()):
-    outs = tuple(jax.ShapeDtypeStruct(s, d) for s, d in outs)
+    specs = out_specs or [VMEM] * len(outs)
+    in_specs = in_specs or [VMEM] * len(ins)
+    ins = [pltpu.with_memory_space_constraint(x, pltpu.HBM) if spec is HBM else x for x, spec in zip(ins, in_specs)]
+    outs = tuple(pltpu.HBM(*o) if spec is HBM else jax.ShapeDtypeStruct(*o) for o, spec in zip(outs, specs))
     return pl.pallas_call(
         body,
         out_shape=outs,
-        in_specs=in_specs or [VMEM] * len(ins),
-        out_specs=tuple(out_specs or [VMEM] * len(outs)),
+        in_specs=in_specs,
+        out_specs=tuple(specs),
         scratch_shapes=list(scratch),
         interpret=INTERPRET,
         compiler_params=pltpu.CompilerParams(vmem_limit_bytes=48 << 20),
@@ -85,7 +89,9 @@
     lax.fori_loop(0, peers // GROUP, go, 0)
 
 
-def select_body(at_ref, mask_ref, feats_ref, sel_ref, send_hbm, member_ref, mine_ref, unit_ref, pack_ref, sems):
+def select_body(
+    at_ref, mask_ref, feats_ref, sel_ref, send_hbm, member_hbm, mine_hbm, unit_ref, pack_ref, member_ref, mine_ref, sems, late_sems
+):
     crops, patches = mask_ref.shape
     mask = mask_ref[...].astype(f32)
     upto = (iota((patches, patches), 0) <= iota((patches, patches), 1)).astype(f32).astype(bf16)
@@ -116,15 +122,22 @@
     at = iota((EXTRA, CAP), 0)
     tail = jnp.where(at == 0, live, jnp.where(at == 1, weight * GRAD_SCALE, 0.0)).astype(bf16)
     mine_ref[...] = tail
+    late = copies([(member_ref, member_hbm), (mine_ref, mine_hbm)], late_sems)
+    for copy in late:
+        copy.start()
     pack_ref[0:HALF, :] = unit_ref[pl.ds(pl.multiple_of(at_ref[0] * HALF, HALF), HALF), :]
     pack_ref[HALF : HALF + EXTRA, :] = tail
     peers = send_hbm.shape[0]
     make = lambda g: pltpu.make_async_copy(pack_ref, send_hbm.at[g], sems.at[g])
     start_all(peers, make)
+    for copy in late:
+        copy.wait()
     wait_all(peers, make)
 
 
-def columns_body(student_ref, teacher_ref, cols_ref, student_t_ref, teacher_t_ref, norm_ref):
+def columns_body(
+    student_ref, teacher_ref, cols_hbm, student_t_hbm, teacher_t_hbm, norm_hbm, cols_ref, student_t_ref, teacher_t_ref, norm_ref, sems
+):
     for part in chunks_of(student_ref.shape[1]):
         wide = student_ref[:, part].astype(f32)
         norm = jnp.sqrt(jnp.sum(wide * wide, axis=0, keepdims=True) + EPS)
@@ -135,16 +148,29 @@
         wide = teacher_ref[:, part].astype(f32)
         norm = jnp.sqrt(jnp.sum(wide * wide, axis=0, keepdims=True) + EPS)
         teacher_t_ref[part, :] = (wide / norm).T.astype(bf16)
-
-
-def weights_body(at_ref, w_in_ref, w_out_ref, pack_ref):
-    rows, hid = w_in_ref.shape
+    held = (cols_ref, student_t_ref, teacher_t_ref, norm_ref)
+    stores = copies(list(zip(held, (cols_hbm, student_t_hbm, teacher_t_hbm, norm_hbm))), sems)
+    for store in stores:
+        store.start()
+    for store in stores:
+        store.wait()
+
+
+def weights_body(at_ref, w_in_hbm, w_out_hbm, pack_hbm, sems):
+    rows, hid = w_in_hbm.shape
     half = hid // 2
-    bot = w_out_ref.shape[1]
-    lines = w_out_ref.shape[0] * bot // half
-    pack_ref[0:rows, :] = w_in_ref[:, pl.ds(pl.multiple_of(at_ref[0] * half, half), half)]
+    bot = w_out_hbm.shape[1]
+    lines = w_out_hbm.shape[0] * bot // half
+    column = pl.multiple_of(at_ref[0] * half, half)
+    pairs = [(w_in_hbm.at[:, pl.ds(column, half)], pack_hbm.at[0:rows, :])]
     for q in range(half // bot):
-        pack_ref[rows : rows + lines, q * bot : (q + 1) * bot] = w_out_ref[q * lines : (q + 1) * lines, :]
+        source = w_out_hbm.at[q * lines : (q + 1) * lines, :]
+        pairs.append((source, pack_hbm.at[rows : rows + lines, q * bot : (q + 1) * bot]))
+    moves = copies(pairs, sems)
+    for move in moves:
+        move.start()
+    for move in moves:
+        move.wait()
 
 
 def weight_loads(at_ref, w_hbm, w_in_ref, w_out_ref, sems):
@@ -162,19 +188,29 @@
     return copies(pairs, sems)
 
 
+def tokens_body(sel_ref, tokens_hbm, rows_hbm, tokens_ref, rows_ref, sems):
+    load = pltpu.make_async_copy(tokens_hbm, tokens_ref, sems.at[0])
+    load.start()
+    load.wait()
+    rows_ref[...] = mm(sel_ref[...], tokens_ref[...]).astype(bf16)
+    store = pltpu.make_async_copy(rows_ref, rows_hbm, sems.at[1])
+    store.start()
+    store.wait()
+
+
 def forward_body(
-    at_ref, sel_ref, tokens_hbm, w_hbm, rows_ref, hidden_ref, slope_ref, feats_ref, tokens_ref, w_in_ref, w_out_ref, sems, tsem
+    at_ref, rows_hbm, w_hbm, hidden_hbm, slope_hbm, feats_ref,
+    rows_ref, hidden_ref, slope_ref, w_in_ref, w_out_ref, sems, own_sems,
 ):
-    tokens = pltpu.make_async_copy(tokens_hbm, tokens_ref, tsem)
-    tokens.start()
+    first = pltpu.make_async_copy(rows_hbm, rows_ref, own_sems.at[0])
+    first.start()
     loads = weight_loads(at_ref, w_hbm, w_in_ref, w_out_ref, sems)
     for load in loads:
         load.start()
-    tokens.wait()
-    rows = mm(sel_ref[...], tokens_ref[...]).astype(bf16)
-    rows_ref[...] = rows
+    first.wait()
     for load in loads:
         load.wait()
+    rows = rows_ref[...]
     feats = jnp.zeros(feats_ref.shape, f32)
     for part in chunks_of(hidden_ref.shape[1]):
         pre = mm(rows, w_in_ref[:, part])
@@ -184,15 +220,21 @@
         hidden_ref[:, part] = hidden
         feats = feats + mm(hidden, w_out_ref[part, :])
     feats_ref[...] = feats
-
-
-def unit_body(feats_ref, other_ref, unit_ref, inv_ref, rows_ref):
+    stores = copies([(hidden_ref, hidden_hbm), (slope_ref, slope_hbm)], own_sems)
+    for store in stores:
+        store.start()
+    for store in stores:
+        store.wait()
+
+
+def unit_of(feats_ref, other_ref):
     feats = feats_ref[...] + other_ref[...]
     inv = lax.rsqrt(jnp.sum(feats * feats, axis=1, keepdims=True) + EPS)
-    unit = feats * inv
-    unit_ref[...] = unit.T
-    inv_ref[...] = jnp.broadcast_to(inv, feats.shape).T[0:8]
-    rows_ref[...] = unit.astype(bf16)
+    return (feats * inv, inv)
+
+
+def unit_body(feats_ref, other_ref, rows_ref):
+    rows_ref[...] = unit_of(feats_ref, other_ref)[0].astype(bf16)
 
 
 def chunks_of(width):
@@ -209,8 +251,8 @@
 
 
 def expo_body(
-    at_ref, cols_ref, own_hbm, other_hbm, expo_hbm, part_ref, live_ref, weight_ref,
-    rows_ref, tail_ref, expo_ref, total_ref, sums_ref, sems, own_sems, other_sems, tail_sems,
+    at_ref, cols_hbm, own_hbm, other_hbm, expo_hbm, part_ref, live_ref,
+    cols_ref, rows_ref, tail_ref, expo_ref, total_ref, sums_ref, sems, own_sems, other_sems, tail_sems,
 ):
     peers = own_hbm.shape[0]
     width = cols_ref.shape[0]
@@ -222,18 +264,20 @@
     load_other = lambda q: pltpu.make_async_copy(rows_of(other_hbm, q), rows_at(q, 1 - core), other_sems.at[q])
     load_tail = pltpu.make_async_copy(own_hbm.at[:, HALF : HALF + EXTRA, :], tail_ref, tail_sems.at[0])
     store = lambda q: pltpu.make_async_copy(group(expo_ref, q), group(expo_hbm, q), sems.at[q])
+    load_cols = pltpu.make_async_copy(cols_hbm, cols_ref, tail_sems.at[1])
+    load_cols.start()
     load_tail.start()
     start_all(number, load_own)
     start_all(number, load_other)
     total_ref[...] = jnp.zeros_like(total_ref)
     load_tail.wait()
+    load_cols.wait()
 
     def first(g):
         rows = rows_ref[g].reshape(CAP, rows_ref.shape[3])
         tail = tail_ref[g].astype(f32)
         live = tail[0:1]
         live_ref[pl.ds(g, 1), :] = live
-        weight_ref[pl.ds(g, 1), :] = tail[1:2]
         for part in chunks_of(width):
             cos = mm(cols_ref[part, :], rows, NT)
             expo = jnp.exp(cos * (1.0 / TEACHER_TEMP)) * live
@@ -320,8 +364,8 @@
 
 
 def last_body(
-    at_ref, expo_hbm, parts_ref, live_ref, cols_ref, keep_hbm, give_hbm, total_ref,
-    expo_ref, scale_ref, halves_ref, sems, keep_sems, give_sems,
+    at_ref, expo_hbm, parts_ref, live_ref, cols_ref, keep_hbm, give_hbm, total_hbm,
+    expo_ref, total_ref, scale_ref, halves_ref, sems, keep_sems, give_sems,
 ):
     peers = expo_ref.shape[0]
     core = at_ref[0]
@@ -344,9 +388,12 @@
         divide_up(g, acc, pull, halves_ref)
         return 0
 
+    spare = pltpu.make_async_copy(total_ref, total_hbm, sems.at[0])
+    spare.start()
     over_groups(peers, step, (), (give, keep), UNROLL)
     wait_all(number, give)
     wait_all(number, keep)
+    spare.wait()
 
 
 def student_body(
@@ -383,8 +430,8 @@
 
 
 def columns_grad_body(
-    expo_hbm, raised_hbm, scale_ref, got_hbm, rows_hbm, proto_ref, norm_ref,
-    grad_ref, expo_ref, raised_ref, acc_ref, tail_ref, rows_ref, esems, rsems, tail_sems, row_sems,
+    expo_hbm, raised_hbm, scale_hbm, got_hbm, rows_hbm, proto_hbm, norm_hbm,
+    grad_ref, scale_ref, proto_ref, norm_ref, expo_ref, raised_ref, acc_ref, tail_ref, rows_ref, esems, rsems, tail_sems, row_sems, late_sems,
 ):
     peers = expo_ref.shape[0]
     load = lambda q: pltpu.make_async_copy(group(expo_hbm, q), group(expo_ref, q), esems.at[q])
@@ -392,7 +439,10 @@
     load_rows = lambda q: pltpu.make_async_copy(group(rows_hbm, q), group(rows_ref, q), row_sems.at[q])
     lines = got_hbm.shape[1] - EXTRA
     load_tail = pltpu.make_async_copy(got_hbm.at[:, lines : lines + EXTRA, :], tail_ref, tail_sems.at[0])
+    load_scale = pltpu.make_async_copy(scale_hbm, scale_ref, tail_sems.at[1])
+    late = copies([(proto_hbm, proto_ref), (norm_hbm, norm_ref)], late_sems)
     load_tail.start()
+    load_scale.start()
 
     def begin(q, _):
         for make in (load_rows, load, load_raised):
@@ -400,8 +450,11 @@
         return 0
 
     lax.fori_loop(0, peers // GROUP, begin, 0)
+    for copy in late:
+        copy.start()
     acc_ref[...] = jnp.zeros_like(acc_ref)
     load_tail.wait()
+    load_scale.wait()
 
     def step(g):
         tail = tail_ref[g].astype(f32)
@@ -415,6 +468,8 @@
         return 0
 
     over_groups(peers, step, (load_rows, load, load_raised), (), UNROLL)
+    for copy in late:
+        copy.wait()
     for part in chunks_of(acc_ref.shape[0]):
         grad = acc_ref[part, :].T
         norm = norm_ref[:, part]
@@ -434,8 +489,8 @@
 
 
 def backward_body(
-    at_ref, both_ref, other_ref, mine_ref, member_ref, unit_ref, inv_ref, rows_ref, hidden_ref, slope_ref, w_hbm,
-    send_hbm, grad_rows_ref, loss_ref, w_in_ref, w_out_ref, send_ref, pre_ref, out_ref, sems, send_sems,
+    at_ref, both_ref, other_ref, mine_ref, member_ref, feats_ref, feats_other_ref, rows_ref, hidden_ref, slope_ref, w_hbm,
+    send_hbm, grad_rows_hbm, loss_ref, w_in_ref, w_out_ref, send_ref, pre_ref, out_ref, grad_rows_ref, sems, send_sems, rows_sem,
 ):
     peers = w_hbm.shape[0]
     loads = weight_loads(at_ref, w_hbm, w_in_ref, w_out_ref, sems)
@@ -449,16 +504,20 @@
     push = push[0:CAP]
     scale = live / (pull[CAP : CAP + 1] + 1.0 - live)
     pull = pull[0:CAP]
-    unit = unit_ref[...]
+    unit, inv = unit_of(feats_ref, feats_other_ref)
+    inv = jnp.broadcast_to(inv, unit.shape).T[0:1]
+    unit = unit.T
     cross = jnp.sum(unit.astype(bf16).astype(f32) * pull, axis=0, keepdims=True) * (1.0 / STUDENT_TEMP)
     row_loss = jnp.log(norm_sum) - scale * cross
     loss = jnp.sum(member_ref[...] * row_loss, axis=1, keepdims=True)
-    loss_ref[...] = jnp.broadcast_to(loss, loss_ref.shape)
+    square = (member_ref.shape[0], 128)
+    loss = jnp.where(iota(square, 0) == iota(square, 1), loss, 0.0)
+    loss_ref[...] = jnp.sum(loss, axis=0, keepdims=True)[:, 0 : loss_ref.shape[1]]
     alpha = weight / norm_sum
     beta = weight * scale
     grad_unit = push * alpha - pull * beta
     inner = jnp.sum(unit * grad_unit, axis=0, keepdims=True)
-    grad_feats = (inv_ref[0:1] * (grad_unit - unit * inner)).T.astype(bf16)
+    grad_feats = (inv * (grad_unit - unit * inner)).T.astype(bf16)
     for load in loads:
         load.wait()
     width = send_ref.shape[2]
@@ -469,6 +528,8 @@
         grad_rows = grad_rows + mm(grad_pre, w_in_ref[:, part], NT)
         out_ref[part, :] = mm(hidden_ref[:, part], grad_feats, TN).astype(bf16)
     grad_rows_ref[...] = grad_rows.astype(bf16)
+    rows_out = pltpu.make_async_copy(grad_rows_ref, grad_rows_hbm, rows_sem.at[0])
+    rows_out.start()
     core, level = (at_ref[0], at_ref[1])
     own = pre_ref[:, pl.ds(pl.multiple_of(level * width, width), width)]
     grad_in = mm(rows_ref[...], own, TN).astype(bf16)
@@ -488,6 +549,7 @@
         send_ref[g, per : per + share, :] = jnp.where(core == g // (peers // 2), out, jnp.zeros_like(out))
         send_ref[g, per + share : per + share + EXTRA, :] = rows
         store(g).start()
+    rows_out.wait()
     wait_all(peers, store)
 
 
@@ -502,15 +564,20 @@
     wait_all(pieces, store)
 
 
-def gather_grads_body(got_ref, send_ref):
-    peers = got_ref.shape[0]
-    lines = send_ref.shape[1]
-    acc = got_ref[0, 0:lines, :].astype(f32)
+def gather_grads_body(got_hbm, send_hbm, got_ref, sum_ref, load_sems, sems):
+    peers = got_hbm.shape[0]
+    lines = sum_ref.shape[0]
+    load = lambda g: pltpu.make_async_copy(got_hbm.at[g, 0:lines, :], got_ref.at[g], load_sems.at[g])
+    start_all(peers, load)
+    load(0).wait()
+    acc = got_ref[0].astype(f32)
     for g in range(1, peers):
-        acc = acc + got_ref[g, 0:lines, :].astype(f32)
-    acc = acc.astype(bf16)
-    for t in range(send_ref.shape[0]):
-        send_ref[t] = acc
+        load(g).wait()
+        acc = acc + got_ref[g].astype(f32)
+    sum_ref[...] = acc.astype(bf16)
+    store = lambda t: pltpu.make_async_copy(sum_ref, send_hbm.at[t], sems.at[t])
+    start_all(send_hbm.shape[0], store)
+    wait_all(send_hbm.shape[0], store)
 
 
 def weight_grads_body(at_ref, parts_ref, grad_in_ref, grad_out_ref):
@@ -533,11 +600,12 @@
     big, small = ((dp, width, CAP), (dp, CAP))
     return call(
         expo_body,
-        [(big, bf16), ((tensor, *small), bf16), (small, f32), (small, f32)],
+        [(big, bf16), ((tensor, *small), bf16), (small, f32)],
         (at, cols_t, own, other),
-        in_specs=[SMEM, VMEM, HBM, HBM],
-        out_specs=[HBM, VMEM, VMEM, VMEM],
+        in_specs=[SMEM, HBM, ANY, ANY],
+        out_specs=[HBM, VMEM, VMEM],
         scratch=[
+            pltpu.VMEM((width, bot), bf16),
             pltpu.VMEM((dp, 2, HALF, bot), bf16),
             pltpu.VMEM((dp, EXTRA, bot), bf16),
             pltpu.VMEM(big, bf16),
@@ -568,9 +636,10 @@
         [(halves, bf16), (halves, bf16), ((width, 128), f32)],
         (at, expo, got, live, cols),
         in_specs=[SMEM, HBM, VMEM, VMEM, VMEM],
-        out_specs=[HBM, HBM, VMEM],
+        out_specs=[HBM, HBM, HBM],
         scratch=[
             pltpu.VMEM(expo.shape, bf16),
+            pltpu.VMEM((width, 128), f32),
             pltpu.VMEM(live.shape, f32),
             pltpu.VMEM((2, *halves), bf16),
             *[sem(dp // GROUP)] * 3,
@@ -602,14 +671,18 @@
         columns_grad_body,
         [(proto.shape, f32)],
         (expo, raised, scale, got, rows, proto, norm),
-        in_specs=[HBM, HBM, VMEM, HBM, HBM, VMEM, VMEM],
+        in_specs=[HBM] * 3 + [ANY] + [HBM] * 3,
         scratch=[
+            pltpu.VMEM(scale.shape, f32),
+            pltpu.VMEM(proto.shape, bf16),
+            pltpu.VMEM(norm.shape, f32),
             held,
             held,
             pltpu.VMEM(proto.shape[::-1], f32),
             pltpu.VMEM((dp, EXTRA, CAP), bf16),
             pltpu.VMEM(rows.shape, bf16),
             *[sem(dp // GROUP)] * 4,
+            sem(2),
         ],
     )[0]
 
@@ -638,7 +711,11 @@
     return (keep.astype(f32) + sibling(give).astype(f32)).astype(bf16)
 
 
-def slot_sums_body(parts_hbm, out_ref, parts_ref, sems):
+def slot_sums_body(*refs):
+    *earlier, parts_hbm, out_hbm, parts_ref, out_ref, sems, out_sem = refs
+    moves = [pltpu.make_async_copy(ref.at[0], out_ref.at[0], out_sem.at[0]) for ref in earlier]
+    for move in moves:
+        move.start()
     peers = parts_hbm.shape[0]
     load = lambda g: pltpu.make_async_copy(parts_hbm.at[g], parts_ref.at[g], sems.at[g])
     start_all(peers, load)
@@ -647,13 +724,24 @@
     for g in range(1, peers):
         load(g).wait()
         acc = acc + parts_ref[g].astype(f32)
-    out_ref[...] = acc.astype(bf16)
-
-
-def slot_sums(parts):
-    out = parts.shape[1:]
-    scratch = [pltpu.VMEM(parts.shape, bf16), pltpu.SemaphoreType.DMA((parts.shape[0],))]
-    return call(slot_sums_body, [(out, bf16)], (parts,), in_specs=[HBM], scratch=scratch)[0]
+    out_ref[len(earlier)] = acc.astype(bf16)
+    for move in moves:
+        move.wait()
+    store = pltpu.make_async_copy(out_ref, out_hbm, out_sem.at[0])
+    store.start()
+    store.wait()
+
+
+def slot_sums(parts, *earlier):
+    out = (1 + len(earlier), *parts.shape[1:])
+    return call(
+        slot_sums_body,
+        [(out, bf16)],
+        (*earlier, parts),
+        in_specs=[HBM] * len(earlier) + [ANY],
+        out_specs=[HBM],
+        scratch=[pltpu.VMEM(parts.shape, bf16), pltpu.VMEM(out, bf16), sem(parts.shape[0]), sem(1)],
+    )[0]
 
 
 def after(x, earlier):
@@ -673,7 +761,7 @@
     at = jnp.stack([t % 2, t // 2, g // (dp // 2)])
 
     lines = per + w_out.shape[0] * bot // half
-    (w_pack,) = call(weights_body, [((lines, half), bf16)], (at, w_in, w_out), in_specs=[SMEM, VMEM, VMEM])
+    (w_pack,) = call(weights_body, [((lines, half), bf16)], (at, w_in, w_out), in_specs=[SMEM, HBM, HBM], out_specs=[HBM], scratch=[sem(1 + half // bot)])
     w_all = lax.all_gather(w_pack, "dp", axis=0, tiled=True).reshape(dp, lines, half)
     dma = pltpu.SemaphoreType.DMA
     sems = dma((dp,))
@@ -682,8 +770,15 @@
         [((CAP, tokens.shape[0]), bf16), ((dp, HALF + EXTRA, bot), bf16), ((8, CAP), f32), ((EXTRA, CAP), bf16)],
         (at, masks, teacher_feats),
         in_specs=[SMEM, VMEM, VMEM],
-        out_specs=[VMEM, HBM, VMEM, VMEM],
-        scratch=[pltpu.VMEM((CAP, bot), bf16), pltpu.VMEM((HALF + EXTRA, bot), bf16), sems],
+        out_specs=[VMEM, HBM, HBM, HBM],
+        scratch=[
+            pltpu.VMEM((CAP, bot), bf16),
+            pltpu.VMEM((HALF + EXTRA, bot), bf16),
+            pltpu.VMEM((8, CAP), f32),
+            pltpu.VMEM((EXTRA, CAP), bf16),
+            sems,
+            sem(2),
+        ],
     )
     packs = exchange(send, "dp")
     others = sibling(packs)
@@ -691,20 +786,43 @@
         columns_body,
         [((bot, width), bf16), ((width, bot), bf16), ((width, bot), bf16), ((1, width), f32)],
         (proto_student, proto_teacher),
-    )
-    expo, part, live, _ = run_expo(at, teacher_t, packs, others, tensor)
+        out_specs=[HBM] * 4,
+        scratch=[
+            pltpu.VMEM((bot, width), bf16),
+            pltpu.VMEM((width, bot), bf16),
+            pltpu.VMEM((width, bot), bf16),
+            pltpu.VMEM((1, width), f32),
+            sem(4),
+        ],
+    )
+    expo, part, live = run_expo(at, teacher_t, packs, others, tensor)
     loads = dma((dp + 2 * dp,))
     w_held = [pltpu.VMEM((dim, half), bf16), pltpu.VMEM((half, bot), bf16)]
-    rows, hidden, slope, feats = call(
+    (rows,) = call(
+        tokens_body,
+        [((CAP, dim), bf16)],
+        (sel, tokens),
+        in_specs=[VMEM, HBM],
+        out_specs=[HBM],
+        scratch=[pltpu.VMEM(tokens.shape, bf16), pltpu.VMEM((CAP, dim), bf16), sem(2)],
+    )
+    hidden, slope, feats = call(
         forward_body,
-        [((CAP, dim), bf16), ((CAP, half), bf16), ((CAP, half), f32), ((CAP, bot), f32)],
-        (at, sel, tokens, after(w_all, part)),
-        in_specs=[SMEM, VMEM, HBM, HBM],
-        scratch=[pltpu.VMEM(tokens.shape, bf16), *w_held, loads, dma(())],
-    )
-    unit, inv, student_rows = call(
-        unit_body, [((bot, CAP), f32), ((8, CAP), f32), ((CAP, bot), bf16)], (feats, sibling(feats))
-    )
+        [((CAP, half), bf16), ((CAP, half), f32), ((CAP, bot), f32)],
+        (at, rows, after(w_all, part)),
+        in_specs=[SMEM, HBM, HBM],
+        out_specs=[HBM, HBM, VMEM],
+        scratch=[
+            pltpu.VMEM((CAP, dim), bf16),
+            pltpu.VMEM((CAP, half), bf16),
+            pltpu.VMEM((CAP, half), f32),
+            *w_held,
+            loads,
+            sem(2),
+        ],
+    )
+    feats_other = sibling(feats)
+    (student_rows,) = call(unit_body, [((CAP, bot), bf16)], (feats, feats_other))
     all_rows = lax.all_gather(student_rows, "dp", axis=0, tiled=True).reshape(dp, CAP, bot)
     got = everywhere(part, live.shape)
     part = run_balance(expo, got, live, tensor)
@@ -715,24 +833,26 @@
     all_rows = after(all_rows, pull)
     raised, keep, give = run_student(at, student_t, cols, all_rows)
     push_got = exchange(paired(keep, give), "dp")
-    both = jnp.stack([slot_sums(pull_got), slot_sums(push_got)])
+    both = slot_sums(push_got, slot_sums(pull_got))
     near, far, last = (levels(both, by) for by in (1, 2, 3))
     wide = lambda x: x.astype(f32)
     both = (wide(both) + wide(near)) + (wide(far) + wide(last))
     back_lines = per + share + EXTRA
     send, grad_rows, loss = call(
         backward_body,
-        [((dp, back_lines, bot), bf16), ((CAP, dim), bf16), ((8, 128), f32)],
-        (at, both, sibling(both), mine, member, unit, inv, rows, hidden, slope, w_all),
+        [((dp, back_lines, bot), bf16), ((CAP, dim), bf16), ((1, masks.shape[0]), f32)],
+        (at, both, sibling(both), mine, member, feats, feats_other, rows, hidden, slope, w_all),
         in_specs=[SMEM] + [VMEM] * 9 + [HBM],
-        out_specs=[HBM, VMEM, VMEM],
+        out_specs=[HBM, HBM, VMEM],
         scratch=[
             *w_held,
             pltpu.VMEM((dp, back_lines, bot), bf16),
             pltpu.VMEM((CAP, half), bf16),
             pltpu.VMEM((half, bot), bf16),
+            pltpu.VMEM((CAP, dim), bf16),
             loads,
             sems,
+            sem(1),
         ],
     )
     got = exchange(send, "dp")
@@ -746,13 +866,20 @@
         scratch=[pltpu.VMEM(d_shape, bf16), dma((pieces,))],
     )
     got, d_tokens = lax.optimization_barrier((got, d_tokens))
-    (sent,) = call(gather_grads_body, [((tensor, per + share, bot), bf16)], (got,))
+    (sent,) = call(
+        gather_grads_body,
+        [((tensor, per + share, bot), bf16)],
+        (got,),
+        in_specs=[ANY],
+        out_specs=[HBM],
+        scratch=[pltpu.VMEM((dp, per + share, bot), bf16), pltpu.VMEM((per + share, bot), bf16), sems, sem(tensor)],
+    )
     parts = exchange(sent, "tensor")
     grad_proto = run_columns_grad(expo, raised, scale, got, all_rows, proto_student, norm)
     grad_in, grad_out = call(
         weight_grads_body, [((per, hid), f32), ((w_out.shape[0], bot), f32)], (at, parts), in_specs=[SMEM, VMEM]
     )
-    return (d_tokens.reshape(tokens.shape), grad_in, grad_out, grad_proto, loss[: masks.shape[0], 0])
+    return (d_tokens.reshape(tokens.shape), grad_in, grad_out, grad_proto, loss.reshape(masks.shape[0]))
 
 
 def solution(mesh):

time: 274 us -> 277 us (1.011)
  Pallas kernels: 66.3 us -> 83.2 us
  local copies, waits for them, and re-layouts: 14.4 us -> 1.77 us
  waiting for transfers between devices: 75.1 us -> 69.2 us
    pallas_call x18 -> x19, Pallas kernels: 66.3 us -> 83.2 us  [call(): pl.pallas_call(body, out_shape=outs, in_specs=in_specs, out_specs=tuple(s...]
    unnamed x58 -> x26, local copies, waits for them, and re-layouts: 13.8 us -> 1.77 us
    all_gather x1, waiting for transfers between devices: 17.3 us -> 13.7 us  [parts_of(): lax.all_gather(w_pack, 'dp', axis=0, tiled=True).reshape(dp, lines, half)]
  transfers between devices with their start and end apart: 15 -> 15, of which waited for: 12 -> 11; matrix products, arithmetic and copies ran while one was open for 2% -> 2% of each run, Pallas kernels for 14% -> 16%
where the time goes in v1:
time: 277 us; the launch traced here: 276 us
  Pallas kernels  83.2 us (30%)
  blocking collectives  69.7 us (25%)
  waiting for transfers between devices  69.2 us (25%)
  starting transfers between devices  31.4 us (11%)
  between operations  14.4 us (5%)
  other arithmetic  6.17 us (2%)
    pallas_call x19, Pallas kernels, call(): pl.pallas_call(body, out_shape=outs, in_specs=in_specs, out_specs=tuple(s...  83.2 us
    all_to_all x5, blocking collectives, exchange(): return lax.all_to_all(x, axis, split_axis=0, concat_axis=0, tiled=True)  69.7 us
    all_to_all x4, waiting for transfers between devices, exchange(): return lax.all_to_all(x, axis, split_axis=0, concat_axis=0, tiled=True)  44.1 us
    all_to_all x4, starting transfers between devices, exchange(): return lax.all_to_all(x, axis, split_axis=0, concat_axis=0, tiled=True)  17.7 us
    all_gather x1, waiting for transfers between devices, parts_of(): lax.all_gather(w_pack, 'dp', axis=0, tiled=True).reshape(dp, lines, half)  13.7 us
    ppermute x6, starting transfers between devices, sibling(): return lax.ppermute(x, 'tensor', [(i, i ^ 1) for i in range(peers)])  10.3 us
    ppermute x6, waiting for transfers between devices, sibling(): return lax.ppermute(x, 'tensor', [(i, i ^ 1) for i in range(peers)])  6.86 us
  transfers between devices with their start and end apart: 15, of which 11 were waited for; matrix products, arithmetic and copies ran while one was open for 2% of the time, Pallas kernels for 16%

profile of v1, /device:TPU:1, one launch (start us, length us, event | category | flops | bytes accessed | tf_op | source)
XLA Modules:
  0.0 275.8 jit_solution(8019410817168088352)
XLA Ops:
  7.3 9.6 %shard_map.119 = bf16[128,1024]{1,0:T(8,128)(2,1)} custom-call(s32[3]{0:T(128)S(1)} %pad_add_fusion.at_ref, bf16[96,2048]{1,0:T(8,128)(2,1)} %w_in_hbm.1, bf16[128,256]{1,0:T(8,128)(2,1)} %w_out_hbm.1), custom_call_target="tpu_custom_call" | custom-call | tf_op jit(solution)/shard_map/pallas_call | solution.py:37
  17.7 2.4 shard_map.111
  20.1 29.2 %all_to_all.45.own_hbm = bf16[16,144,256]{2,1,0:T(8,128)(2,1)S(1)} all-to-all(bf16[16,144,256]{2,1,0:T(8,128)(2,1)} %get-tuple-element.35), channel_id=1, replica_groups=mesh['dp'=16,'tensor'=8] {'dp'}, dimensions={0} | all-to-all | bytes 2359296 | tf_op jit(solution)/shard_map/all_to_all | solution.py:691
  49.3 2.2 collective-permute-start
  53.1 3.8 %shard_map.118.rows_hbm.rows_ref = bf16[256,1536]{1,0:T(8,128)(2,1)} custom-call(bf16[256,1024]{1,0:T(8,128)(2,1)S(1)} %get-tuple-element.43.sel_ref, bf16[1024,1536]{1,0:T(8,128)(2,1)} %tokens_hbm.1), custom_call_target="tpu_custom_call" | custom-call | tf_op jit(solution)/shard_map/pallas_call | solution.py:37
  56.9 7.8 %shard_map.112 = (bf16[16,1024,256]{2,1,0:T(8,128)(2,1)}, bf16[8,16,256]{2,1,0:T(8,128)(2,1)S(1)}, f32[16,256]{1,0:T(8,128)S(1)}) custom-call(s32[3]{0:T(128)S(1)} %pad_add_fusion.at_ref, bf16[1024,256]{1,0:T(8,128)(2,1)} %get-tuple-element.34.cols_hbm, bf16[16,144,256]{2,1,0:T(8,128)(2,1)S(1)} %all_to_all.45.own_hbm, ...), custom_call_target="tpu_custom_call" | custom-call | tf_op jit(solution)/shard_map/pallas_call | solution.py:37
  64.7 13.7 %all-gather.3.cloned.1.call-done = bf16[2048,1024]{1,0:T(8,128)(2,1)} async-done(((bf16[128,1024]{1,0:T(8,128)(2,1)}), bf16[2048,1024]{1,0:T(8,128)(2,1)}) %all-gather.3.cloned.1.call-update) | async-done | bytes 4194320 | tf_op jit(solution)/shard_map/all_gather | solution.py:765
  78.4 6.4 %shard_map.120 = (bf16[256,1024]{1,0:T(8,128)(2,1)}, f32[256,1024]{1,0:T(8,128)}, f32[256,256]{1,0:T(8,128)S(1)}) custom-call(s32[3]{0:T(128)S(1)} %pad_add_fusion.at_ref, bf16[256,1536]{1,0:T(8,128)(2,1)} %shard_map.118.rows_hbm.rows_ref, bf16[16,128,1024]{2,1,0:T(8,128)(2,1)} %bitcast.7), custom_call_target="tpu_custom_call" | custom-call | tf_op jit(solution)/shard_map/pallas_call | solution.py:37
  87.7 9.4 %all_to_all.46.parts_ref = bf16[8,16,256]{2,1,0:T(8,128)(2,1)S(1)} all-to-all(bf16[8,16,256]{2,1,0:T(8,128)(2,1)S(1)} %get-tuple-element.37), channel_id=1, replica_groups=mesh['dp'=16,'tensor'=8] {'tensor'}, dimensions={0} | all-to-all | bytes 131072 | tf_op jit(solution)/shard_map/all_to_all | solution.py:691
  97.2 11.7 %all_to_all.47.parts_ref = bf16[16,16,256]{2,1,0:T(8,128)(2,1)S(1)} all-to-all(bf16[16,16,256]{2,1,0:T(8,128)(2,1)S(1)} %shard_map.113), channel_id=1, replica_groups=mesh['dp'=16,'tensor'=8] {'dp'}, dimensions={0} | all-to-all | bytes 262144 | tf_op jit(solution)/shard_map/all_to_all | solution.py:691
  108.8 6.0 %shard_map.114 = bf16[8,16,256]{2,1,0:T(8,128)(2,1)S(1)} custom-call(bf16[16,1024,256]{2,1,0:T(8,128)(2,1)} %get-tuple-element.36.expo_hbm, bf16[16,16,256]{2,1,0:T(8,128)(2,1)S(1)} %all_to_all.47.parts_ref, f32[16,256]{1,0:T(8,128)S(1)} %get-tuple-element.38.live_ref), custom_call_target="tpu_custom_call" | custom-call | tf_op jit(solution)/shard_map/pallas_call | solution.py:37
  114.8 9.4 %all_to_all.48.parts_ref = bf16[8,16,256]{2,1,0:T(8,128)(2,1)S(1)} all-to-all(bf16[8,16,256]{2,1,0:T(8,128)(2,1)S(1)} %shard_map.114), channel_id=1, replica_groups=mesh['dp'=16,'tensor'=8] {'tensor'}, dimensions={0} | all-to-all | bytes 131072 | tf_op jit(solution)/shard_map/all_to_all | solution.py:691
  124.2 10.1 %all_to_all.49.parts_ref = bf16[16,16,256]{2,1,0:T(8,128)(2,1)S(1)} all-to-all(bf16[16,16,256]{2,1,0:T(8,128)(2,1)S(1)} %shard_map.115), channel_id=1, replica_groups=mesh['dp'=16,'tensor'=8] {'dp'}, dimensions={0} | all-to-all | bytes 262144 | tf_op jit(solution)/shard_map/all_to_all | solution.py:691
  134.3 8.6 %shard_map.116 = (bf16[16,272,128]{2,1,0:T(8,128)(2,1)}, bf16[16,272,128]{2,1,0:T(8,128)(2,1)}, f32[1024,128]{1,0:T(8,128)}) custom-call(s32[3]{0:T(128)S(1)} %pad_add_fusion.at_ref, bf16[16,1024,256]{2,1,0:T(8,128)(2,1)} %get-tuple-element.36.expo_hbm, bf16[16,16,256]{2,1,0:T(8,128)(2,1)S(1)} %all_to_all.49.parts_ref, ...), custom_call_target="tpu_custom_call" | custom-call | tf_op jit(solution)/shard_map/pallas_call | solution.py:37
  144.8 2.6 collective-permute-done.1
  147.4 2.6 add_convert_fusion.1
  150.0 9.2 %shard_map.122 = (bf16[16,1024,256]{2,1,0:T(8,128)(2,1)}, bf16[16,272,128]{2,1,0:T(8,128)(2,1)}, bf16[16,272,128]{2,1,0:T(8,128)(2,1)}) custom-call(s32[3]{0:T(128)S(1)} %pad_add_fusion.at_ref, bf16[1024,256]{1,0:T(8,128)(2,1)S(1)} %copy-done.7, bf16[256,1024]{1,0:T(8,128)(2,1)S(1)} %copy-done.2, bf16[16,256,256]{2,1,0:T(8,128)(2,1)} %bitcast.9), custom_call_target="tpu_custom_call" | custom-call | tf_op jit(solution)/shard_map/pallas_call | solution.py:37
  159.8 3.7 %all-to-all-start.5 = ((bf16[16,272,128]{2,1,0:T(8,128)(2,1)}), bf16[16,272,128]{2,1,0:T(8,128)(2,1)S(1)}, u32[]{:S(2)}, u32[]{:S(2)}) async-start(bf16[16,272,128]{2,1,0:T(8,128)(2,1)} %add_convert_fusion.1), calls=%async_computation.5 | async-start | bytes 2228224 | tf_op jit(solution)/shard_map/all_to_all | solution.py:691
  163.5 2.5 add_convert_fusion
  166.1 16.7 %all-to-all-done.5.refs_0_ = bf16[16,272,128]{2,1,0:T(8,128)(2,1)S(1)} async-done(((bf16[16,272,128]{2,1,0:T(8,128)(2,1)}), bf16[16,272,128]{2,1,0:T(8,128)(2,1)S(1)}, u32[]{:S(2)}, u32[]{:S(2)}) %all-to-all-start.5) | async-done | bytes 1114144 | tf_op jit(solution)/shard_map/all_to_all | solution.py:691
  182.8 3.7 %all-to-all-start.6 = ((bf16[16,272,128]{2,1,0:T(8,128)(2,1)}), bf16[16,272,128]{2,1,0:T(8,128)(2,1)S(1)}, u32[]{:S(2)}, u32[]{:S(2)}) async-start(bf16[16,272,128]{2,1,0:T(8,128)(2,1)} %add_convert_fusion), calls=%async_computation.6 | async-start | bytes 2228224 | tf_op jit(solution)/shard_map/all_to_all | solution.py:691
  186.5 2.5 shard_map.117.refs_0_
  189.1 14.1 %all-to-all-done.6.refs_1_ = bf16[16,272,128]{2,1,0:T(8,128)(2,1)S(1)} async-done(((bf16[16,272,128]{2,1,0:T(8,128)(2,1)}), bf16[16,272,128]{2,1,0:T(8,128)(2,1)S(1)}, u32[]{:S(2)}, u32[]{:S(2)}) %all-to-all-start.6) | async-done | bytes 1114144 | tf_op jit(solution)/shard_map/all_to_all | solution.py:691
  203.2 2.5 shard_map.123
  214.5 3.9 %collective-permute-start.7 = (f32[2,272,128]{2,1,0:T(8,128)S(1)}, f32[2,272,128]{2,1,0:T(8,128)S(1)}, u32[]{:S(2)}, u32[]{:S(2)}) collective-permute-start(f32[2,272,128]{2,1,0:T(8,128)S(1)} %add_add_fusion.both_ref), channel_id=1, source_target_pairs={{0,1},{1,0},{2,3},{3,2},{4,5},{5,4},{6,7},{7,6},{8,9},{9,8},{10,11... | collective-permute-start | bytes 835592 | tf_op jit(solution)/shard_map/ppermute | solution.py:696
  220.6 6.5 %shard_map.124 = (bf16[16,144,256]{2,1,0:T(8,128)(2,1)}, bf16[256,1536]{1,0:T(8,128)(2,1)}, f32[1,4]{1,0:T(1,128)}) custom-call(s32[3]{0:T(128)S(1)} %pad_add_fusion.at_ref, f32[2,272,128]{2,1,0:T(8,128)S(1)} %add_add_fusion.both_ref, f32[2,272,128]{2,1,0:T(8,128)S(1)} %collective-permute-done.7.other_ref, bf16[16,256]{1,0:T(8,128)(2,1)S(1)} %copy-done.10, ...), custom_call_target="tpu_custom_call" | custom-call | tf_op jit(solution)/shard_map/pallas_call | solution.py:37
  227.2 4.5 %all-to-all-start.7 = ((bf16[16,144,256]{2,1,0:T(8,128)(2,1)}), bf16[16,144,256]{2,1,0:T(8,128)(2,1)S(1)}, u32[]{:S(2)}, u32[]{:S(2)}) async-start(bf16[16,144,256]{2,1,0:T(8,128)(2,1)} %get-tuple-element.53), calls=%async_computation.7 | async-start | bytes 2359296 | tf_op jit(solution)/shard_map/all_to_all | solution.py:691
  234.4 2.1 shard_map.125
  236.5 13.2 %all-to-all-done.7.got_hbm = bf16[16,144,256]{2,1,0:T(8,128)(2,1)S(1)} async-done(((bf16[16,144,256]{2,1,0:T(8,128)(2,1)}), bf16[16,144,256]{2,1,0:T(8,128)(2,1)S(1)}, u32[]{:S(2)}, u32[]{:S(2)}) %all-to-all-start.7) | async-done | bytes 1179680 | tf_op jit(solution)/shard_map/all_to_all | solution.py:691
  249.7 2.6 shard_map.126
  252.3 5.8 %all-to-all-start.8 = ((bf16[8,128,256]{2,1,0:T(8,128)(2,1)}), bf16[8,128,256]{2,1,0:T(8,128)(2,1)S(1)}, u32[]{:S(2)}, u32[]{:S(2)}) async-start(bf16[8,128,256]{2,1,0:T(8,128)(2,1)} %shard_map.126), calls=%async_computation.8 | async-start | bytes 1048576 | tf_op jit(solution)/shard_map/all_to_all | solution.py:691
  258.0 9.3 %shard_map.128 = f32[256,1024]{1,0:T(8,128)} custom-call(bf16[16,1024,256]{2,1,0:T(8,128)(2,1)} %get-tuple-element.36.expo_hbm, bf16[16,1024,256]{2,1,0:T(8,128)(2,1)} %get-tuple-element.59.raised_hbm, f32[1024,128]{1,0:T(8,128)} %get-tuple-element.60.scale_hbm, bf16[16,144,256]{2,1,0:T(8,128)(2,1)S(1)} %all-to-all-done.7.got_hbm, ...), custom_call_target="tpu_custom_call" | custom-call | tf_op jit(solution)/shard_map/pallas_call | solution.py:37
  (54 shorter events, 23.1 us)
Async XLA Ops:
  7.2 9.9 %copy-start.5 = (bf16[1024,256]{1,0:T(8,128)(2,1)S(1)}, bf16[1024,256]{1,0:T(8,128)(2,1)}, u32[]{:S(2)}) copy-start(bf16[1024,256]{1,0:T(8,128)(2,1)} %feats_ref.1) | copy-start | bytes 1572868
  7.2 71.3 %all-gather.3.cloned.1.call-start = ((), (), s32[]{:S(2)}) async-start(), calls=%async_computation.9 | async-start | bytes 4456448 | tf_op jit(solution)/shard_map/all_gather | solution.py:765
  17.0 133.0 %all-gather.5.cloned.1.call-start = ((), (), s32[]{:S(2)}) async-start(), calls=%async_computation.10 | async-start | bytes 2228224 | tf_op jit(solution)/shard_map/all_gather | solution.py:826
  17.0 0.7 copy-start.11
  20.1 31.5 %copy-start.1 = (bf16[256,1024]{1,0:T(8,128)(2,1)S(1)}, bf16[256,1024]{1,0:T(8,128)(2,1)}, u32[]{:S(2)}) copy-start(bf16[256,1024]{1,0:T(8,128)(2,1)} %proto_hbm.1) | copy-start | bytes 1572868
  20.1 31.5 %copy-start.6 = (bf16[256,1024]{1,0:T(8,128)(2,1)S(1)}, bf16[256,1024]{1,0:T(8,128)(2,1)}, u32[]{:S(2)}) copy-start(bf16[256,1024]{1,0:T(8,128)(2,1)} %teacher_ref.1) | copy-start | bytes 1572868
  49.3 7.6 %collective-permute-start = (bf16[16,144,256]{2,1,0:T(8,128)(2,1)S(1)}, bf16[16,144,256]{2,1,0:T(8,128)(2,1)S(1)}, u32[]{:S(2)}, u32[]{:S(2)}) collective-permute-start(bf16[16,144,256]{2,1,0:T(8,128)(2,1)S(1)} %all_to_all.45.own_hbm), channel_id=1, source_target_pairs={{0,1},{1,0},{2,3},{3,2},{4,5},{5,4},{6,7},{7,6},{8,9},{9,8},{10,11... | collective-permute-start | bytes 3538952 | tf_op jit(solution)/shard_map/ppermute | solution.py:696
  84.8 2.1 collective-permute-start.2
  108.8 25.5 %copy-start.2 = (bf16[256,1024]{1,0:T(8,128)(2,1)S(1)}, bf16[256,1024]{1,0:T(8,128)(2,1)}, u32[]{:S(2)}) copy-start(bf16[256,1024]{1,0:T(8,128)(2,1)} %get-tuple-element.39.cols_ref) | copy-start | bytes 1572868
  142.9 4.5 %collective-permute-start.1 = (bf16[16,272,128]{2,1,0:T(8,128)(2,1)}, bf16[16,272,128]{2,1,0:T(8,128)(2,1)S(1)}, u32[]{:S(2)}, u32[]{:S(2)}) collective-permute-start(bf16[16,272,128]{2,1,0:T(8,128)(2,1)} %get-tuple-element.41), channel_id=1, source_target_pairs={{0,1},{1,0},{2,3},{3,2},{4,5},{5,4},{6,7},{7,6},{8,9},{9,8},{10,11... | collective-permute-start | bytes 3342344 | tf_op jit(solution)/shard_map/ppermute | solution.py:696
  147.4 2.6 copy-start.7
  159.2 4.4 %copy-start.12 = (bf16[16,272,128]{2,1,0:T(8,128)(2,1)S(1)}, bf16[16,272,128]{2,1,0:T(8,128)(2,1)}, u32[]{:S(2)}) copy-start(bf16[16,272,128]{2,1,0:T(8,128)(2,1)} %get-tuple-element.47) | copy-start | bytes 3342340
  159.2 4.3 %collective-permute-start.3 = (bf16[16,272,128]{2,1,0:T(8,128)(2,1)}, bf16[16,272,128]{2,1,0:T(8,128)(2,1)}, u32[]{:S(2)}, u32[]{:S(2)}) collective-permute-start(bf16[16,272,128]{2,1,0:T(8,128)(2,1)} %get-tuple-element.48), channel_id=1, source_target_pairs={{0,1},{1,0},{2,3},{3,2},{4,5},{5,4},{6,7},{7,6},{8,9},{9,8},{10,11... | collective-permute-start | bytes 3342344 | tf_op jit(solution)/shard_map/ppermute | solution.py:696
  159.8 23.0 %all-to-all-start.5 = ((bf16[16,272,128]{2,1,0:T(8,128)(2,1)}), bf16[16,272,128]{2,1,0:T(8,128)(2,1)S(1)}, u32[]{:S(2)}, u32[]{:S(2)}) async-start(bf16[16,272,128]{2,1,0:T(8,128)(2,1)} %add_convert_fusion.1), calls=%async_computation.5 | async-start | bytes 2228224 | tf_op jit(solution)/shard_map/all_to_all | solution.py:691
  182.8 20.4 %all-to-all-start.6 = ((bf16[16,272,128]{2,1,0:T(8,128)(2,1)}), bf16[16,272,128]{2,1,0:T(8,128)(2,1)S(1)}, u32[]{:S(2)}, u32[]{:S(2)}) async-start(bf16[16,272,128]{2,1,0:T(8,128)(2,1)} %add_convert_fusion), calls=%async_computation.6 | async-start | bytes 2228224 | tf_op jit(solution)/shard_map/all_to_all | solution.py:691
  189.1 30.5 %copy-start = (bf16[256,1536]{1,0:T(8,128)(2,1)S(1)}, bf16[256,1536]{1,0:T(8,128)(2,1)}, u32[]{:S(2)}) copy-start(bf16[256,1536]{1,0:T(8,128)(2,1)} %shard_map.118.rows_hbm.rows_ref) | copy-start | bytes 2359300
  189.1 30.5 %copy-start.9 = (f32[8,256]{1,0:T(8,128)S(1)}, f32[8,256]{1,0:T(8,128)}, u32[]{:S(2)}) copy-start(f32[8,256]{1,0:T(8,128)} %get-tuple-element.50.member_ref) | copy-start | bytes 24580
  189.1 30.5 %copy-start.10 = (bf16[16,256]{1,0:T(8,128)(2,1)S(1)}, bf16[16,256]{1,0:T(8,128)(2,1)}, u32[]{:S(2)}) copy-start(bf16[16,256]{1,0:T(8,128)(2,1)} %get-tuple-element.49.mine_ref) | copy-start | bytes 24580
  203.2 16.4 %copy-start.3 = (f32[256,1024]{1,0:T(8,128)S(1)}, f32[256,1024]{1,0:T(8,128)}, u32[]{:S(2)}) copy-start(f32[256,1024]{1,0:T(8,128)} %get-tuple-element.52.slope_ref) | copy-start | bytes 3145732
  205.7 5.4 %collective-permute-start.6 = (bf16[2,272,128]{2,1,0:T(8,128)(2,1)}, bf16[2,272,128]{2,1,0:T(8,128)(2,1)S(1)}, u32[]{:S(2)}, u32[]{:S(2)}) collective-permute-start(bf16[2,272,128]{2,1,0:T(8,128)(2,1)} %shard_map.123), channel_id=1, source_target_pairs={{0,6},{1,7},{2,4},{3,5},{4,2},{5,3},{6,0},{7,1},{8,14},{9,15},{10,... | collective-permute-start | bytes 417800 | tf_op jit(solution)/shard_map/ppermute | solution.py:707
  207.5 5.6 %collective-permute-start.5 = (bf16[2,272,128]{2,1,0:T(8,128)(2,1)}, bf16[2,272,128]{2,1,0:T(8,128)(2,1)S(1)}, u32[]{:S(2)}, u32[]{:S(2)}) collective-permute-start(bf16[2,272,128]{2,1,0:T(8,128)(2,1)} %shard_map.123), channel_id=1, source_target_pairs={{0,4},{1,5},{2,6},{3,7},{4,0},{5,1},{6,2},{7,3},{8,12},{9,13},{10,... | collective-permute-start | bytes 417800 | tf_op jit(solution)/shard_map/ppermute | solution.py:707
  208.1 5.4 %collective-permute-start.4 = (bf16[2,272,128]{2,1,0:T(8,128)(2,1)}, bf16[2,272,128]{2,1,0:T(8,128)(2,1)S(1)}, u32[]{:S(2)}, u32[]{:S(2)}) collective-permute-start(bf16[2,272,128]{2,1,0:T(8,128)(2,1)} %shard_map.123), channel_id=1, source_target_pairs={{0,2},{1,3},{2,0},{3,1},{4,6},{5,7},{6,4},{7,5},{8,10},{9,11},{10,... | collective-permute-start | bytes 417800 | tf_op jit(solution)/shard_map/ppermute | solution.py:707
  214.5 5.1 %collective-permute-start.7 = (f32[2,272,128]{2,1,0:T(8,128)S(1)}, f32[2,272,128]{2,1,0:T(8,128)S(1)}, u32[]{:S(2)}, u32[]{:S(2)}) collective-permute-start(f32[2,272,128]{2,1,0:T(8,128)S(1)} %add_add_fusion.both_ref), channel_id=1, source_target_pairs={{0,1},{1,0},{2,3},{3,2},{4,5},{5,4},{6,7},{7,6},{8,9},{9,8},{10,11... | collective-permute-start | bytes 835592 | tf_op jit(solution)/shard_map/ppermute | solution.py:696
  219.6 1.0 copy-start.8
  227.2 4.5 %copy-start.4 = (bf16[256,1536]{1,0:T(8,128)(2,1)S(1)}, bf16[256,1536]{1,0:T(8,128)(2,1)}, u32[]{:S(2)}) copy-start(bf16[256,1536]{1,0:T(8,128)(2,1)} %get-tuple-element.54.rows_ref) | copy-start | bytes 2359300
  227.2 22.5 %all-to-all-start.7 = ((bf16[16,144,256]{2,1,0:T(8,128)(2,1)}), bf16[16,144,256]{2,1,0:T(8,128)(2,1)S(1)}, u32[]{:S(2)}, u32[]{:S(2)}) async-start(bf16[16,144,256]{2,1,0:T(8,128)(2,1)} %get-tuple-element.53), calls=%async_computation.7 | async-start | bytes 2359296 | tf_op jit(solution)/shard_map/all_to_all | solution.py:691
  231.7 2.6 collective-permute-start.8
  252.3 15.2 %all-to-all-start.8 = ((bf16[8,128,256]{2,1,0:T(8,128)(2,1)}), bf16[8,128,256]{2,1,0:T(8,128)(2,1)S(1)}, u32[]{:S(2)}, u32[]{:S(2)}) async-start(bf16[8,128,256]{2,1,0:T(8,128)(2,1)} %shard_map.126), calls=%async_computation.8 | async-start | bytes 1048576 | tf_op jit(solution)/shard_map/all_to_all | solution.py:691
Sparse Core Ops, SparseCore 0:
  17.1 61.2 all-gather.2
  87.8 42.8 all-gather.4

commit v2 on v1

--- a/solution.py
+++ b/solution.py
@@ -156,21 +156,17 @@
         store.wait()
 
 
-def weights_body(at_ref, w_in_hbm, w_out_hbm, pack_hbm, sems):
-    rows, hid = w_in_hbm.shape
+def weights_body(at_ref, w_in_ref, w_out_ref, pack_hbm, pack_ref, sems):
+    rows, hid = w_in_ref.shape
     half = hid // 2
-    bot = w_out_hbm.shape[1]
-    lines = w_out_hbm.shape[0] * bot // half
-    column = pl.multiple_of(at_ref[0] * half, half)
-    pairs = [(w_in_hbm.at[:, pl.ds(column, half)], pack_hbm.at[0:rows, :])]
+    bot = w_out_ref.shape[1]
+    lines = w_out_ref.shape[0] * bot // half
+    pack_ref[0:rows, :] = w_in_ref[:, pl.ds(pl.multiple_of(at_ref[0] * half, half), half)]
     for q in range(half // bot):
-        source = w_out_hbm.at[q * lines : (q + 1) * lines, :]
-        pairs.append((source, pack_hbm.at[rows : rows + lines, q * bot : (q + 1) * bot]))
-    moves = copies(pairs, sems)
-    for move in moves:
-        move.start()
-    for move in moves:
-        move.wait()
+        pack_ref[rows : rows + lines, q * bot : (q + 1) * bot] = w_out_ref[q * lines : (q + 1) * lines, :]
+    store = pltpu.make_async_copy(pack_ref, pack_hbm, sems.at[0])
+    store.start()
+    store.wait()
 
 
 def weight_loads(at_ref, w_hbm, w_in_ref, w_out_ref, sems):
@@ -199,7 +195,7 @@
 
 
 def forward_body(
-    at_ref, rows_hbm, w_hbm, hidden_hbm, slope_hbm, feats_ref,
+    at_ref, rows_hbm, w_hbm, hidden_hbm, slope_hbm, feats_ref, w_in_hbm, w_out_hbm,
     rows_ref, hidden_ref, slope_ref, w_in_ref, w_out_ref, sems, own_sems,
 ):
     first = pltpu.make_async_copy(rows_hbm, rows_ref, own_sems.at[0])
@@ -210,6 +206,9 @@
     first.wait()
     for load in loads:
         load.wait()
+    keeps = copies([(w_in_ref, w_in_hbm), (w_out_ref, w_out_hbm)], sems)
+    for keep in keeps:
+        keep.start()
     rows = rows_ref[...]
     feats = jnp.zeros(feats_ref.shape, f32)
     for part in chunks_of(hidden_ref.shape[1]):
@@ -223,7 +222,7 @@
     stores = copies([(hidden_ref, hidden_hbm), (slope_ref, slope_hbm)], own_sems)
     for store in stores:
         store.start()
-    for store in stores:
+    for store in keeps + stores:
         store.wait()
 
 
@@ -489,11 +488,12 @@
 
 
 def backward_body(
-    at_ref, both_ref, other_ref, mine_ref, member_ref, feats_ref, feats_other_ref, rows_ref, hidden_ref, slope_ref, w_hbm,
-    send_hbm, grad_rows_hbm, loss_ref, w_in_ref, w_out_ref, send_ref, pre_ref, out_ref, grad_rows_ref, sems, send_sems, rows_sem,
+    at_ref, both_ref, other_ref, mine_ref, member_ref, feats_ref, feats_other_ref, rows_hbm, slope_hbm, hidden_hbm, w_in_hbm, w_out_hbm,
+    send_hbm, grad_rows_hbm, loss_ref, w_out_ref, slope_ref, w_in_ref, hidden_ref, rows_ref, send_ref, pre_ref, out_ref, grad_rows_ref, send_sems, rows_sem, load_sems,
 ):
-    peers = w_hbm.shape[0]
-    loads = weight_loads(at_ref, w_hbm, w_in_ref, w_out_ref, sems)
+    peers = send_ref.shape[0]
+    sources = (w_out_hbm, slope_hbm, w_in_hbm, hidden_hbm, rows_hbm)
+    loads = copies(list(zip(sources, (w_out_ref, slope_ref, w_in_ref, hidden_ref, rows_ref))), load_sems)
     for load in loads:
         load.start()
     tail = mine_ref[...].astype(f32)
@@ -567,12 +567,13 @@
 def gather_grads_body(got_hbm, send_hbm, got_ref, sum_ref, load_sems, sems):
     peers = got_hbm.shape[0]
     lines = sum_ref.shape[0]
-    load = lambda g: pltpu.make_async_copy(got_hbm.at[g, 0:lines, :], got_ref.at[g], load_sems.at[g])
-    start_all(peers, load)
-    load(0).wait()
-    acc = got_ref[0].astype(f32)
-    for g in range(1, peers):
-        load(g).wait()
+    source = lambda q: got_hbm.at[pl.ds(q * GROUP, GROUP), 0:lines, :]
+    load = lambda q: pltpu.make_async_copy(source(q), group(got_ref, q), load_sems.at[q])
+    start_all(peers // GROUP, load)
+    acc = jnp.zeros(got_ref.shape[1:], f32)
+    for g in range(peers):
+        if g % GROUP == 0:
+            load(g // GROUP).wait()
         acc = acc + got_ref[g].astype(f32)
     sum_ref[...] = acc.astype(bf16)
     store = lambda t: pltpu.make_async_copy(sum_ref, send_hbm.at[t], sems.at[t])
@@ -636,7 +637,7 @@
         [(halves, bf16), (halves, bf16), ((width, 128), f32)],
         (at, expo, got, live, cols),
         in_specs=[SMEM, HBM, VMEM, VMEM, VMEM],
-        out_specs=[HBM, HBM, HBM],
+        out_specs=[ANY, ANY, HBM],
         scratch=[
             pltpu.VMEM(expo.shape, bf16),
             pltpu.VMEM((width, 128), f32),
@@ -655,7 +656,7 @@
         [(big, bf16), (halves, bf16), (halves, bf16)],
         (at, cols_t, cols, rows),
         in_specs=[SMEM, VMEM, VMEM, HBM],
-        out_specs=[HBM, HBM, HBM],
+        out_specs=[HBM, ANY, ANY],
         scratch=[
             pltpu.VMEM(rows.shape, bf16),
             pltpu.VMEM(big, bf16),
@@ -717,12 +718,12 @@
     for move in moves:
         move.start()
     peers = parts_hbm.shape[0]
-    load = lambda g: pltpu.make_async_copy(parts_hbm.at[g], parts_ref.at[g], sems.at[g])
-    start_all(peers, load)
-    load(0).wait()
-    acc = parts_ref[0].astype(f32)
-    for g in range(1, peers):
-        load(g).wait()
+    load = lambda q: pltpu.make_async_copy(group(parts_hbm, q), group(parts_ref, q), sems.at[q])
+    start_all(peers // GROUP, load)
+    acc = jnp.zeros(parts_ref.shape[1:], f32)
+    for g in range(peers):
+        if g % GROUP == 0:
+            load(g // GROUP).wait()
         acc = acc + parts_ref[g].astype(f32)
     out_ref[len(earlier)] = acc.astype(bf16)
     for move in moves:
@@ -740,7 +741,7 @@
         (*earlier, parts),
         in_specs=[HBM] * len(earlier) + [ANY],
         out_specs=[HBM],
-        scratch=[pltpu.VMEM(parts.shape, bf16), pltpu.VMEM(out, bf16), sem(parts.shape[0]), sem(1)],
+        scratch=[pltpu.VMEM(parts.shape, bf16), pltpu.VMEM(out, bf16), sem(parts.shape[0] // GROUP), sem(1)],
     )[0]
 
 
@@ -761,7 +762,7 @@
     at = jnp.stack([t % 2, t // 2, g // (dp // 2)])
 
     lines = per + w_out.shape[0] * bot // half
-    (w_pack,) = call(weights_body, [((lines, half), bf16)], (at, w_in, w_out), in_specs=[SMEM, HBM, HBM], out_specs=[HBM], scratch=[sem(1 + half // bot)])
+    (w_pack,) = call(weights_body, [((lines, half), bf16)], (at, w_in, w_out), in_specs=[SMEM, VMEM, VMEM], out_specs=[HBM], scratch=[pltpu.VMEM((lines, half), bf16), sem(1)])
     w_all = lax.all_gather(w_pack, "dp", axis=0, tiled=True).reshape(dp, lines, half)
     dma = pltpu.SemaphoreType.DMA
     sems = dma((dp,))
@@ -806,12 +807,12 @@
         out_specs=[HBM],
         scratch=[pltpu.VMEM(tokens.shape, bf16), pltpu.VMEM((CAP, dim), bf16), sem(2)],
     )
-    hidden, slope, feats = call(
+    hidden, slope, feats, w_in_half, w_out_half = call(
         forward_body,
-        [((CAP, half), bf16), ((CAP, half), f32), ((CAP, bot), f32)],
+        [((CAP, half), bf16), ((CAP, half), f32), ((CAP, bot), f32), ((dim, half), bf16), ((half, bot), bf16)],
         (at, rows, after(w_all, part)),
         in_specs=[SMEM, HBM, HBM],
-        out_specs=[HBM, HBM, VMEM],
+        out_specs=[HBM, HBM, VMEM, HBM, HBM],
         scratch=[
             pltpu.VMEM((CAP, dim), bf16),
             pltpu.VMEM((CAP, half), bf16),
@@ -841,18 +842,22 @@
     send, grad_rows, loss = call(
         backward_body,
         [((dp, back_lines, bot), bf16), ((CAP, dim), bf16), ((1, masks.shape[0]), f32)],
-        (at, both, sibling(both), mine, member, feats, feats_other, rows, hidden, slope, w_all),
-        in_specs=[SMEM] + [VMEM] * 9 + [HBM],
+        (at, both, sibling(both), mine, member, feats, feats_other, rows, slope, hidden, w_in_half, w_out_half),
+        in_specs=[SMEM] + [VMEM] * 6 + [HBM] * 5,
         out_specs=[HBM, HBM, VMEM],
         scratch=[
-            *w_held,
+            pltpu.VMEM((half, bot), bf16),
+            pltpu.VMEM((CAP, half), f32),
+            pltpu.VMEM((dim, half), bf16),
+            pltpu.VMEM((CAP, half), bf16),
+            pltpu.VMEM((CAP, dim), bf16),
             pltpu.VMEM((dp, back_lines, bot), bf16),
             pltpu.VMEM((CAP, half), bf16),
             pltpu.VMEM((half, bot), bf16),
             pltpu.VMEM((CAP, dim), bf16),
-            loads,
             sems,
             sem(1),
+            sem(5),
         ],
     )
     got = exchange(send, "dp")

time: 277 us -> 266 us (0.960)
  Pallas kernels: 83.2 us -> 71.9 us
    pallas_call x19, Pallas kernels: 83.2 us -> 71.9 us  [call(): pl.pallas_call(body, out_shape=outs, in_specs=in_specs, out_specs=tuple(s...]
  transfers between devices with their start and end apart: 15 -> 15, of which waited for: 11 -> 11; matrix products, arithmetic and copies ran while one was open for 2% -> 1% of each run, Pallas kernels for 16% -> 16%
where the time goes in v2:
time: 266 us; the launch traced here: 265 us
  Pallas kernels  71.9 us (27%)
  waiting for transfers between devices  70.1 us (26%)
  blocking collectives  69.7 us (26%)
  starting transfers between devices  31.4 us (12%)
  between operations  14.3 us (5%)
  other arithmetic  5 us (2%)
    pallas_call x19, Pallas kernels, call(): pl.pallas_call(body, out_shape=outs, in_specs=in_specs, out_specs=tuple(s...  71.9 us
    all_to_all x5, blocking collectives, exchange(): return lax.all_to_all(x, axis, split_axis=0, concat_axis=0, tiled=True)  69.7 us
    all_to_all x4, waiting for transfers between devices, exchange(): return lax.all_to_all(x, axis, split_axis=0, concat_axis=0, tiled=True)  45.5 us
    all_to_all x4, starting transfers between devices, exchange(): return lax.all_to_all(x, axis, split_axis=0, concat_axis=0, tiled=True)  17.7 us
    all_gather x1, waiting for transfers between devices, parts_of(): lax.all_gather(w_pack, 'dp', axis=0, tiled=True).reshape(dp, lines, half)  13.4 us
    ppermute x6, starting transfers between devices, sibling(): return lax.ppermute(x, 'tensor', [(i, i ^ 1) for i in range(peers)])  10.3 us
    ppermute x6, waiting for transfers between devices, sibling(): return lax.ppermute(x, 'tensor', [(i, i ^ 1) for i in range(peers)])  6.65 us
  transfers between devices with their start and end apart: 15, of which 11 were waited for; matrix products, arithmetic and copies ran while one was open for 1% of the time, Pallas kernels for 16%

profile of v2, /device:TPU:1, one launch (start us, length us, event | category | flops | bytes accessed | tf_op | source)
XLA Modules:
  0.0 265.0 jit_solution(11110808443370565132)
XLA Ops:
  11.2 2.4 shard_map.111
  13.6 29.2 %all_to_all.45.own_hbm = bf16[16,144,256]{2,1,0:T(8,128)(2,1)S(1)} all-to-all(bf16[16,144,256]{2,1,0:T(8,128)(2,1)} %get-tuple-element.37), channel_id=1, replica_groups=mesh['dp'=16,'tensor'=8] {'dp'}, dimensions={0} | all-to-all | bytes 2359296 | tf_op jit(solution)/shard_map/all_to_all | solution.py:692
  42.8 2.2 collective-permute-start
  46.6 3.8 %shard_map.118.rows_hbm = bf16[256,1536]{1,0:T(8,128)(2,1)} custom-call(bf16[256,1024]{1,0:T(8,128)(2,1)S(1)} %get-tuple-element.45.sel_ref, bf16[1024,1536]{1,0:T(8,128)(2,1)} %tokens_hbm.1), custom_call_target="tpu_custom_call" | custom-call | tf_op jit(solution)/shard_map/pallas_call | solution.py:37
  50.4 8.1 %shard_map.112 = (bf16[16,1024,256]{2,1,0:T(8,128)(2,1)}, bf16[8,16,256]{2,1,0:T(8,128)(2,1)S(1)}, f32[16,256]{1,0:T(8,128)S(1)}) custom-call(s32[3]{0:T(128)S(1)} %pad_add_fusion.at_ref, bf16[1024,256]{1,0:T(8,128)(2,1)} %get-tuple-element.36.cols_hbm, bf16[16,144,256]{2,1,0:T(8,128)(2,1)S(1)} %all_to_all.45.own_hbm, ...), custom_call_target="tpu_custom_call" | custom-call | tf_op jit(solution)/shard_map/pallas_call | solution.py:37
  58.5 13.4 %all-gather.3.cloned.1.call-done = bf16[2048,1024]{1,0:T(8,128)(2,1)} async-done(((bf16[128,1024]{1,0:T(8,128)(2,1)}), bf16[2048,1024]{1,0:T(8,128)(2,1)}) %all-gather.3.cloned.1.call-update) | async-done | bytes 4194320 | tf_op jit(solution)/shard_map/all_gather | solution.py:766
  71.9 6.4 %shard_map.120 = (bf16[256,1024]{1,0:T(8,128)(2,1)}, f32[256,1024]{1,0:T(8,128)}, f32[256,256]{1,0:T(8,128)S(1)}, bf16[1536,1024]{1,0:T(8,128)(2,1)}, bf16[1024,256]{1,0:T(8,128)(2,1)}) custom-call(s32[3]{0:T(128)S(1)} %pad_add_fusion.at_ref, bf16[256,1536]{1,0:T(8,128)(2,1)} %shard_map.118.rows_hbm, bf16[16,128,1024]{2,1,0:T(8,128)(2,1)} %bitcast.9), custom_call_target="tpu_custom_call" | custom-call | tf_op jit(solution)/shard_map/pallas_call | solution.py:37
  81.2 9.4 %all_to_all.46.parts_ref = bf16[8,16,256]{2,1,0:T(8,128)(2,1)S(1)} all-to-all(bf16[8,16,256]{2,1,0:T(8,128)(2,1)S(1)} %get-tuple-element.39), channel_id=1, replica_groups=mesh['dp'=16,'tensor'=8] {'tensor'}, dimensions={0} | all-to-all | bytes 131072 | tf_op jit(solution)/shard_map/all_to_all | solution.py:692
  90.6 11.7 %all_to_all.47.parts_ref = bf16[16,16,256]{2,1,0:T(8,128)(2,1)S(1)} all-to-all(bf16[16,16,256]{2,1,0:T(8,128)(2,1)S(1)} %shard_map.113), channel_id=1, replica_groups=mesh['dp'=16,'tensor'=8] {'dp'}, dimensions={0} | all-to-all | bytes 262144 | tf_op jit(solution)/shard_map/all_to_all | solution.py:692
  102.3 6.2 %shard_map.114 = bf16[8,16,256]{2,1,0:T(8,128)(2,1)S(1)} custom-call(bf16[16,1024,256]{2,1,0:T(8,128)(2,1)} %get-tuple-element.38.expo_hbm, bf16[16,16,256]{2,1,0:T(8,128)(2,1)S(1)} %all_to_all.47.parts_ref, f32[16,256]{1,0:T(8,128)S(1)} %get-tuple-element.40.live_ref), custom_call_target="tpu_custom_call" | custom-call | tf_op jit(solution)/shard_map/pallas_call | solution.py:37
  108.5 9.4 %all_to_all.48.parts_ref = bf16[8,16,256]{2,1,0:T(8,128)(2,1)S(1)} all-to-all(bf16[8,16,256]{2,1,0:T(8,128)(2,1)S(1)} %shard_map.114), channel_id=1, replica_groups=mesh['dp'=16,'tensor'=8] {'tensor'}, dimensions={0} | all-to-all | bytes 131072 | tf_op jit(solution)/shard_map/all_to_all | solution.py:692
  117.9 10.0 %all_to_all.49.parts_ref = bf16[16,16,256]{2,1,0:T(8,128)(2,1)S(1)} all-to-all(bf16[16,16,256]{2,1,0:T(8,128)(2,1)S(1)} %shard_map.115), channel_id=1, replica_groups=mesh['dp'=16,'tensor'=8] {'dp'}, dimensions={0} | all-to-all | bytes 262144 | tf_op jit(solution)/shard_map/all_to_all | solution.py:692
  127.9 8.3 %shard_map.116 = (bf16[16,272,128]{2,1,0:T(8,128)(2,1)S(1)}, bf16[16,272,128]{2,1,0:T(8,128)(2,1)S(1)}, f32[1024,128]{1,0:T(8,128)}) custom-call(s32[3]{0:T(128)S(1)} %pad_add_fusion.at_ref, bf16[16,1024,256]{2,1,0:T(8,128)(2,1)} %get-tuple-element.38.expo_hbm, bf16[16,16,256]{2,1,0:T(8,128)(2,1)S(1)} %all_to_all.49.parts_ref, ...), custom_call_target="tpu_custom_call" | custom-call | tf_op jit(solution)/shard_map/pallas_call | solution.py:37
  136.2 1.9 collective-permute-start.1
  138.1 2.4 collective-permute-done.1
  141.8 9.2 %shard_map.122 = (bf16[16,1024,256]{2,1,0:T(8,128)(2,1)}, bf16[16,272,128]{2,1,0:T(8,128)(2,1)S(1)}, bf16[16,272,128]{2,1,0:T(8,128)(2,1)}) custom-call(s32[3]{0:T(128)S(1)} %pad_add_fusion.at_ref, bf16[1024,256]{1,0:T(8,128)(2,1)S(1)} %copy-done.5, bf16[256,1024]{1,0:T(8,128)(2,1)S(1)} %copy-done.1, bf16[16,256,256]{2,1,0:T(8,128)(2,1)} %bitcast.7), custom_call_target="tpu_custom_call" | custom-call | tf_op jit(solution)/shard_map/pallas_call | solution.py:37
  151.7 3.7 %all-to-all-start.5 = ((bf16[16,272,128]{2,1,0:T(8,128)(2,1)}), bf16[16,272,128]{2,1,0:T(8,128)(2,1)S(1)}, u32[]{:S(2)}, u32[]{:S(2)}) async-start(bf16[16,272,128]{2,1,0:T(8,128)(2,1)} %add_convert_fusion.1), calls=%async_computation.5 | async-start | bytes 2228224 | tf_op jit(solution)/shard_map/all_to_all | solution.py:692
  155.4 2.6 add_convert_fusion
  158.0 16.7 %all-to-all-done.5.refs_0_ = bf16[16,272,128]{2,1,0:T(8,128)(2,1)S(1)} async-done(((bf16[16,272,128]{2,1,0:T(8,128)(2,1)}), bf16[16,272,128]{2,1,0:T(8,128)(2,1)S(1)}, u32[]{:S(2)}, u32[]{:S(2)}) %all-to-all-start.5) | async-done | bytes 1114144 | tf_op jit(solution)/shard_map/all_to_all | solution.py:692
  174.7 3.7 %all-to-all-start.6 = ((bf16[16,272,128]{2,1,0:T(8,128)(2,1)}), bf16[16,272,128]{2,1,0:T(8,128)(2,1)S(1)}, u32[]{:S(2)}, u32[]{:S(2)}) async-start(bf16[16,272,128]{2,1,0:T(8,128)(2,1)} %add_convert_fusion), calls=%async_computation.6 | async-start | bytes 2228224 | tf_op jit(solution)/shard_map/all_to_all | solution.py:692
  179.5 15.6 %all-to-all-done.6.refs_1_ = bf16[16,272,128]{2,1,0:T(8,128)(2,1)S(1)} async-done(((bf16[16,272,128]{2,1,0:T(8,128)(2,1)}), bf16[16,272,128]{2,1,0:T(8,128)(2,1)S(1)}, u32[]{:S(2)}, u32[]{:S(2)}) %all-to-all-start.6) | async-done | bytes 1114144 | tf_op jit(solution)/shard_map/all_to_all | solution.py:692
  196.7 1.7 collective-permute-start.6
  200.0 2.1 collective-permute-done.6
  202.1 2.0 collective-permute-done.5
  205.5 3.9 %collective-permute-start.7 = (f32[2,272,128]{2,1,0:T(8,128)S(1)}, f32[2,272,128]{2,1,0:T(8,128)S(1)}, u32[]{:S(2)}, u32[]{:S(2)}) collective-permute-start(f32[2,272,128]{2,1,0:T(8,128)S(1)} %add_add_fusion.both_ref), channel_id=1, source_target_pairs={{0,1},{1,0},{2,3},{3,2},{4,5},{5,4},{6,7},{7,6},{8,9},{9,8},{10,11... | collective-permute-start | bytes 835592 | tf_op jit(solution)/shard_map/ppermute | solution.py:697
  210.5 7.2 %shard_map.124 = (bf16[16,144,256]{2,1,0:T(8,128)(2,1)}, bf16[256,1536]{1,0:T(8,128)(2,1)}, f32[1,4]{1,0:T(1,128)}) custom-call(s32[3]{0:T(128)S(1)} %pad_add_fusion.at_ref, f32[2,272,128]{2,1,0:T(8,128)S(1)} %add_add_fusion.both_ref, f32[2,272,128]{2,1,0:T(8,128)S(1)} %collective-permute-done.7.other_ref, bf16[16,256]{1,0:T(8,128)(2,1)S(1)} %copy-done.9, ...), custom_call_target="tpu_custom_call" | custom-call | tf_op jit(solution)/shard_map/pallas_call | solution.py:37
  217.7 4.5 %all-to-all-start.7 = ((bf16[16,144,256]{2,1,0:T(8,128)(2,1)}), bf16[16,144,256]{2,1,0:T(8,128)(2,1)S(1)}, u32[]{:S(2)}, u32[]{:S(2)}) async-start(bf16[16,144,256]{2,1,0:T(8,128)(2,1)} %get-tuple-element.57), calls=%async_computation.7 | async-start | bytes 2359296 | tf_op jit(solution)/shard_map/all_to_all | solution.py:692
  223.0 1.9 collective-permute-done.8.other_ref
  224.9 2.1 shard_map.125
  227.0 13.2 %all-to-all-done.7.got_hbm = bf16[16,144,256]{2,1,0:T(8,128)(2,1)S(1)} async-done(((bf16[16,144,256]{2,1,0:T(8,128)(2,1)}), bf16[16,144,256]{2,1,0:T(8,128)(2,1)S(1)}, u32[]{:S(2)}, u32[]{:S(2)}) %all-to-all-start.7) | async-done | bytes 1179680 | tf_op jit(solution)/shard_map/all_to_all | solution.py:692
  241.5 5.8 %all-to-all-start.8 = ((bf16[8,128,256]{2,1,0:T(8,128)(2,1)}), bf16[8,128,256]{2,1,0:T(8,128)(2,1)S(1)}, u32[]{:S(2)}, u32[]{:S(2)}) async-start(bf16[8,128,256]{2,1,0:T(8,128)(2,1)} %shard_map.126), calls=%async_computation.8 | async-start | bytes 1048576 | tf_op jit(solution)/shard_map/all_to_all | solution.py:692
  247.2 9.3 %shard_map.128 = f32[256,1024]{1,0:T(8,128)} custom-call(bf16[16,1024,256]{2,1,0:T(8,128)(2,1)} %get-tuple-element.38.expo_hbm, bf16[16,1024,256]{2,1,0:T(8,128)(2,1)} %get-tuple-element.63.raised_hbm, f32[1024,128]{1,0:T(8,128)} %get-tuple-element.64.scale_hbm, bf16[16,144,256]{2,1,0:T(8,128)(2,1)S(1)} %all-to-all-done.7.got_hbm, ...), custom_call_target="tpu_custom_call" | custom-call | tf_op jit(solution)/shard_map/pallas_call | solution.py:37
  (50 shorter events, 20.7 us)
Async XLA Ops:
  7.2 3.3 %copy-start.3 = (bf16[1024,256]{1,0:T(8,128)(2,1)S(1)}, bf16[1024,256]{1,0:T(8,128)(2,1)}, u32[]{:S(2)}) copy-start(bf16[1024,256]{1,0:T(8,128)(2,1)} %feats_ref.1) | copy-start | bytes 1572868
  7.2 64.7 %all-gather.3.cloned.1.call-start = ((), (), s32[]{:S(2)}) async-start(), calls=%async_computation.9 | async-start | bytes 4456448 | tf_op jit(solution)/shard_map/all_gather | solution.py:766
  7.3 1.0 copy-start.6
  8.3 0.8 copy-start.7
  10.5 131.3 %all-gather.5.cloned.1.call-start = ((), (), s32[]{:S(2)}) async-start(), calls=%async_computation.10 | async-start | bytes 2228224 | tf_op jit(solution)/shard_map/all_gather | solution.py:827
  10.5 0.7 copy-start.10
  13.6 31.5 %copy-start = (bf16[256,1024]{1,0:T(8,128)(2,1)S(1)}, bf16[256,1024]{1,0:T(8,128)(2,1)}, u32[]{:S(2)}) copy-start(bf16[256,1024]{1,0:T(8,128)(2,1)} %proto_hbm.1) | copy-start | bytes 1572868
  13.6 31.5 %copy-start.4 = (bf16[256,1024]{1,0:T(8,128)(2,1)S(1)}, bf16[256,1024]{1,0:T(8,128)(2,1)}, u32[]{:S(2)}) copy-start(bf16[256,1024]{1,0:T(8,128)(2,1)} %teacher_ref.1) | copy-start | bytes 1572868
  42.8 7.6 %collective-permute-start = (bf16[16,144,256]{2,1,0:T(8,128)(2,1)S(1)}, bf16[16,144,256]{2,1,0:T(8,128)(2,1)S(1)}, u32[]{:S(2)}, u32[]{:S(2)}) collective-permute-start(bf16[16,144,256]{2,1,0:T(8,128)(2,1)S(1)} %all_to_all.45.own_hbm), channel_id=1, source_target_pairs={{0,1},{1,0},{2,3},{3,2},{4,5},{5,4},{6,7},{7,6},{8,9},{9,8},{10,11... | collective-permute-start | bytes 3538952 | tf_op jit(solution)/shard_map/ppermute | solution.py:697
  78.3 2.1 collective-permute-start.2
  102.3 25.6 %copy-start.1 = (bf16[256,1024]{1,0:T(8,128)(2,1)S(1)}, bf16[256,1024]{1,0:T(8,128)(2,1)}, u32[]{:S(2)}) copy-start(bf16[256,1024]{1,0:T(8,128)(2,1)} %get-tuple-element.41.cols_ref) | copy-start | bytes 1572868
  136.2 4.3 %collective-permute-start.1 = (bf16[16,272,128]{2,1,0:T(8,128)(2,1)S(1)}, bf16[16,272,128]{2,1,0:T(8,128)(2,1)S(1)}, u32[]{:S(2)}, u32[]{:S(2)}) collective-permute-start(bf16[16,272,128]{2,1,0:T(8,128)(2,1)S(1)} %get-tuple-element.43), channel_id=1, source_target_pairs={{0,1},{1,0},{2,3},{3,2},{4,5},{5,4},{6,7},{7,6},{8,9},{9,8},{10,11... | collective-permute-start | bytes 3342344 | tf_op jit(solution)/shard_map/ppermute | solution.py:697
  140.5 1.3 copy-start.5
  151.0 4.3 %collective-permute-start.3 = (bf16[16,272,128]{2,1,0:T(8,128)(2,1)}, bf16[16,272,128]{2,1,0:T(8,128)(2,1)}, u32[]{:S(2)}, u32[]{:S(2)}) collective-permute-start(bf16[16,272,128]{2,1,0:T(8,128)(2,1)} %get-tuple-element.50), channel_id=1, source_target_pairs={{0,1},{1,0},{2,3},{3,2},{4,5},{5,4},{6,7},{7,6},{8,9},{9,8},{10,11... | collective-permute-start | bytes 3342344 | tf_op jit(solution)/shard_map/ppermute | solution.py:697
  151.7 23.0 %all-to-all-start.5 = ((bf16[16,272,128]{2,1,0:T(8,128)(2,1)}), bf16[16,272,128]{2,1,0:T(8,128)(2,1)S(1)}, u32[]{:S(2)}, u32[]{:S(2)}) async-start(bf16[16,272,128]{2,1,0:T(8,128)(2,1)} %add_convert_fusion.1), calls=%async_computation.5 | async-start | bytes 2228224 | tf_op jit(solution)/shard_map/all_to_all | solution.py:692
  174.7 20.4 %all-to-all-start.6 = ((bf16[16,272,128]{2,1,0:T(8,128)(2,1)}), bf16[16,272,128]{2,1,0:T(8,128)(2,1)S(1)}, u32[]{:S(2)}, u32[]{:S(2)}) async-start(bf16[16,272,128]{2,1,0:T(8,128)(2,1)} %add_convert_fusion), calls=%async_computation.6 | async-start | bytes 2228224 | tf_op jit(solution)/shard_map/all_to_all | solution.py:692
  179.4 31.1 %copy-start.8 = (f32[8,256]{1,0:T(8,128)S(1)}, f32[8,256]{1,0:T(8,128)}, u32[]{:S(2)}) copy-start(f32[8,256]{1,0:T(8,128)} %get-tuple-element.52.member_ref) | copy-start | bytes 24580
  179.5 31.1 %copy-start.9 = (bf16[16,256]{1,0:T(8,128)(2,1)S(1)}, bf16[16,256]{1,0:T(8,128)(2,1)}, u32[]{:S(2)}) copy-start(bf16[16,256]{1,0:T(8,128)(2,1)} %get-tuple-element.51.mine_ref) | copy-start | bytes 24580
  196.7 5.4 %collective-permute-start.6 = (bf16[2,272,128]{2,1,0:T(8,128)(2,1)}, bf16[2,272,128]{2,1,0:T(8,128)(2,1)S(1)}, u32[]{:S(2)}, u32[]{:S(2)}) collective-permute-start(bf16[2,272,128]{2,1,0:T(8,128)(2,1)} %shard_map.123), channel_id=1, source_target_pairs={{0,6},{1,7},{2,4},{3,5},{4,2},{5,3},{6,0},{7,1},{8,14},{9,15},{10,... | collective-permute-start | bytes 417800 | tf_op jit(solution)/shard_map/ppermute | solution.py:708
  198.4 5.6 %collective-permute-start.5 = (bf16[2,272,128]{2,1,0:T(8,128)(2,1)}, bf16[2,272,128]{2,1,0:T(8,128)(2,1)S(1)}, u32[]{:S(2)}, u32[]{:S(2)}) collective-permute-start(bf16[2,272,128]{2,1,0:T(8,128)(2,1)} %shard_map.123), channel_id=1, source_target_pairs={{0,4},{1,5},{2,6},{3,7},{4,0},{5,1},{6,2},{7,3},{8,12},{9,13},{10,... | collective-permute-start | bytes 417800 | tf_op jit(solution)/shard_map/ppermute | solution.py:708
  199.0 5.5 %collective-permute-start.4 = (bf16[2,272,128]{2,1,0:T(8,128)(2,1)}, bf16[2,272,128]{2,1,0:T(8,128)(2,1)S(1)}, u32[]{:S(2)}, u32[]{:S(2)}) collective-permute-start(bf16[2,272,128]{2,1,0:T(8,128)(2,1)} %shard_map.123), channel_id=1, source_target_pairs={{0,2},{1,3},{2,0},{3,1},{4,6},{5,7},{6,4},{7,5},{8,10},{9,11},{10,... | collective-permute-start | bytes 417800 | tf_op jit(solution)/shard_map/ppermute | solution.py:708
  205.5 5.1 %collective-permute-start.7 = (f32[2,272,128]{2,1,0:T(8,128)S(1)}, f32[2,272,128]{2,1,0:T(8,128)S(1)}, u32[]{:S(2)}, u32[]{:S(2)}) collective-permute-start(f32[2,272,128]{2,1,0:T(8,128)S(1)} %add_add_fusion.both_ref), channel_id=1, source_target_pairs={{0,1},{1,0},{2,3},{3,2},{4,5},{5,4},{6,7},{7,6},{8,9},{9,8},{10,11... | collective-permute-start | bytes 835592 | tf_op jit(solution)/shard_map/ppermute | solution.py:697
  217.7 4.5 %copy-start.2 = (bf16[256,1536]{1,0:T(8,128)(2,1)S(1)}, bf16[256,1536]{1,0:T(8,128)(2,1)}, u32[]{:S(2)}) copy-start(bf16[256,1536]{1,0:T(8,128)(2,1)} %get-tuple-element.58.rows_ref) | copy-start | bytes 2359300
  217.7 22.5 %all-to-all-start.7 = ((bf16[16,144,256]{2,1,0:T(8,128)(2,1)}), bf16[16,144,256]{2,1,0:T(8,128)(2,1)S(1)}, u32[]{:S(2)}, u32[]{:S(2)}) async-start(bf16[16,144,256]{2,1,0:T(8,128)(2,1)} %get-tuple-element.57), calls=%async_computation.7 | async-start | bytes 2359296 | tf_op jit(solution)/shard_map/all_to_all | solution.py:692
  222.3 2.6 %collective-permute-start.8 = (bf16[256,1536]{1,0:T(8,128)(2,1)S(1)}, bf16[256,1536]{1,0:T(8,128)(2,1)S(1)}, u32[]{:S(2)}, u32[]{:S(2)}) collective-permute-start(bf16[256,1536]{1,0:T(8,128)(2,1)S(1)} %copy-done.2), channel_id=1, source_target_pairs={{0,1},{1,0},{2,3},{3,2},{4,5},{5,4},{6,7},{7,6},{8,9},{9,8},{10,11... | collective-permute-start | bytes 2359304 | tf_op jit(solution)/shard_map/ppermute | solution.py:697
  241.5 15.2 %all-to-all-start.8 = ((bf16[8,128,256]{2,1,0:T(8,128)(2,1)}), bf16[8,128,256]{2,1,0:T(8,128)(2,1)S(1)}, u32[]{:S(2)}, u32[]{:S(2)}) async-start(bf16[8,128,256]{2,1,0:T(8,128)(2,1)} %shard_map.126), calls=%async_computation.8 | async-start | bytes 1048576 | tf_op jit(solution)/shard_map/all_to_all | solution.py:692
Sparse Core Ops, SparseCore 0:
  10.6 61.2 all-gather.2
  81.3 42.8 all-gather.4

commit v3 on v2

--- a/solution.py
+++ b/solution.py
@@ -156,26 +156,39 @@
         store.wait()
 
 
-def weights_body(at_ref, w_in_ref, w_out_ref, pack_hbm, pack_ref, sems):
-    rows, hid = w_in_ref.shape
+def weights_body(at_ref, w_in_hbm, w_out_hbm, pack_hbm, pack_ref, sems):
+    rows, hid = w_in_hbm.shape
     half = hid // 2
-    bot = w_out_ref.shape[1]
-    lines = w_out_ref.shape[0] * bot // half
-    pack_ref[0:rows, :] = w_in_ref[:, pl.ds(pl.multiple_of(at_ref[0] * half, half), half)]
+    bot = w_out_hbm.shape[1]
+    lines = w_out_hbm.shape[0] * bot // half
+    column = pl.multiple_of(at_ref[0] * half, half)
+    pairs = [(w_in_hbm.at[:, pl.ds(column, half)], pack_ref.at[0:rows, :])]
     for q in range(half // bot):
-        pack_ref[rows : rows + lines, q * bot : (q + 1) * bot] = w_out_ref[q * lines : (q + 1) * lines, :]
+        source = w_out_hbm.at[q * lines : (q + 1) * lines, :]
+        pairs.append((source, pack_ref.at[rows : rows + lines, q * bot : (q + 1) * bot]))
+    loads = copies(pairs, sems)
+    for load in loads:
+        load.start()
+    for load in loads:
+        load.wait()
     store = pltpu.make_async_copy(pack_ref, pack_hbm, sems.at[0])
     store.start()
     store.wait()
 
 
-def weight_loads(at_ref, w_hbm, w_in_ref, w_out_ref, sems):
+def w_in_loads(w_hbm, w_in_ref, sems):
     peers = w_hbm.shape[0]
     rows = w_in_ref.shape[0] // peers
-    lines = w_hbm.shape[1] - rows
+    return copies([(w_hbm.at[g, 0:rows, :], w_in_ref.at[g * rows : (g + 1) * rows, :]) for g in range(peers)], sems)
+
+
+def w_out_loads(at_ref, w_hbm, w_out_ref, sems):
+    peers = w_hbm.shape[0]
     bot = w_out_ref.shape[1]
     quarters = w_hbm.shape[2] // bot
-    pairs = [(w_hbm.at[g, 0:rows, :], w_in_ref.at[g * rows : (g + 1) * rows, :]) for g in range(peers)]
+    lines = w_out_ref.shape[0] // (peers // 2 * quarters)
+    rows = w_hbm.shape[1] - lines
+    pairs = []
     for i in range(peers // 2):
         for q in range(quarters):
             source = w_hbm.at[at_ref[0] * (peers // 2) + i, rows : rows + lines, q * bot : (q + 1) * bot]
@@ -195,18 +208,18 @@
 
 
 def forward_body(
-    at_ref, rows_hbm, w_hbm, hidden_hbm, slope_hbm, feats_ref, w_in_hbm, w_out_hbm,
-    rows_ref, hidden_ref, slope_ref, w_in_ref, w_out_ref, sems, own_sems,
+    at_ref, rows_hbm, w_hbm, hidden_hbm, slope_hbm, feats_ref, w_out_hbm,
+    rows_ref, hidden_ref, slope_ref, w_in_ref, w_out_ref, sems, out_sems, own_sems,
 ):
     first = pltpu.make_async_copy(rows_hbm, rows_ref, own_sems.at[0])
     first.start()
-    loads = weight_loads(at_ref, w_hbm, w_in_ref, w_out_ref, sems)
+    loads = w_in_loads(w_hbm, w_in_ref, sems) + w_out_loads(at_ref, w_hbm, w_out_ref, out_sems)
     for load in loads:
         load.start()
     first.wait()
     for load in loads:
         load.wait()
-    keeps = copies([(w_in_ref, w_in_hbm), (w_out_ref, w_out_hbm)], sems)
+    keeps = copies([(w_out_ref, w_out_hbm)], sems)
     for keep in keeps:
         keep.start()
     rows = rows_ref[...]
@@ -476,8 +489,8 @@
         grad_ref[:, part] = (grad - unit * jnp.sum(unit * grad, axis=0, keepdims=True)) / norm
 
 
-def join(core, both_ref, other_ref, at):
-    own, other = (both_ref[at], other_ref[at])
+def join(core, own_ref, other_ref):
+    own, other = (own_ref[0], other_ref[0])
     low = core == 0
     return jnp.concatenate([jnp.where(low, own, other), jnp.where(low, other, own)], axis=1)
 
@@ -488,18 +501,19 @@
 
 
 def backward_body(
-    at_ref, both_ref, other_ref, mine_ref, member_ref, feats_ref, feats_other_ref, rows_hbm, slope_hbm, hidden_hbm, w_in_hbm, w_out_hbm,
-    send_hbm, grad_rows_hbm, loss_ref, w_out_ref, slope_ref, w_in_ref, hidden_ref, rows_ref, send_ref, pre_ref, out_ref, grad_rows_ref, send_sems, rows_sem, load_sems,
+    at_ref, pull_ref, pull_other_ref, push_ref, push_other_ref, mine_ref, member_ref, feats_ref, feats_other_ref,
+    rows_hbm, slope_hbm, hidden_hbm, w_out_hbm,
+    send_hbm, pre_hbm, loss_ref, w_out_ref, slope_ref, hidden_ref, rows_ref, send_ref, pre_ref, out_ref, send_sems, pre_sem, load_sems,
 ):
     peers = send_ref.shape[0]
-    sources = (w_out_hbm, slope_hbm, w_in_hbm, hidden_hbm, rows_hbm)
-    loads = copies(list(zip(sources, (w_out_ref, slope_ref, w_in_ref, hidden_ref, rows_ref))), load_sems)
+    sources = (w_out_hbm, slope_hbm, rows_hbm, hidden_hbm)
+    loads = copies(list(zip(sources, (w_out_ref, slope_ref, rows_ref, hidden_ref))), load_sems)
     for load in loads:
         load.start()
     tail = mine_ref[...].astype(f32)
     live, weight = (tail[0:1], tail[1:2] * (1.0 / STUDENT_TEMP))
-    pull = join(at_ref[0], both_ref, other_ref, 0)
-    push = join(at_ref[0], both_ref, other_ref, 1)
+    pull = join(at_ref[0], pull_ref, pull_other_ref)
+    push = join(at_ref[0], push_ref, push_other_ref)
     norm_sum = push[CAP : CAP + 1]
     push = push[0:CAP]
     scale = live / (pull[CAP : CAP + 1] + 1.0 - live)
@@ -518,18 +532,17 @@
     grad_unit = push * alpha - pull * beta
     inner = jnp.sum(unit * grad_unit, axis=0, keepdims=True)
     grad_feats = (inv * (grad_unit - unit * inner)).T.astype(bf16)
-    for load in loads:
-        load.wait()
     width = send_ref.shape[2]
-    grad_rows = jnp.zeros(grad_rows_ref.shape, f32)
+    loads[0].wait()
+    loads[1].wait()
     for part in chunks_of(hidden_ref.shape[1]):
-        grad_pre = (mm(grad_feats, w_out_ref[part, :], NT) * slope_ref[:, part]).astype(bf16)
-        pre_ref[:, part] = grad_pre
-        grad_rows = grad_rows + mm(grad_pre, w_in_ref[:, part], NT)
+        pre_ref[:, part] = (mm(grad_feats, w_out_ref[part, :], NT) * slope_ref[:, part]).astype(bf16)
+    pre_out = pltpu.make_async_copy(pre_ref, pre_hbm, pre_sem.at[0])
+    pre_out.start()
+    loads[2].wait()
+    loads[3].wait()
+    for part in chunks_of(hidden_ref.shape[1]):
         out_ref[part, :] = mm(hidden_ref[:, part], grad_feats, TN).astype(bf16)
-    grad_rows_ref[...] = grad_rows.astype(bf16)
-    rows_out = pltpu.make_async_copy(grad_rows_ref, grad_rows_hbm, rows_sem.at[0])
-    rows_out.start()
     core, level = (at_ref[0], at_ref[1])
     own = pre_ref[:, pl.ds(pl.multiple_of(level * width, width), width)]
     grad_in = mm(rows_ref[...], own, TN).astype(bf16)
@@ -549,8 +562,20 @@
         send_ref[g, per : per + share, :] = jnp.where(core == g // (peers // 2), out, jnp.zeros_like(out))
         send_ref[g, per + share : per + share + EXTRA, :] = rows
         store(g).start()
-    rows_out.wait()
+    pre_out.wait()
     wait_all(peers, store)
+
+
+def backward_rows_body(pre_ref, w_hbm, out_hbm, w_in_ref, out_ref, sems, out_sem):
+    loads = w_in_loads(w_hbm, w_in_ref, sems)
+    for load in loads:
+        load.start()
+    for load in loads:
+        load.wait()
+    out_ref[...] = mm(pre_ref[...], w_in_ref[...], NT).astype(bf16)
+    store = pltpu.make_async_copy(out_ref, out_hbm, out_sem.at[0])
+    store.start()
+    store.wait()
 
 
 def place_body(sel_ref, rows_ref, other_ref, out_hbm, out_ref, sems):
@@ -708,15 +733,17 @@
     return lax.ppermute(x, "tensor", [(i, i ^ (2 * by)) for i in range(peers)])
 
 
+def level_sums(x):
+    near, far, last = (levels(x, by) for by in (1, 2, 3))
+    wide = lambda y: y.astype(f32)
+    return (wide(x) + wide(near)) + (wide(far) + wide(last))
+
+
 def paired(keep, give):
     return (keep.astype(f32) + sibling(give).astype(f32)).astype(bf16)
 
 
-def slot_sums_body(*refs):
-    *earlier, parts_hbm, out_hbm, parts_ref, out_ref, sems, out_sem = refs
-    moves = [pltpu.make_async_copy(ref.at[0], out_ref.at[0], out_sem.at[0]) for ref in earlier]
-    for move in moves:
-        move.start()
+def slot_sums_body(parts_hbm, out_hbm, parts_ref, out_ref, sems, out_sem):
     peers = parts_hbm.shape[0]
     load = lambda q: pltpu.make_async_copy(group(parts_hbm, q), group(parts_ref, q), sems.at[q])
     start_all(peers // GROUP, load)
@@ -725,21 +752,19 @@
         if g % GROUP == 0:
             load(g // GROUP).wait()
         acc = acc + parts_ref[g].astype(f32)
-    out_ref[len(earlier)] = acc.astype(bf16)
-    for move in moves:
-        move.wait()
+    out_ref[0] = acc.astype(bf16)
     store = pltpu.make_async_copy(out_ref, out_hbm, out_sem.at[0])
     store.start()
     store.wait()
 
 
-def slot_sums(parts, *earlier):
-    out = (1 + len(earlier), *parts.shape[1:])
+def slot_sums(parts):
+    out = (1, *parts.shape[1:])
     return call(
         slot_sums_body,
         [(out, bf16)],
-        (*earlier, parts),
-        in_specs=[HBM] * len(earlier) + [ANY],
+        (parts,),
+        in_specs=[ANY],
         out_specs=[HBM],
         scratch=[pltpu.VMEM(parts.shape, bf16), pltpu.VMEM(out, bf16), sem(parts.shape[0] // GROUP), sem(1)],
     )[0]
@@ -762,7 +787,7 @@
     at = jnp.stack([t % 2, t // 2, g // (dp // 2)])
 
     lines = per + w_out.shape[0] * bot // half
-    (w_pack,) = call(weights_body, [((lines, half), bf16)], (at, w_in, w_out), in_specs=[SMEM, VMEM, VMEM], out_specs=[HBM], scratch=[pltpu.VMEM((lines, half), bf16), sem(1)])
+    (w_pack,) = call(weights_body, [((lines, half), bf16)], (at, w_in, w_out), in_specs=[SMEM, HBM, HBM], out_specs=[HBM], scratch=[pltpu.VMEM((lines, half), bf16), sem(1 + half // bot)])
     w_all = lax.all_gather(w_pack, "dp", axis=0, tiled=True).reshape(dp, lines, half)
     dma = pltpu.SemaphoreType.DMA
     sems = dma((dp,))
@@ -797,7 +822,6 @@
         ],
     )
     expo, part, live = run_expo(at, teacher_t, packs, others, tensor)
-    loads = dma((dp + 2 * dp,))
     w_held = [pltpu.VMEM((dim, half), bf16), pltpu.VMEM((half, bot), bf16)]
     (rows,) = call(
         tokens_body,
@@ -807,18 +831,19 @@
         out_specs=[HBM],
         scratch=[pltpu.VMEM(tokens.shape, bf16), pltpu.VMEM((CAP, dim), bf16), sem(2)],
     )
-    hidden, slope, feats, w_in_half, w_out_half = call(
+    hidden, slope, feats, w_out_half = call(
         forward_body,
-        [((CAP, half), bf16), ((CAP, half), f32), ((CAP, bot), f32), ((dim, half), bf16), ((half, bot), bf16)],
+        [((CAP, half), bf16), ((CAP, half), f32), ((CAP, bot), f32), ((half, bot), bf16)],
         (at, rows, after(w_all, part)),
         in_specs=[SMEM, HBM, HBM],
-        out_specs=[HBM, HBM, VMEM, HBM, HBM],
+        out_specs=[HBM, HBM, VMEM, HBM],
         scratch=[
             pltpu.VMEM((CAP, dim), bf16),
             pltpu.VMEM((CAP, half), bf16),
             pltpu.VMEM((CAP, half), f32),
             *w_held,
-            loads,
+            sems,
+            sem(2 * dp),
             sem(2),
         ],
     )
@@ -834,33 +859,39 @@
     all_rows = after(all_rows, pull)
     raised, keep, give = run_student(at, student_t, cols, all_rows)
     push_got = exchange(paired(keep, give), "dp")
-    both = slot_sums(push_got, slot_sums(pull_got))
-    near, far, last = (levels(both, by) for by in (1, 2, 3))
-    wide = lambda x: x.astype(f32)
-    both = (wide(both) + wide(near)) + (wide(far) + wide(last))
+    pull = level_sums(slot_sums(pull_got))
+    pull_other = sibling(pull)
+    push = level_sums(slot_sums(push_got))
+    push_other = sibling(push)
     back_lines = per + share + EXTRA
-    send, grad_rows, loss = call(
+    send, grad_pre, loss = call(
         backward_body,
-        [((dp, back_lines, bot), bf16), ((CAP, dim), bf16), ((1, masks.shape[0]), f32)],
-        (at, both, sibling(both), mine, member, feats, feats_other, rows, slope, hidden, w_in_half, w_out_half),
-        in_specs=[SMEM] + [VMEM] * 6 + [HBM] * 5,
+        [((dp, back_lines, bot), bf16), ((CAP, half), bf16), ((1, masks.shape[0]), f32)],
+        (at, pull, pull_other, push, push_other, mine, member, feats, feats_other, rows, slope, hidden, w_out_half),
+        in_specs=[SMEM] + [VMEM] * 8 + [HBM] * 4,
         out_specs=[HBM, HBM, VMEM],
         scratch=[
             pltpu.VMEM((half, bot), bf16),
             pltpu.VMEM((CAP, half), f32),
-            pltpu.VMEM((dim, half), bf16),
             pltpu.VMEM((CAP, half), bf16),
             pltpu.VMEM((CAP, dim), bf16),
             pltpu.VMEM((dp, back_lines, bot), bf16),
             pltpu.VMEM((CAP, half), bf16),
             pltpu.VMEM((half, bot), bf16),
-            pltpu.VMEM((CAP, dim), bf16),
             sems,
             sem(1),
-            sem(5),
+            sem(4),
         ],
     )
     got = exchange(send, "dp")
+    (grad_rows,) = call(
+        backward_rows_body,
+        [((CAP, dim), bf16)],
+        (grad_pre, w_all),
+        in_specs=[VMEM, HBM],
+        out_specs=[HBM],
+        scratch=[pltpu.VMEM((dim, half), bf16), pltpu.VMEM((CAP, dim), bf16), sems, sem(1)],
+    )
     pieces = 4
     d_shape = (pieces, tokens.shape[0] // pieces, dim)
     (d_tokens,) = call(

time: 266 us -> 261 us (0.981)
  waiting for transfers between devices: 70.1 us -> 58.6 us
  starting transfers between devices: 31.4 us -> 36.5 us
    all_to_all x4, waiting for transfers between devices: 45.5 us -> 38.3 us  [exchange(): return lax.all_to_all(x, axis, split_axis=0, concat_axis=0, tiled=True)]
    ppermute x3 -> x6, waiting for transfers between devices: 4.48 us -> 0.02 us  [levels(): return lax.ppermute(x, 'tensor', [(i, i ^ 2 * by) for i in range(peers)])]
    ppermute x3 -> x6, starting transfers between devices: 3.33 us -> 6.67 us  [levels(): return lax.ppermute(x, 'tensor', [(i, i ^ 2 * by) for i in range(peers)])]
    ppermute x6 -> x7, starting transfers between devices: 10.3 us -> 13.5 us  [sibling(): return lax.ppermute(x, 'tensor', [(i, i ^ 1) for i in range(peers)])]
    pallas_call x19 -> x20, Pallas kernels: 71.9 us -> 73.8 us  [call(): pl.pallas_call(body, out_shape=outs, in_specs=in_specs, out_specs=tuple(s...]
    ppermute x6 -> x7, waiting for transfers between devices: 6.65 us -> 6.68 us  [sibling(): return lax.ppermute(x, 'tensor', [(i, i ^ 1) for i in range(peers)])]
  transfers between devices with their start and end apart: 15 -> 19, of which waited for: 11 -> 8; matrix products, arithmetic and copies ran while one was open for 1% -> 2% of each run, Pallas kernels for 16% -> 18%
where the time goes in v3:
time: 261 us; the launch traced here: 260 us
  Pallas kernels  73.8 us (28%)
  blocking collectives  69.7 us (27%)
  waiting for transfers between devices  58.6 us (22%)
  starting transfers between devices  36.5 us (14%)
  between operations  14.4 us (6%)
  other arithmetic  4.94 us (2%)
    pallas_call x20, Pallas kernels, call(): pl.pallas_call(body, out_shape=outs, in_specs=in_specs, out_specs=tuple(s...  73.8 us
    all_to_all x5, blocking collectives, exchange(): return lax.all_to_all(x, axis, split_axis=0, concat_axis=0, tiled=True)  69.7 us
    all_to_all x4, waiting for transfers between devices, exchange(): return lax.all_to_all(x, axis, split_axis=0, concat_axis=0, tiled=True)  38.3 us
    all_to_all x4, starting transfers between devices, exchange(): return lax.all_to_all(x, axis, split_axis=0, concat_axis=0, tiled=True)  16.2 us
    ppermute x7, starting transfers between devices, sibling(): return lax.ppermute(x, 'tensor', [(i, i ^ 1) for i in range(peers)])  13.5 us
    all_gather x1, waiting for transfers between devices, parts_of(): lax.all_gather(w_pack, 'dp', axis=0, tiled=True).reshape(dp, lines, half)  13.5 us
    ppermute x7, waiting for transfers between devices, sibling(): return lax.ppermute(x, 'tensor', [(i, i ^ 1) for i in range(peers)])  6.68 us
    ppermute x6, starting transfers between devices, levels(): return lax.ppermute(x, 'tensor', [(i, i ^ 2 * by) for i in range(peers)])  6.67 us
  transfers between devices with their start and end apart: 19, of which 8 were waited for; matrix products, arithmetic and copies ran while one was open for 2% of the time, Pallas kernels for 18%

profile of v3, /device:TPU:1, one launch (start us, length us, event | category | flops | bytes accessed | tf_op | source)
XLA Modules:
  0.0 259.7 jit_solution(5732042861468491996)
XLA Ops:
  7.3 2.2 shard_map.119
  10.3 2.4 shard_map.111
  12.8 29.2 %all_to_all.45.own_hbm = bf16[16,144,256]{2,1,0:T(8,128)(2,1)S(1)} all-to-all(bf16[16,144,256]{2,1,0:T(8,128)(2,1)} %get-tuple-element.36), channel_id=1, replica_groups=mesh['dp'=16,'tensor'=8] {'dp'}, dimensions={0} | all-to-all | bytes 2359296 | tf_op jit(solution)/shard_map/all_to_all | solution.py:717
  42.0 2.2 collective-permute-start
  45.7 3.8 %shard_map.118.rows_hbm = bf16[256,1536]{1,0:T(8,128)(2,1)} custom-call(bf16[256,1024]{1,0:T(8,128)(2,1)S(1)} %get-tuple-element.44.sel_ref, bf16[1024,1536]{1,0:T(8,128)(2,1)} %tokens_hbm.1), custom_call_target="tpu_custom_call" | custom-call | tf_op jit(solution)/shard_map/pallas_call | solution.py:37
  49.6 8.1 %shard_map.112 = (bf16[16,1024,256]{2,1,0:T(8,128)(2,1)}, bf16[8,16,256]{2,1,0:T(8,128)(2,1)S(1)}, f32[16,256]{1,0:T(8,128)S(1)}) custom-call(s32[3]{0:T(128)S(1)} %pad_add_fusion.at_ref, bf16[1024,256]{1,0:T(8,128)(2,1)} %get-tuple-element.35.cols_hbm, bf16[16,144,256]{2,1,0:T(8,128)(2,1)S(1)} %all_to_all.45.own_hbm, ...), custom_call_target="tpu_custom_call" | custom-call | tf_op jit(solution)/shard_map/pallas_call | solution.py:37
  57.6 13.5 %all-gather.3.cloned.1.call-done = bf16[2048,1024]{1,0:T(8,128)(2,1)} async-done(((bf16[128,1024]{1,0:T(8,128)(2,1)}), bf16[2048,1024]{1,0:T(8,128)(2,1)}) %all-gather.3.cloned.1.call-update) | async-done | bytes 4194320 | tf_op jit(solution)/shard_map/all_gather | solution.py:791
  71.2 6.3 %shard_map.120 = (bf16[256,1024]{1,0:T(8,128)(2,1)}, f32[256,1024]{1,0:T(8,128)}, f32[256,256]{1,0:T(8,128)S(1)}, bf16[1024,256]{1,0:T(8,128)(2,1)}) custom-call(s32[3]{0:T(128)S(1)} %pad_add_fusion.at_ref, bf16[256,1536]{1,0:T(8,128)(2,1)} %shard_map.118.rows_hbm, bf16[16,128,1024]{2,1,0:T(8,128)(2,1)} %bitcast.7), custom_call_target="tpu_custom_call" | custom-call | tf_op jit(solution)/shard_map/pallas_call | solution.py:37
  80.4 9.4 %all_to_all.46.parts_ref = bf16[8,16,256]{2,1,0:T(8,128)(2,1)S(1)} all-to-all(bf16[8,16,256]{2,1,0:T(8,128)(2,1)S(1)} %get-tuple-element.38), channel_id=1, replica_groups=mesh['dp'=16,'tensor'=8] {'tensor'}, dimensions={0} | all-to-all | bytes 131072 | tf_op jit(solution)/shard_map/all_to_all | solution.py:717
  89.9 11.7 %all_to_all.47.parts_ref = bf16[16,16,256]{2,1,0:T(8,128)(2,1)S(1)} all-to-all(bf16[16,16,256]{2,1,0:T(8,128)(2,1)S(1)} %shard_map.113), channel_id=1, replica_groups=mesh['dp'=16,'tensor'=8] {'dp'}, dimensions={0} | all-to-all | bytes 262144 | tf_op jit(solution)/shard_map/all_to_all | solution.py:717
  101.5 6.2 %shard_map.114 = bf16[8,16,256]{2,1,0:T(8,128)(2,1)S(1)} custom-call(bf16[16,1024,256]{2,1,0:T(8,128)(2,1)} %get-tuple-element.37.expo_hbm, bf16[16,16,256]{2,1,0:T(8,128)(2,1)S(1)} %all_to_all.47.parts_ref, f32[16,256]{1,0:T(8,128)S(1)} %get-tuple-element.39.live_ref), custom_call_target="tpu_custom_call" | custom-call | tf_op jit(solution)/shard_map/pallas_call | solution.py:37
  107.7 9.4 %all_to_all.48.parts_ref = bf16[8,16,256]{2,1,0:T(8,128)(2,1)S(1)} all-to-all(bf16[8,16,256]{2,1,0:T(8,128)(2,1)S(1)} %shard_map.114), channel_id=1, replica_groups=mesh['dp'=16,'tensor'=8] {'tensor'}, dimensions={0} | all-to-all | bytes 131072 | tf_op jit(solution)/shard_map/all_to_all | solution.py:717
  117.1 10.0 %all_to_all.49.parts_ref = bf16[16,16,256]{2,1,0:T(8,128)(2,1)S(1)} all-to-all(bf16[16,16,256]{2,1,0:T(8,128)(2,1)S(1)} %shard_map.115), channel_id=1, replica_groups=mesh['dp'=16,'tensor'=8] {'dp'}, dimensions={0} | all-to-all | bytes 262144 | tf_op jit(solution)/shard_map/all_to_all | solution.py:717
  127.1 8.3 %shard_map.116 = (bf16[16,272,128]{2,1,0:T(8,128)(2,1)S(1)}, bf16[16,272,128]{2,1,0:T(8,128)(2,1)S(1)}, f32[1024,128]{1,0:T(8,128)}) custom-call(s32[3]{0:T(128)S(1)} %pad_add_fusion.at_ref, bf16[16,1024,256]{2,1,0:T(8,128)(2,1)} %get-tuple-element.37.expo_hbm, bf16[16,16,256]{2,1,0:T(8,128)(2,1)S(1)} %all_to_all.49.parts_ref, ...), custom_call_target="tpu_custom_call" | custom-call | tf_op jit(solution)/shard_map/pallas_call | solution.py:37
  135.4 1.9 collective-permute-start.1
  137.3 2.4 collective-permute-done.1
  141.0 9.2 %shard_map.122 = (bf16[16,1024,256]{2,1,0:T(8,128)(2,1)}, bf16[16,272,128]{2,1,0:T(8,128)(2,1)S(1)}, bf16[16,272,128]{2,1,0:T(8,128)(2,1)}) custom-call(s32[3]{0:T(128)S(1)} %pad_add_fusion.at_ref, bf16[1024,256]{1,0:T(8,128)(2,1)S(1)} %copy-done.5, bf16[256,1024]{1,0:T(8,128)(2,1)S(1)} %copy-done.2, bf16[16,256,256]{2,1,0:T(8,128)(2,1)} %bitcast.9), custom_call_target="tpu_custom_call" | custom-call | tf_op jit(solution)/shard_map/pallas_call | solution.py:37
  150.9 3.7 %all-to-all-start.5 = ((bf16[16,272,128]{2,1,0:T(8,128)(2,1)}), bf16[16,272,128]{2,1,0:T(8,128)(2,1)S(1)}, u32[]{:S(2)}, u32[]{:S(2)}) async-start(bf16[16,272,128]{2,1,0:T(8,128)(2,1)} %add_convert_fusion.1), calls=%async_computation.5 | async-start | bytes 2228224 | tf_op jit(solution)/shard_map/all_to_all | solution.py:717
  154.6 2.6 %add_convert_fusion = bf16[16,272,128]{2,1,0:T(8,128)(2,1)} fusion(bf16[16,272,128]{2,1,0:T(8,128)(2,1)} %collective-permute-done.7, bf16[16,272,128]{2,1,0:T(8,128)(2,1)S(1)} %get-tuple-element.48), kind=kLoop, calls=%fused_computation | loop fusion | flops 2228224 | bytes 3342336 | tf_op jit(solution)/shard_map/convert_element_type | solution.py:743
  157.2 16.7 %all-to-all-done.5.parts_hbm = bf16[16,272,128]{2,1,0:T(8,128)(2,1)S(1)} async-done(((bf16[16,272,128]{2,1,0:T(8,128)(2,1)}), bf16[16,272,128]{2,1,0:T(8,128)(2,1)S(1)}, u32[]{:S(2)}, u32[]{:S(2)}) %all-to-all-start.5) | async-done | bytes 1114144 | tf_op jit(solution)/shard_map/all_to_all | solution.py:717
  173.9 3.7 %all-to-all-start.6 = ((bf16[16,272,128]{2,1,0:T(8,128)(2,1)}), bf16[16,272,128]{2,1,0:T(8,128)(2,1)S(1)}, u32[]{:S(2)}, u32[]{:S(2)}) async-start(bf16[16,272,128]{2,1,0:T(8,128)(2,1)} %add_convert_fusion), calls=%async_computation.6 | async-start | bytes 2228224 | tf_op jit(solution)/shard_map/all_to_all | solution.py:717
  182.0 12.3 %all-to-all-done.6.parts_hbm = bf16[16,272,128]{2,1,0:T(8,128)(2,1)S(1)} async-done(((bf16[16,272,128]{2,1,0:T(8,128)(2,1)}), bf16[16,272,128]{2,1,0:T(8,128)(2,1)S(1)}, u32[]{:S(2)}, u32[]{:S(2)}) %all-to-all-start.6) | async-done | bytes 1114144 | tf_op jit(solution)/shard_map/all_to_all | solution.py:717
  198.7 3.6 %collective-permute-start.5 = (f32[1,272,128]{2,1,0:T(8,128)S(1)}, f32[1,272,128]{2,1,0:T(8,128)S(1)}, u32[]{:S(2)}, u32[]{:S(2)}) collective-permute-start(f32[1,272,128]{2,1,0:T(8,128)S(1)} %add_add_fusion.1.pull_ref), channel_id=1, source_target_pairs={{0,1},{1,0},{2,3},{3,2},{4,5},{5,4},{6,7},{7,6},{8,9},{9,8},{10,11... | collective-permute-start | bytes 417800 | tf_op jit(solution)/shard_map/ppermute | solution.py:722
  203.2 3.8 %collective-permute-start.11 = (f32[1,272,128]{2,1,0:T(8,128)S(1)}, f32[1,272,128]{2,1,0:T(8,128)S(1)}, u32[]{:S(2)}, u32[]{:S(2)}) collective-permute-start(f32[1,272,128]{2,1,0:T(8,128)S(1)} %add_add_fusion.push_ref), channel_id=1, source_target_pairs={{0,1},{1,0},{2,3},{3,2},{4,5},{5,4},{6,7},{7,6},{8,9},{9,8},{10,11... | collective-permute-start | bytes 417800 | tf_op jit(solution)/shard_map/ppermute | solution.py:722
  208.0 4.7 %shard_map.124 = (bf16[16,144,256]{2,1,0:T(8,128)(2,1)}, bf16[256,1024]{1,0:T(8,128)(2,1)}, f32[1,4]{1,0:T(1,128)}) custom-call(s32[3]{0:T(128)S(1)} %pad_add_fusion.at_ref, f32[1,272,128]{2,1,0:T(8,128)S(1)} %add_add_fusion.1.pull_ref, f32[1,272,128]{2,1,0:T(8,128)S(1)} %collective-permute-done.5.pull_other_ref, f32[1,272,128]{2,1,0:T(8,128)S(1)} %add_add_fusion.push_ref, ...), custom_call_target="tpu_custom_call" | custom-call | tf_op jit(solution)/shard_map/pallas_call | solution.py:37
  212.7 3.8 %all-to-all-start.7 = ((bf16[16,144,256]{2,1,0:T(8,128)(2,1)}), bf16[16,144,256]{2,1,0:T(8,128)(2,1)S(1)}, u32[]{:S(2)}, u32[]{:S(2)}) async-start(bf16[16,144,256]{2,1,0:T(8,128)(2,1)} %get-tuple-element.55), calls=%async_computation.7 | async-start | bytes 2359296 | tf_op jit(solution)/shard_map/all_to_all | solution.py:717
  216.6 4.0 %shard_map.125.rows_ref = bf16[256,1536]{1,0:T(8,128)(2,1)} custom-call(bf16[256,1024]{1,0:T(8,128)(2,1)S(1)} %copy-done.6, bf16[16,128,1024]{2,1,0:T(8,128)(2,1)} %bitcast.8), custom_call_target="tpu_custom_call" | custom-call | tf_op jit(solution)/shard_map/pallas_call | solution.py:37
  221.0 2.1 collective-permute-done.12.other_ref
  224.3 2.1 shard_map.126
  226.4 9.3 %all-to-all-done.7.got_hbm = bf16[16,144,256]{2,1,0:T(8,128)(2,1)S(1)} async-done(((bf16[16,144,256]{2,1,0:T(8,128)(2,1)}), bf16[16,144,256]{2,1,0:T(8,128)(2,1)S(1)}, u32[]{:S(2)}, u32[]{:S(2)}) %all-to-all-start.7) | async-done | bytes 1179680 | tf_op jit(solution)/shard_map/all_to_all | solution.py:717
  236.9 5.0 %all-to-all-start.8 = ((bf16[8,128,256]{2,1,0:T(8,128)(2,1)}), bf16[8,128,256]{2,1,0:T(8,128)(2,1)S(1)}, u32[]{:S(2)}, u32[]{:S(2)}) async-start(bf16[8,128,256]{2,1,0:T(8,128)(2,1)} %shard_map.127), calls=%async_computation.8 | async-start | bytes 1048576 | tf_op jit(solution)/shard_map/all_to_all | solution.py:717
  241.9 9.3 %shard_map.129 = f32[256,1024]{1,0:T(8,128)} custom-call(bf16[16,1024,256]{2,1,0:T(8,128)(2,1)} %get-tuple-element.37.expo_hbm, bf16[16,1024,256]{2,1,0:T(8,128)(2,1)} %get-tuple-element.61.raised_hbm, f32[1024,128]{1,0:T(8,128)} %get-tuple-element.62.scale_hbm, bf16[16,144,256]{2,1,0:T(8,128)(2,1)S(1)} %all-to-all-done.7.got_hbm, ...), custom_call_target="tpu_custom_call" | custom-call | tf_op jit(solution)/shard_map/pallas_call | solution.py:37
  (60 shorter events, 22.3 us)
Async XLA Ops:
  7.2 2.5 copy-start.3
  7.2 64.0 %all-gather.3.cloned.1.call-start = ((), (), s32[]{:S(2)}) async-start(), calls=%async_computation.9 | async-start | bytes 4456448 | tf_op jit(solution)/shard_map/all_gather | solution.py:791
  9.6 131.4 %all-gather.5.cloned.1.call-start = ((), (), s32[]{:S(2)}) async-start(), calls=%async_computation.10 | async-start | bytes 2228224 | tf_op jit(solution)/shard_map/all_gather | solution.py:852
  9.7 0.7 copy-start.9
  12.7 31.5 %copy-start.1 = (bf16[256,1024]{1,0:T(8,128)(2,1)S(1)}, bf16[256,1024]{1,0:T(8,128)(2,1)}, u32[]{:S(2)}) copy-start(bf16[256,1024]{1,0:T(8,128)(2,1)} %proto_hbm.1) | copy-start | bytes 1572868
  12.7 31.5 %copy-start.4 = (bf16[256,1024]{1,0:T(8,128)(2,1)S(1)}, bf16[256,1024]{1,0:T(8,128)(2,1)}, u32[]{:S(2)}) copy-start(bf16[256,1024]{1,0:T(8,128)(2,1)} %teacher_ref.1) | copy-start | bytes 1572868
  42.0 7.6 %collective-permute-start = (bf16[16,144,256]{2,1,0:T(8,128)(2,1)S(1)}, bf16[16,144,256]{2,1,0:T(8,128)(2,1)S(1)}, u32[]{:S(2)}, u32[]{:S(2)}) collective-permute-start(bf16[16,144,256]{2,1,0:T(8,128)(2,1)S(1)} %all_to_all.45.own_hbm), channel_id=1, source_target_pairs={{0,1},{1,0},{2,3},{3,2},{4,5},{5,4},{6,7},{7,6},{8,9},{9,8},{10,11... | collective-permute-start | bytes 3538952 | tf_op jit(solution)/shard_map/ppermute | solution.py:722
  77.5 2.1 collective-permute-start.6
  101.5 25.6 %copy-start.2 = (bf16[256,1024]{1,0:T(8,128)(2,1)S(1)}, bf16[256,1024]{1,0:T(8,128)(2,1)}, u32[]{:S(2)}) copy-start(bf16[256,1024]{1,0:T(8,128)(2,1)} %get-tuple-element.40.cols_ref) | copy-start | bytes 1572868
  135.4 4.3 %collective-permute-start.1 = (bf16[16,272,128]{2,1,0:T(8,128)(2,1)S(1)}, bf16[16,272,128]{2,1,0:T(8,128)(2,1)S(1)}, u32[]{:S(2)}, u32[]{:S(2)}) collective-permute-start(bf16[16,272,128]{2,1,0:T(8,128)(2,1)S(1)} %get-tuple-element.42), channel_id=1, source_target_pairs={{0,1},{1,0},{2,3},{3,2},{4,5},{5,4},{6,7},{7,6},{8,9},{9,8},{10,11... | collective-permute-start | bytes 3342344 | tf_op jit(solution)/shard_map/ppermute | solution.py:722
  139.7 1.3 copy-start.5
  150.2 4.3 %collective-permute-start.7 = (bf16[16,272,128]{2,1,0:T(8,128)(2,1)}, bf16[16,272,128]{2,1,0:T(8,128)(2,1)}, u32[]{:S(2)}, u32[]{:S(2)}) collective-permute-start(bf16[16,272,128]{2,1,0:T(8,128)(2,1)} %get-tuple-element.49), channel_id=1, source_target_pairs={{0,1},{1,0},{2,3},{3,2},{4,5},{5,4},{6,7},{7,6},{8,9},{9,8},{10,11... | collective-permute-start | bytes 3342344 | tf_op jit(solution)/shard_map/ppermute | solution.py:722
  150.9 23.0 %all-to-all-start.5 = ((bf16[16,272,128]{2,1,0:T(8,128)(2,1)}), bf16[16,272,128]{2,1,0:T(8,128)(2,1)S(1)}, u32[]{:S(2)}, u32[]{:S(2)}) async-start(bf16[16,272,128]{2,1,0:T(8,128)(2,1)} %add_convert_fusion.1), calls=%async_computation.5 | async-start | bytes 2228224 | tf_op jit(solution)/shard_map/all_to_all | solution.py:717
  173.9 20.4 %all-to-all-start.6 = ((bf16[16,272,128]{2,1,0:T(8,128)(2,1)}), bf16[16,272,128]{2,1,0:T(8,128)(2,1)S(1)}, u32[]{:S(2)}, u32[]{:S(2)}) async-start(bf16[16,272,128]{2,1,0:T(8,128)(2,1)} %add_convert_fusion), calls=%async_computation.6 | async-start | bytes 2228224 | tf_op jit(solution)/shard_map/all_to_all | solution.py:717
  178.6 20.0 %copy-start.10 = (bf16[1,272,128]{2,1,0:T(8,128)(2,1)S(1)}, bf16[1,272,128]{2,1,0:T(8,128)(2,1)}, u32[]{:S(2)}) copy-start(bf16[1,272,128]{2,1,0:T(8,128)(2,1)} %shard_map.117) | copy-start | bytes 208900
  178.6 29.4 %copy-start.7 = (f32[8,256]{1,0:T(8,128)S(1)}, f32[8,256]{1,0:T(8,128)}, u32[]{:S(2)}) copy-start(f32[8,256]{1,0:T(8,128)} %get-tuple-element.51.member_ref) | copy-start | bytes 24580
  178.6 29.4 %copy-start.8 = (bf16[16,256]{1,0:T(8,128)(2,1)S(1)}, bf16[16,256]{1,0:T(8,128)(2,1)}, u32[]{:S(2)}) copy-start(bf16[16,256]{1,0:T(8,128)(2,1)} %get-tuple-element.50.mine_ref) | copy-start | bytes 24580
  178.6 18.9 %collective-permute-start.4 = (bf16[1,272,128]{2,1,0:T(8,128)(2,1)}, bf16[1,272,128]{2,1,0:T(8,128)(2,1)S(1)}, u32[]{:S(2)}, u32[]{:S(2)}) collective-permute-start(bf16[1,272,128]{2,1,0:T(8,128)(2,1)} %shard_map.117), channel_id=1, source_target_pairs={{0,6},{1,7},{2,4},{3,5},{4,2},{5,3},{6,0},{7,1},{8,14},{9,15},{10,... | collective-permute-start | bytes 208904 | tf_op jit(solution)/shard_map/ppermute | solution.py:733
  180.3 18.3 %collective-permute-start.3 = (bf16[1,272,128]{2,1,0:T(8,128)(2,1)}, bf16[1,272,128]{2,1,0:T(8,128)(2,1)S(1)}, u32[]{:S(2)}, u32[]{:S(2)}) collective-permute-start(bf16[1,272,128]{2,1,0:T(8,128)(2,1)} %shard_map.117), channel_id=1, source_target_pairs={{0,4},{1,5},{2,6},{3,7},{4,0},{5,1},{6,2},{7,3},{8,12},{9,13},{10,... | collective-permute-start | bytes 208904 | tf_op jit(solution)/shard_map/ppermute | solution.py:733
  181.0 17.7 %collective-permute-start.2 = (bf16[1,272,128]{2,1,0:T(8,128)(2,1)}, bf16[1,272,128]{2,1,0:T(8,128)(2,1)S(1)}, u32[]{:S(2)}, u32[]{:S(2)}) collective-permute-start(bf16[1,272,128]{2,1,0:T(8,128)(2,1)} %shard_map.117), channel_id=1, source_target_pairs={{0,2},{1,3},{2,0},{3,1},{4,6},{5,7},{6,4},{7,5},{8,10},{9,11},{10,... | collective-permute-start | bytes 208904 | tf_op jit(solution)/shard_map/ppermute | solution.py:733
  195.3 7.0 %collective-permute-start.10 = (bf16[1,272,128]{2,1,0:T(8,128)(2,1)}, bf16[1,272,128]{2,1,0:T(8,128)(2,1)S(1)}, u32[]{:S(2)}, u32[]{:S(2)}) collective-permute-start(bf16[1,272,128]{2,1,0:T(8,128)(2,1)} %shard_map.123), channel_id=1, source_target_pairs={{0,6},{1,7},{2,4},{3,5},{4,2},{5,3},{6,0},{7,1},{8,14},{9,15},{10,... | collective-permute-start | bytes 208904 | tf_op jit(solution)/shard_map/ppermute | solution.py:733
  197.0 5.3 %collective-permute-start.9 = (bf16[1,272,128]{2,1,0:T(8,128)(2,1)}, bf16[1,272,128]{2,1,0:T(8,128)(2,1)S(1)}, u32[]{:S(2)}, u32[]{:S(2)}) collective-permute-start(bf16[1,272,128]{2,1,0:T(8,128)(2,1)} %shard_map.123), channel_id=1, source_target_pairs={{0,4},{1,5},{2,6},{3,7},{4,0},{5,1},{6,2},{7,3},{8,12},{9,13},{10,... | collective-permute-start | bytes 208904 | tf_op jit(solution)/shard_map/ppermute | solution.py:733
  197.6 4.7 %collective-permute-start.8 = (bf16[1,272,128]{2,1,0:T(8,128)(2,1)}, bf16[1,272,128]{2,1,0:T(8,128)(2,1)S(1)}, u32[]{:S(2)}, u32[]{:S(2)}) collective-permute-start(bf16[1,272,128]{2,1,0:T(8,128)(2,1)} %shard_map.123), channel_id=1, source_target_pairs={{0,2},{1,3},{2,0},{3,1},{4,6},{5,7},{6,4},{7,5},{8,10},{9,11},{10,... | collective-permute-start | bytes 208904 | tf_op jit(solution)/shard_map/ppermute | solution.py:733
  198.7 8.3 %collective-permute-start.5 = (f32[1,272,128]{2,1,0:T(8,128)S(1)}, f32[1,272,128]{2,1,0:T(8,128)S(1)}, u32[]{:S(2)}, u32[]{:S(2)}) collective-permute-start(f32[1,272,128]{2,1,0:T(8,128)S(1)} %add_add_fusion.1.pull_ref), channel_id=1, source_target_pairs={{0,1},{1,0},{2,3},{3,2},{4,5},{5,4},{6,7},{7,6},{8,9},{9,8},{10,11... | collective-permute-start | bytes 417800 | tf_op jit(solution)/shard_map/ppermute | solution.py:722
  203.2 4.8 %collective-permute-start.11 = (f32[1,272,128]{2,1,0:T(8,128)S(1)}, f32[1,272,128]{2,1,0:T(8,128)S(1)}, u32[]{:S(2)}, u32[]{:S(2)}) collective-permute-start(f32[1,272,128]{2,1,0:T(8,128)S(1)} %add_add_fusion.push_ref), channel_id=1, source_target_pairs={{0,1},{1,0},{2,3},{3,2},{4,5},{5,4},{6,7},{7,6},{8,9},{9,8},{10,11... | collective-permute-start | bytes 417800 | tf_op jit(solution)/shard_map/ppermute | solution.py:722
  212.7 3.9 %copy-start.6 = (bf16[256,1024]{1,0:T(8,128)(2,1)S(1)}, bf16[256,1024]{1,0:T(8,128)(2,1)}, u32[]{:S(2)}) copy-start(bf16[256,1024]{1,0:T(8,128)(2,1)} %get-tuple-element.56.pre_ref) | copy-start | bytes 1572868
  212.7 23.0 %all-to-all-start.7 = ((bf16[16,144,256]{2,1,0:T(8,128)(2,1)}), bf16[16,144,256]{2,1,0:T(8,128)(2,1)S(1)}, u32[]{:S(2)}, u32[]{:S(2)}) async-start(bf16[16,144,256]{2,1,0:T(8,128)(2,1)} %get-tuple-element.55), calls=%async_computation.7 | async-start | bytes 2359296 | tf_op jit(solution)/shard_map/all_to_all | solution.py:717
  220.6 2.6 collective-permute-start.12
  223.1 1.1 copy-start
  236.9 14.4 %all-to-all-start.8 = ((bf16[8,128,256]{2,1,0:T(8,128)(2,1)}), bf16[8,128,256]{2,1,0:T(8,128)(2,1)S(1)}, u32[]{:S(2)}, u32[]{:S(2)}) async-start(bf16[8,128,256]{2,1,0:T(8,128)(2,1)} %shard_map.127), calls=%async_computation.8 | async-start | bytes 1048576 | tf_op jit(solution)/shard_map/all_to_all | solution.py:717
Sparse Core Ops, SparseCore 0:
  10.1 60.9 all-gather.2
  80.5 42.8 all-gather.4

commit v4 on v3

--- a/solution.py
+++ b/solution.py
@@ -264,7 +264,7 @@
 
 def expo_body(
     at_ref, cols_hbm, own_hbm, other_hbm, expo_hbm, part_ref, live_ref,
-    cols_ref, rows_ref, tail_ref, expo_ref, total_ref, sums_ref, sems, own_sems, other_sems, tail_sems,
+    cols_ref, rows_ref, tail_ref, expo_ref, total_ref, sems, own_sems, other_sems, tail_sems,
 ):
     peers = own_hbm.shape[0]
     width = cols_ref.shape[0]
@@ -299,7 +299,7 @@
 
     over_groups(peers, first, (load_own, load_other), (store,), UNROLL)
     spread_scale(total_ref)
-    row_parts(expo_ref, total_ref, sums_ref, part_ref)
+    row_parts(expo_ref, total_ref, part_ref)
     wait_all(number, store)
 
 
@@ -313,24 +313,19 @@
     return jnp.concatenate([expo[:, 0:128] * scale, expo[:, 128:256] * scale], axis=1)
 
 
-def row_parts(expo_ref, scale_ref, sums_ref, part_ref):
+def row_parts(expo_ref, scale_ref, part_ref):
     def step(g):
         acc = jnp.zeros((8, CAP), f32)
         for part in chunks_of(scale_ref.shape[0]):
             acc = acc + fold(scaled(expo_ref[g, part, :].astype(f32), scale_ref[part, :]))
-        sums_ref[pl.ds(g, 1), :] = jnp.sum(acc, axis=0, keepdims=True)
+        part_ref[pl.ds(g, 1), :] = jnp.sum(acc, axis=0, keepdims=True)
         return 0
 
     over_groups(expo_ref.shape[0], step, unroll=UNROLL)
-    sums = sums_ref[...].astype(bf16)
-    for t in range(part_ref.shape[0]):
-        part_ref[t] = sums
-
-
-def relay_body(parts_ref, out_ref):
-    sums = parts_ref[0].astype(f32)
-    for t in range(1, parts_ref.shape[0]):
-        sums = sums + parts_ref[t].astype(f32)
+
+
+def relay_body(own_ref, near_ref, far_ref, last_ref, out_ref):
+    sums = (own_ref[...] + near_ref[...]) + (far_ref[...] + last_ref[...])
     sums = sums.astype(bf16)
     for g in range(out_ref.shape[0]):
         out_ref[g] = sums
@@ -358,12 +353,12 @@
     spread_scale(total_ref)
 
 
-def balance_body(expo_hbm, parts_ref, live_ref, part_ref, expo_ref, total_ref, sums_ref, scale_ref, sems):
+def balance_body(expo_hbm, parts_ref, live_ref, part_ref, expo_ref, total_ref, scale_ref, sems):
     load = lambda q: pltpu.make_async_copy(group(expo_hbm, q), group(expo_ref, q), sems.at[q])
     start_all(expo_ref.shape[0] // GROUP, load)
     scales_from(parts_ref, live_ref, scale_ref)
     column_sums(load, expo_ref, scale_ref, total_ref)
-    row_parts(expo_ref, total_ref, sums_ref, part_ref)
+    row_parts(expo_ref, total_ref, part_ref)
 
 
 def divide_up(g, acc, pull, halves_ref):
@@ -621,12 +616,12 @@
     return pltpu.SemaphoreType.DMA((number,))
 
 
-def run_expo(at, cols_t, own, other, tensor):
+def run_expo(at, cols_t, own, other):
     dp, (width, bot) = (own.shape[0], cols_t.shape)
     big, small = ((dp, width, CAP), (dp, CAP))
     return call(
         expo_body,
-        [(big, bf16), ((tensor, *small), bf16), (small, f32)],
+        [(big, bf16), (small, f32), (small, f32)],
         (at, cols_t, own, other),
         in_specs=[SMEM, HBM, ANY, ANY],
         out_specs=[HBM, VMEM, VMEM],
@@ -636,21 +631,20 @@
             pltpu.VMEM((dp, EXTRA, bot), bf16),
             pltpu.VMEM(big, bf16),
             pltpu.VMEM((width, 128), f32),
-            pltpu.VMEM(small, f32),
             *[sem(dp // GROUP)] * 4,
         ],
     )
 
 
-def run_balance(expo, got, live, tensor):
+def run_balance(expo, got, live):
     dp, width, _ = expo.shape
     small = pltpu.VMEM(live.shape, f32)
     return call(
         balance_body,
-        [((tensor, *live.shape), bf16)],
+        [(live.shape, f32)],
         (expo, got, live),
         in_specs=[HBM, VMEM, VMEM],
-        scratch=[pltpu.VMEM(expo.shape, bf16), pltpu.VMEM((width, 128), f32), small, small, sem(dp // GROUP)],
+        scratch=[pltpu.VMEM(expo.shape, bf16), pltpu.VMEM((width, 128), f32), small, sem(dp // GROUP)],
     )[0]
 
 
@@ -722,9 +716,10 @@
     return lax.ppermute(x, "tensor", [(i, i ^ 1) for i in range(peers)])
 
 
-def everywhere(part, small):
-    got = exchange(part, "tensor")
-    (sums,) = call(relay_body, [((small[0], *small), bf16)], (got,))
+def everywhere(part):
+    both = part + sibling(part)
+    near, far, last = (levels(both, by) for by in (1, 2, 3))
+    (sums,) = call(relay_body, [((part.shape[0], *part.shape), bf16)], (both, near, far, last))
     return exchange(sums, "dp")
 
 
@@ -821,7 +816,7 @@
             sem(4),
         ],
     )
-    expo, part, live = run_expo(at, teacher_t, packs, others, tensor)
+    expo, part, live = run_expo(at, teacher_t, packs, others)
     w_held = [pltpu.VMEM((dim, half), bf16), pltpu.VMEM((half, bot), bf16)]
     (rows,) = call(
         tokens_body,
@@ -850,9 +845,9 @@
     feats_other = sibling(feats)
     (student_rows,) = call(unit_body, [((CAP, bot), bf16)], (feats, feats_other))
     all_rows = lax.all_gather(student_rows, "dp", axis=0, tiled=True).reshape(dp, CAP, bot)
-    got = everywhere(part, live.shape)
-    part = run_balance(expo, got, live, tensor)
-    got = everywhere(part, live.shape)
+    got = everywhere(part)
+    part = run_balance(expo, got, live)
+    got = everywhere(part)
     keep, give, scale = run_last(at, expo, got, live, cols)
     pull = paired(keep, give)
     pull_got = exchange(pull, "dp")

time: 261 us -> 260 us (level)
  blocking collectives: 69.7 us -> 51.6 us
  starting transfers between devices: 36.5 us -> 47.4 us
  waiting for transfers between devices: 58.6 us -> 65.6 us
    all_to_all x5 -> x3, blocking collectives: 69.7 us -> 51.6 us  [exchange(): return lax.all_to_all(x, axis, split_axis=0, concat_axis=0, tiled=True)]
    ppermute x6 -> x12, starting transfers between devices: 6.67 us -> 13.2 us  [levels(): return lax.ppermute(x, 'tensor', [(i, i ^ 2 * by) for i in range(peers)])]
    ppermute x6 -> x12, waiting for transfers between devices: 0.02 us -> 5.39 us  [levels(): return lax.ppermute(x, 'tensor', [(i, i ^ 2 * by) for i in range(peers)])]
    ppermute x7 -> x9, starting transfers between devices: 13.5 us -> 17.8 us  [sibling(): return lax.ppermute(x, 'tensor', [(i, i ^ 1) for i in range(peers)])]
    ppermute x7 -> x9, waiting for transfers between devices: 6.68 us -> 8.36 us  [sibling(): return lax.ppermute(x, 'tensor', [(i, i ^ 1) for i in range(peers)])]
  transfers between devices with their start and end apart: 19 -> 27, of which waited for: 8 -> 14; matrix products, arithmetic and copies ran while one was open for 2% -> 2% of each run, Pallas kernels for 18% -> 18%
where the time goes in v4:
time: 260 us; the launch traced here: 259 us
  Pallas kernels  73.8 us (28%)
  waiting for transfers between devices  65.6 us (25%)
  blocking collectives  51.6 us (20%)
  starting transfers between devices  47.4 us (18%)
  between operations  14.4 us (6%)
  other arithmetic  4.96 us (2%)
    pallas_call x20, Pallas kernels, call(): pl.pallas_call(body, out_shape=outs, in_specs=in_specs, out_specs=tuple(s...  73.8 us
    all_to_all x3, blocking collectives, exchange(): return lax.all_to_all(x, axis, split_axis=0, concat_axis=0, tiled=True)  51.6 us
    all_to_all x4, waiting for transfers between devices, exchange(): return lax.all_to_all(x, axis, split_axis=0, concat_axis=0, tiled=True)  38.3 us
    ppermute x9, starting transfers between devices, sibling(): return lax.ppermute(x, 'tensor', [(i, i ^ 1) for i in range(peers)])  17.8 us
    all_to_all x4, starting transfers between devices, exchange(): return lax.all_to_all(x, axis, split_axis=0, concat_axis=0, tiled=True)  16.2 us
    all_gather x1, waiting for transfers between devices, parts_of(): lax.all_gather(w_pack, 'dp', axis=0, tiled=True).reshape(dp, lines, half)  13.5 us
    ppermute x12, starting transfers between devices, levels(): return lax.ppermute(x, 'tensor', [(i, i ^ 2 * by) for i in range(peers)])  13.2 us
    ppermute x9, waiting for transfers between devices, sibling(): return lax.ppermute(x, 'tensor', [(i, i ^ 1) for i in range(peers)])  8.36 us
  transfers between devices with their start and end apart: 27, of which 14 were waited for; matrix products, arithmetic and copies ran while one was open for 2% of the time, Pallas kernels for 18%

profile of v4, /device:TPU:1, one launch (start us, length us, event | category | flops | bytes accessed | tf_op | source)
XLA Modules:
  0.0 259.5 jit_solution(5118480801918318709)
XLA Ops:
  7.3 2.2 shard_map.119
  10.3 2.4 shard_map.111
  12.7 29.3 %all_to_all.35.own_hbm = bf16[16,144,256]{2,1,0:T(8,128)(2,1)S(1)} all-to-all(bf16[16,144,256]{2,1,0:T(8,128)(2,1)} %get-tuple-element.36), channel_id=1, replica_groups=mesh['dp'=16,'tensor'=8] {'dp'}, dimensions={0} | all-to-all | bytes 2359296 | tf_op jit(solution)/shard_map/all_to_all | solution.py:711
  42.0 2.2 collective-permute-start
  45.7 3.8 %shard_map.118.rows_hbm = bf16[256,1536]{1,0:T(8,128)(2,1)} custom-call(bf16[256,1024]{1,0:T(8,128)(2,1)S(1)} %get-tuple-element.44.sel_ref, bf16[1024,1536]{1,0:T(8,128)(2,1)} %tokens_hbm.1), custom_call_target="tpu_custom_call" | custom-call | tf_op jit(solution)/shard_map/pallas_call | solution.py:37
  49.5 8.1 %shard_map.112 = (bf16[16,1024,256]{2,1,0:T(8,128)(2,1)}, f32[16,256]{1,0:T(8,128)S(1)}, f32[16,256]{1,0:T(8,128)S(1)}) custom-call(s32[3]{0:T(128)S(1)} %pad_add_fusion.at_ref, bf16[1024,256]{1,0:T(8,128)(2,1)} %get-tuple-element.35.cols_hbm, bf16[16,144,256]{2,1,0:T(8,128)(2,1)S(1)} %all_to_all.35.own_hbm, ...), custom_call_target="tpu_custom_call" | custom-call | tf_op jit(solution)/shard_map/pallas_call | solution.py:37
  57.6 13.5 %all-gather.3.cloned.1.call-done = bf16[2048,1024]{1,0:T(8,128)(2,1)} async-done(((bf16[128,1024]{1,0:T(8,128)(2,1)}), bf16[2048,1024]{1,0:T(8,128)(2,1)}) %all-gather.3.cloned.1.call-update) | async-done | bytes 4194320 | tf_op jit(solution)/shard_map/all_gather | solution.py:786
  71.2 6.3 %shard_map.120 = (bf16[256,1024]{1,0:T(8,128)(2,1)}, f32[256,1024]{1,0:T(8,128)}, f32[256,256]{1,0:T(8,128)S(1)}, bf16[1024,256]{1,0:T(8,128)(2,1)}) custom-call(s32[3]{0:T(128)S(1)} %pad_add_fusion.at_ref, bf16[256,1536]{1,0:T(8,128)(2,1)} %shard_map.118.rows_hbm, bf16[16,128,1024]{2,1,0:T(8,128)(2,1)} %bitcast.7), custom_call_target="tpu_custom_call" | custom-call | tf_op jit(solution)/shard_map/pallas_call | solution.py:37
  81.7 2.7 %collective-permute-start.4 = (f32[16,256]{1,0:T(8,128)S(1)}, f32[16,256]{1,0:T(8,128)S(1)}, u32[]{:S(2)}, u32[]{:S(2)}) collective-permute-start(f32[16,256]{1,0:T(8,128)S(1)} %add.37.own_ref), channel_id=1, source_target_pairs={{0,6},{1,7},{2,4},{3,5},{4,2},{5,3},{6,0},{7,1},{8,14},{9,15},{10,... | collective-permute-start | bytes 49160 | tf_op jit(solution)/shard_map/ppermute | solution.py:728
  85.5 3.0 %collective-permute-done.3.far_ref = f32[16,256]{1,0:T(8,128)S(1)} collective-permute-done((f32[16,256]{1,0:T(8,128)S(1)}, f32[16,256]{1,0:T(8,128)S(1)}, u32[]{:S(2)}, u32[]{:S(2)}) %collective-permute-start.3) | collective-permute-done | bytes 16416 | tf_op jit(solution)/shard_map/ppermute | solution.py:728
  88.5 12.0 %all_to_all.36.parts_ref = bf16[16,16,256]{2,1,0:T(8,128)(2,1)S(1)} all-to-all(bf16[16,16,256]{2,1,0:T(8,128)(2,1)S(1)} %shard_map.113), channel_id=1, replica_groups=mesh['dp'=16,'tensor'=8] {'dp'}, dimensions={0} | all-to-all | bytes 262144 | tf_op jit(solution)/shard_map/all_to_all | solution.py:711
  100.4 6.2 %shard_map.114 = f32[16,256]{1,0:T(8,128)S(1)} custom-call(bf16[16,1024,256]{2,1,0:T(8,128)(2,1)} %get-tuple-element.37.expo_hbm, bf16[16,16,256]{2,1,0:T(8,128)(2,1)S(1)} %all_to_all.36.parts_ref, f32[16,256]{1,0:T(8,128)S(1)} %get-tuple-element.39.live_ref), custom_call_target="tpu_custom_call" | custom-call | tf_op jit(solution)/shard_map/pallas_call | solution.py:37
  106.6 2.9 %collective-permute-start.5 = (f32[16,256]{1,0:T(8,128)S(1)}, f32[16,256]{1,0:T(8,128)S(1)}, u32[]{:S(2)}, u32[]{:S(2)}) collective-permute-start(f32[16,256]{1,0:T(8,128)S(1)} %shard_map.114), channel_id=1, source_target_pairs={{0,1},{1,0},{2,3},{3,2},{4,5},{5,4},{6,7},{7,6},{8,9},{9,8},{10,11... | collective-permute-start | bytes 49160 | tf_op jit(solution)/shard_map/ppermute | solution.py:716
  115.6 10.4 %all_to_all.37.parts_ref = bf16[16,16,256]{2,1,0:T(8,128)(2,1)S(1)} all-to-all(bf16[16,16,256]{2,1,0:T(8,128)(2,1)S(1)} %shard_map.115), channel_id=1, replica_groups=mesh['dp'=16,'tensor'=8] {'dp'}, dimensions={0} | all-to-all | bytes 262144 | tf_op jit(solution)/shard_map/all_to_all | solution.py:711
  126.0 8.3 %shard_map.116 = (bf16[16,272,128]{2,1,0:T(8,128)(2,1)S(1)}, bf16[16,272,128]{2,1,0:T(8,128)(2,1)S(1)}, f32[1024,128]{1,0:T(8,128)}) custom-call(s32[3]{0:T(128)S(1)} %pad_add_fusion.at_ref, bf16[16,1024,256]{2,1,0:T(8,128)(2,1)} %get-tuple-element.37.expo_hbm, bf16[16,16,256]{2,1,0:T(8,128)(2,1)S(1)} %all_to_all.37.parts_ref, ...), custom_call_target="tpu_custom_call" | custom-call | tf_op jit(solution)/shard_map/pallas_call | solution.py:37
  134.3 2.8 %collective-permute-start.9 = (bf16[16,272,128]{2,1,0:T(8,128)(2,1)S(1)}, bf16[16,272,128]{2,1,0:T(8,128)(2,1)S(1)}, u32[]{:S(2)}, u32[]{:S(2)}) collective-permute-start(bf16[16,272,128]{2,1,0:T(8,128)(2,1)S(1)} %get-tuple-element.42), channel_id=1, source_target_pairs={{0,1},{1,0},{2,3},{3,2},{4,5},{5,4},{6,7},{7,6},{8,9},{9,8},{10,11... | collective-permute-start | bytes 3342344 | tf_op jit(solution)/shard_map/ppermute | solution.py:716
  137.0 2.4 collective-permute-done.9
  140.7 9.2 %shard_map.122 = (bf16[16,1024,256]{2,1,0:T(8,128)(2,1)}, bf16[16,272,128]{2,1,0:T(8,128)(2,1)S(1)}, bf16[16,272,128]{2,1,0:T(8,128)(2,1)}) custom-call(s32[3]{0:T(128)S(1)} %pad_add_fusion.at_ref, bf16[1024,256]{1,0:T(8,128)(2,1)S(1)} %copy-done.5, bf16[256,1024]{1,0:T(8,128)(2,1)S(1)} %copy-done.2, bf16[16,256,256]{2,1,0:T(8,128)(2,1)} %bitcast.9), custom_call_target="tpu_custom_call" | custom-call | tf_op jit(solution)/shard_map/pallas_call | solution.py:37
  150.4 3.7 %all-to-all-start.3 = ((bf16[16,272,128]{2,1,0:T(8,128)(2,1)}), bf16[16,272,128]{2,1,0:T(8,128)(2,1)S(1)}, u32[]{:S(2)}, u32[]{:S(2)}) async-start(bf16[16,272,128]{2,1,0:T(8,128)(2,1)} %add_convert_fusion.1), calls=%async_computation.3 | async-start | bytes 2228224 | tf_op jit(solution)/shard_map/all_to_all | solution.py:711
  154.1 2.6 %add_convert_fusion = bf16[16,272,128]{2,1,0:T(8,128)(2,1)} fusion(bf16[16,272,128]{2,1,0:T(8,128)(2,1)} %collective-permute-done.15, bf16[16,272,128]{2,1,0:T(8,128)(2,1)S(1)} %get-tuple-element.48), kind=kLoop, calls=%fused_computation | loop fusion | flops 2228224 | bytes 3342336 | tf_op jit(solution)/shard_map/convert_element_type | solution.py:738
  156.7 16.6 %all-to-all-done.3.parts_hbm = bf16[16,272,128]{2,1,0:T(8,128)(2,1)S(1)} async-done(((bf16[16,272,128]{2,1,0:T(8,128)(2,1)}), bf16[16,272,128]{2,1,0:T(8,128)(2,1)S(1)}, u32[]{:S(2)}, u32[]{:S(2)}) %all-to-all-start.3) | async-done | bytes 1114144 | tf_op jit(solution)/shard_map/all_to_all | solution.py:711
  173.4 3.7 %all-to-all-start.4 = ((bf16[16,272,128]{2,1,0:T(8,128)(2,1)}), bf16[16,272,128]{2,1,0:T(8,128)(2,1)S(1)}, u32[]{:S(2)}, u32[]{:S(2)}) async-start(bf16[16,272,128]{2,1,0:T(8,128)(2,1)} %add_convert_fusion), calls=%async_computation.4 | async-start | bytes 2228224 | tf_op jit(solution)/shard_map/all_to_all | solution.py:711
  181.5 12.3 %all-to-all-done.4.parts_hbm = bf16[16,272,128]{2,1,0:T(8,128)(2,1)S(1)} async-done(((bf16[16,272,128]{2,1,0:T(8,128)(2,1)}), bf16[16,272,128]{2,1,0:T(8,128)(2,1)S(1)}, u32[]{:S(2)}, u32[]{:S(2)}) %all-to-all-start.4) | async-done | bytes 1114144 | tf_op jit(solution)/shard_map/all_to_all | solution.py:711
  198.2 3.6 %collective-permute-start.13 = (f32[1,272,128]{2,1,0:T(8,128)S(1)}, f32[1,272,128]{2,1,0:T(8,128)S(1)}, u32[]{:S(2)}, u32[]{:S(2)}) collective-permute-start(f32[1,272,128]{2,1,0:T(8,128)S(1)} %add_add_fusion.1.pull_ref), channel_id=1, source_target_pairs={{0,1},{1,0},{2,3},{3,2},{4,5},{5,4},{6,7},{7,6},{8,9},{9,8},{10,11... | collective-permute-start | bytes 417800 | tf_op jit(solution)/shard_map/ppermute | solution.py:716
  202.7 4.0 %collective-permute-start.19 = (f32[1,272,128]{2,1,0:T(8,128)S(1)}, f32[1,272,128]{2,1,0:T(8,128)S(1)}, u32[]{:S(2)}, u32[]{:S(2)}) collective-permute-start(f32[1,272,128]{2,1,0:T(8,128)S(1)} %add_add_fusion.push_ref), channel_id=1, source_target_pairs={{0,1},{1,0},{2,3},{3,2},{4,5},{5,4},{6,7},{7,6},{8,9},{9,8},{10,11... | collective-permute-start | bytes 417800 | tf_op jit(solution)/shard_map/ppermute | solution.py:716
  207.8 4.7 %shard_map.124 = (bf16[16,144,256]{2,1,0:T(8,128)(2,1)}, bf16[256,1024]{1,0:T(8,128)(2,1)}, f32[1,4]{1,0:T(1,128)}) custom-call(s32[3]{0:T(128)S(1)} %pad_add_fusion.at_ref, f32[1,272,128]{2,1,0:T(8,128)S(1)} %add_add_fusion.1.pull_ref, f32[1,272,128]{2,1,0:T(8,128)S(1)} %collective-permute-done.13.pull_other_ref, f32[1,272,128]{2,1,0:T(8,128)S(1)} %add_add_fusion.push_ref, ...), custom_call_target="tpu_custom_call" | custom-call | tf_op jit(solution)/shard_map/pallas_call | solution.py:37
  212.5 3.8 %all-to-all-start.5 = ((bf16[16,144,256]{2,1,0:T(8,128)(2,1)}), bf16[16,144,256]{2,1,0:T(8,128)(2,1)S(1)}, u32[]{:S(2)}, u32[]{:S(2)}) async-start(bf16[16,144,256]{2,1,0:T(8,128)(2,1)} %get-tuple-element.55), calls=%async_computation.5 | async-start | bytes 2359296 | tf_op jit(solution)/shard_map/all_to_all | solution.py:711
  216.4 4.0 %shard_map.125.rows_ref = bf16[256,1536]{1,0:T(8,128)(2,1)} custom-call(bf16[256,1024]{1,0:T(8,128)(2,1)S(1)} %copy-done.6, bf16[16,128,1024]{2,1,0:T(8,128)(2,1)} %bitcast.8), custom_call_target="tpu_custom_call" | custom-call | tf_op jit(solution)/shard_map/pallas_call | solution.py:37
  220.8 2.1 collective-permute-done.20.other_ref
  226.2 9.3 %all-to-all-done.5.got_hbm = bf16[16,144,256]{2,1,0:T(8,128)(2,1)S(1)} async-done(((bf16[16,144,256]{2,1,0:T(8,128)(2,1)}), bf16[16,144,256]{2,1,0:T(8,128)(2,1)S(1)}, u32[]{:S(2)}, u32[]{:S(2)}) %all-to-all-start.5) | async-done | bytes 1179680 | tf_op jit(solution)/shard_map/all_to_all | solution.py:711
  236.7 5.0 %all-to-all-start.6 = ((bf16[8,128,256]{2,1,0:T(8,128)(2,1)}), bf16[8,128,256]{2,1,0:T(8,128)(2,1)S(1)}, u32[]{:S(2)}, u32[]{:S(2)}) async-start(bf16[8,128,256]{2,1,0:T(8,128)(2,1)} %shard_map.127), calls=%async_computation.6 | async-start | bytes 1048576 | tf_op jit(solution)/shard_map/all_to_all | solution.py:711
  241.7 9.3 %shard_map.129 = f32[256,1024]{1,0:T(8,128)} custom-call(bf16[16,1024,256]{2,1,0:T(8,128)(2,1)} %get-tuple-element.37.expo_hbm, bf16[16,1024,256]{2,1,0:T(8,128)(2,1)} %get-tuple-element.61.raised_hbm, f32[1024,128]{1,0:T(8,128)} %get-tuple-element.62.scale_hbm, bf16[16,144,256]{2,1,0:T(8,128)(2,1)S(1)} %all-to-all-done.5.got_hbm, ...), custom_call_target="tpu_custom_call" | custom-call | tf_op jit(solution)/shard_map/pallas_call | solution.py:37
  (76 shorter events, 32.7 us)
Async XLA Ops:
  7.2 64.0 %all-gather.3.cloned.1.call-start = ((), (), s32[]{:S(2)}) async-start(), calls=%async_computation.7 | async-start | bytes 4456448 | tf_op jit(solution)/shard_map/all_gather | solution.py:786
  9.6 131.1 %all-gather.5.cloned.1.call-start = ((), (), s32[]{:S(2)}) async-start(), calls=%async_computation.8 | async-start | bytes 2228224 | tf_op jit(solution)/shard_map/all_gather | solution.py:847
  12.7 31.5 %copy-start.1 = (bf16[256,1024]{1,0:T(8,128)(2,1)S(1)}, bf16[256,1024]{1,0:T(8,128)(2,1)}, u32[]{:S(2)}) copy-start(bf16[256,1024]{1,0:T(8,128)(2,1)} %proto_hbm.1) | copy-start | bytes 1572868
  12.7 31.5 %copy-start.4 = (bf16[256,1024]{1,0:T(8,128)(2,1)S(1)}, bf16[256,1024]{1,0:T(8,128)(2,1)}, u32[]{:S(2)}) copy-start(bf16[256,1024]{1,0:T(8,128)(2,1)} %teacher_ref.1) | copy-start | bytes 1572868
  42.0 7.5 %collective-permute-start = (bf16[16,144,256]{2,1,0:T(8,128)(2,1)S(1)}, bf16[16,144,256]{2,1,0:T(8,128)(2,1)S(1)}, u32[]{:S(2)}, u32[]{:S(2)}) collective-permute-start(bf16[16,144,256]{2,1,0:T(8,128)(2,1)S(1)} %all_to_all.35.own_hbm), channel_id=1, source_target_pairs={{0,1},{1,0},{2,3},{3,2},{4,5},{5,4},{6,7},{7,6},{8,9},{9,8},{10,11... | collective-permute-start | bytes 3538952 | tf_op jit(solution)/shard_map/ppermute | solution.py:716
  77.5 2.1 collective-permute-start.14
  80.4 1.3 collective-permute-start.1
  81.7 3.8 %collective-permute-start.4 = (f32[16,256]{1,0:T(8,128)S(1)}, f32[16,256]{1,0:T(8,128)S(1)}, u32[]{:S(2)}, u32[]{:S(2)}) collective-permute-start(f32[16,256]{1,0:T(8,128)S(1)} %add.37.own_ref), channel_id=1, source_target_pairs={{0,6},{1,7},{2,4},{3,5},{4,2},{5,3},{6,0},{7,1},{8,14},{9,15},{10,... | collective-permute-start | bytes 49160 | tf_op jit(solution)/shard_map/ppermute | solution.py:728
  84.4 4.1 %collective-permute-start.3 = (f32[16,256]{1,0:T(8,128)S(1)}, f32[16,256]{1,0:T(8,128)S(1)}, u32[]{:S(2)}, u32[]{:S(2)}) collective-permute-start(f32[16,256]{1,0:T(8,128)S(1)} %add.37.own_ref), channel_id=1, source_target_pairs={{0,4},{1,5},{2,6},{3,7},{4,0},{5,1},{6,2},{7,3},{8,12},{9,13},{10,... | collective-permute-start | bytes 49160 | tf_op jit(solution)/shard_map/ppermute | solution.py:728
  84.7 3.7 %collective-permute-start.2 = (f32[16,256]{1,0:T(8,128)S(1)}, f32[16,256]{1,0:T(8,128)S(1)}, u32[]{:S(2)}, u32[]{:S(2)}) collective-permute-start(f32[16,256]{1,0:T(8,128)S(1)} %add.37.own_ref), channel_id=1, source_target_pairs={{0,2},{1,3},{2,0},{3,1},{4,6},{5,7},{6,4},{7,5},{8,10},{9,11},{10,... | collective-permute-start | bytes 49160 | tf_op jit(solution)/shard_map/ppermute | solution.py:728
  100.4 25.5 %copy-start.2 = (bf16[256,1024]{1,0:T(8,128)(2,1)S(1)}, bf16[256,1024]{1,0:T(8,128)(2,1)}, u32[]{:S(2)}) copy-start(bf16[256,1024]{1,0:T(8,128)(2,1)} %get-tuple-element.40.cols_ref) | copy-start | bytes 1572868
  106.6 3.8 %collective-permute-start.5 = (f32[16,256]{1,0:T(8,128)S(1)}, f32[16,256]{1,0:T(8,128)S(1)}, u32[]{:S(2)}, u32[]{:S(2)}) collective-permute-start(f32[16,256]{1,0:T(8,128)S(1)} %shard_map.114), channel_id=1, source_target_pairs={{0,1},{1,0},{2,3},{3,2},{4,5},{5,4},{6,7},{7,6},{8,9},{9,8},{10,11... | collective-permute-start | bytes 49160 | tf_op jit(solution)/shard_map/ppermute | solution.py:716
  110.4 4.2 %collective-permute-start.8 = (f32[16,256]{1,0:T(8,128)S(1)}, f32[16,256]{1,0:T(8,128)S(1)}, u32[]{:S(2)}, u32[]{:S(2)}) collective-permute-start(f32[16,256]{1,0:T(8,128)S(1)} %add.38.own_ref), channel_id=1, source_target_pairs={{0,6},{1,7},{2,4},{3,5},{4,2},{5,3},{6,0},{7,1},{8,14},{9,15},{10,... | collective-permute-start | bytes 49160 | tf_op jit(solution)/shard_map/ppermute | solution.py:728
  111.4 4.1 %collective-permute-start.7 = (f32[16,256]{1,0:T(8,128)S(1)}, f32[16,256]{1,0:T(8,128)S(1)}, u32[]{:S(2)}, u32[]{:S(2)}) collective-permute-start(f32[16,256]{1,0:T(8,128)S(1)} %add.38.own_ref), channel_id=1, source_target_pairs={{0,4},{1,5},{2,6},{3,7},{4,0},{5,1},{6,2},{7,3},{8,12},{9,13},{10,... | collective-permute-start | bytes 49160 | tf_op jit(solution)/shard_map/ppermute | solution.py:728
  112.2 3.4 %collective-permute-start.6 = (f32[16,256]{1,0:T(8,128)S(1)}, f32[16,256]{1,0:T(8,128)S(1)}, u32[]{:S(2)}, u32[]{:S(2)}) collective-permute-start(f32[16,256]{1,0:T(8,128)S(1)} %add.38.own_ref), channel_id=1, source_target_pairs={{0,2},{1,3},{2,0},{3,1},{4,6},{5,7},{6,4},{7,5},{8,10},{9,11},{10,... | collective-permute-start | bytes 49160 | tf_op jit(solution)/shard_map/ppermute | solution.py:728
  134.3 5.1 %collective-permute-start.9 = (bf16[16,272,128]{2,1,0:T(8,128)(2,1)S(1)}, bf16[16,272,128]{2,1,0:T(8,128)(2,1)S(1)}, u32[]{:S(2)}, u32[]{:S(2)}) collective-permute-start(bf16[16,272,128]{2,1,0:T(8,128)(2,1)S(1)} %get-tuple-element.42), channel_id=1, source_target_pairs={{0,1},{1,0},{2,3},{3,2},{4,5},{5,4},{6,7},{7,6},{8,9},{9,8},{10,11... | collective-permute-start | bytes 3342344 | tf_op jit(solution)/shard_map/ppermute | solution.py:716
  149.9 4.2 %collective-permute-start.15 = (bf16[16,272,128]{2,1,0:T(8,128)(2,1)}, bf16[16,272,128]{2,1,0:T(8,128)(2,1)}, u32[]{:S(2)}, u32[]{:S(2)}) collective-permute-start(bf16[16,272,128]{2,1,0:T(8,128)(2,1)} %get-tuple-element.49), channel_id=1, source_target_pairs={{0,1},{1,0},{2,3},{3,2},{4,5},{5,4},{6,7},{7,6},{8,9},{9,8},{10,11... | collective-permute-start | bytes 3342344 | tf_op jit(solution)/shard_map/ppermute | solution.py:716
  150.4 23.0 %all-to-all-start.3 = ((bf16[16,272,128]{2,1,0:T(8,128)(2,1)}), bf16[16,272,128]{2,1,0:T(8,128)(2,1)S(1)}, u32[]{:S(2)}, u32[]{:S(2)}) async-start(bf16[16,272,128]{2,1,0:T(8,128)(2,1)} %add_convert_fusion.1), calls=%async_computation.3 | async-start | bytes 2228224 | tf_op jit(solution)/shard_map/all_to_all | solution.py:711
  173.4 20.4 %all-to-all-start.4 = ((bf16[16,272,128]{2,1,0:T(8,128)(2,1)}), bf16[16,272,128]{2,1,0:T(8,128)(2,1)S(1)}, u32[]{:S(2)}, u32[]{:S(2)}) async-start(bf16[16,272,128]{2,1,0:T(8,128)(2,1)} %add_convert_fusion), calls=%async_computation.4 | async-start | bytes 2228224 | tf_op jit(solution)/shard_map/all_to_all | solution.py:711
  178.1 29.7 %copy-start.7 = (f32[8,256]{1,0:T(8,128)S(1)}, f32[8,256]{1,0:T(8,128)}, u32[]{:S(2)}) copy-start(f32[8,256]{1,0:T(8,128)} %get-tuple-element.51.member_ref) | copy-start | bytes 24580
  178.1 29.6 %copy-start.8 = (bf16[16,256]{1,0:T(8,128)(2,1)S(1)}, bf16[16,256]{1,0:T(8,128)(2,1)}, u32[]{:S(2)}) copy-start(bf16[16,256]{1,0:T(8,128)(2,1)} %get-tuple-element.50.mine_ref) | copy-start | bytes 24580
  178.2 19.4 %collective-permute-start.12 = (bf16[1,272,128]{2,1,0:T(8,128)(2,1)}, bf16[1,272,128]{2,1,0:T(8,128)(2,1)S(1)}, u32[]{:S(2)}, u32[]{:S(2)}) collective-permute-start(bf16[1,272,128]{2,1,0:T(8,128)(2,1)} %shard_map.117), channel_id=1, source_target_pairs={{0,6},{1,7},{2,4},{3,5},{4,2},{5,3},{6,0},{7,1},{8,14},{9,15},{10,... | collective-permute-start | bytes 208904 | tf_op jit(solution)/shard_map/ppermute | solution.py:728
  180.1 18.0 %collective-permute-start.11 = (bf16[1,272,128]{2,1,0:T(8,128)(2,1)}, bf16[1,272,128]{2,1,0:T(8,128)(2,1)S(1)}, u32[]{:S(2)}, u32[]{:S(2)}) collective-permute-start(bf16[1,272,128]{2,1,0:T(8,128)(2,1)} %shard_map.117), channel_id=1, source_target_pairs={{0,4},{1,5},{2,6},{3,7},{4,0},{5,1},{6,2},{7,3},{8,12},{9,13},{10,... | collective-permute-start | bytes 208904 | tf_op jit(solution)/shard_map/ppermute | solution.py:728
  181.0 17.2 %collective-permute-start.10 = (bf16[1,272,128]{2,1,0:T(8,128)(2,1)}, bf16[1,272,128]{2,1,0:T(8,128)(2,1)S(1)}, u32[]{:S(2)}, u32[]{:S(2)}) collective-permute-start(bf16[1,272,128]{2,1,0:T(8,128)(2,1)} %shard_map.117), channel_id=1, source_target_pairs={{0,2},{1,3},{2,0},{3,1},{4,6},{5,7},{6,4},{7,5},{8,10},{9,11},{10,... | collective-permute-start | bytes 208904 | tf_op jit(solution)/shard_map/ppermute | solution.py:728
  194.8 7.0 %collective-permute-start.18 = (bf16[1,272,128]{2,1,0:T(8,128)(2,1)}, bf16[1,272,128]{2,1,0:T(8,128)(2,1)S(1)}, u32[]{:S(2)}, u32[]{:S(2)}) collective-permute-start(bf16[1,272,128]{2,1,0:T(8,128)(2,1)} %shard_map.123), channel_id=1, source_target_pairs={{0,6},{1,7},{2,4},{3,5},{4,2},{5,3},{6,0},{7,1},{8,14},{9,15},{10,... | collective-permute-start | bytes 208904 | tf_op jit(solution)/shard_map/ppermute | solution.py:728
  196.8 5.0 %collective-permute-start.17 = (bf16[1,272,128]{2,1,0:T(8,128)(2,1)}, bf16[1,272,128]{2,1,0:T(8,128)(2,1)S(1)}, u32[]{:S(2)}, u32[]{:S(2)}) collective-permute-start(bf16[1,272,128]{2,1,0:T(8,128)(2,1)} %shard_map.123), channel_id=1, source_target_pairs={{0,4},{1,5},{2,6},{3,7},{4,0},{5,1},{6,2},{7,3},{8,12},{9,13},{10,... | collective-permute-start | bytes 208904 | tf_op jit(solution)/shard_map/ppermute | solution.py:728
  197.6 4.2 %collective-permute-start.16 = (bf16[1,272,128]{2,1,0:T(8,128)(2,1)}, bf16[1,272,128]{2,1,0:T(8,128)(2,1)S(1)}, u32[]{:S(2)}, u32[]{:S(2)}) collective-permute-start(bf16[1,272,128]{2,1,0:T(8,128)(2,1)} %shard_map.123), channel_id=1, source_target_pairs={{0,2},{1,3},{2,0},{3,1},{4,6},{5,7},{6,4},{7,5},{8,10},{9,11},{10,... | collective-permute-start | bytes 208904 | tf_op jit(solution)/shard_map/ppermute | solution.py:728
  198.2 8.6 %collective-permute-start.13 = (f32[1,272,128]{2,1,0:T(8,128)S(1)}, f32[1,272,128]{2,1,0:T(8,128)S(1)}, u32[]{:S(2)}, u32[]{:S(2)}) collective-permute-start(f32[1,272,128]{2,1,0:T(8,128)S(1)} %add_add_fusion.1.pull_ref), channel_id=1, source_target_pairs={{0,1},{1,0},{2,3},{3,2},{4,5},{5,4},{6,7},{7,6},{8,9},{9,8},{10,11... | collective-permute-start | bytes 417800 | tf_op jit(solution)/shard_map/ppermute | solution.py:716
  202.7 5.0 %collective-permute-start.19 = (f32[1,272,128]{2,1,0:T(8,128)S(1)}, f32[1,272,128]{2,1,0:T(8,128)S(1)}, u32[]{:S(2)}, u32[]{:S(2)}) collective-permute-start(f32[1,272,128]{2,1,0:T(8,128)S(1)} %add_add_fusion.push_ref), channel_id=1, source_target_pairs={{0,1},{1,0},{2,3},{3,2},{4,5},{5,4},{6,7},{7,6},{8,9},{9,8},{10,11... | collective-permute-start | bytes 417800 | tf_op jit(solution)/shard_map/ppermute | solution.py:716
  212.5 23.0 %all-to-all-start.5 = ((bf16[16,144,256]{2,1,0:T(8,128)(2,1)}), bf16[16,144,256]{2,1,0:T(8,128)(2,1)S(1)}, u32[]{:S(2)}, u32[]{:S(2)}) async-start(bf16[16,144,256]{2,1,0:T(8,128)(2,1)} %get-tuple-element.55), calls=%async_computation.5 | async-start | bytes 2359296 | tf_op jit(solution)/shard_map/all_to_all | solution.py:711
  220.3 2.6 collective-permute-start.20
  236.7 14.4 %all-to-all-start.6 = ((bf16[8,128,256]{2,1,0:T(8,128)(2,1)}), bf16[8,128,256]{2,1,0:T(8,128)(2,1)S(1)}, u32[]{:S(2)}, u32[]{:S(2)}) async-start(bf16[8,128,256]{2,1,0:T(8,128)(2,1)} %shard_map.127), calls=%async_computation.6 | async-start | bytes 1048576 | tf_op jit(solution)/shard_map/all_to_all | solution.py:711
  (6 other events, 29.5 us)
Sparse Core Ops, SparseCore 0:
  10.1 60.9 all-gather.2
  80.5 43.3 all-gather.4

commit v5 on v4

--- a/solution.py
+++ b/solution.py
@@ -156,45 +156,38 @@
         store.wait()
 
 
-def weights_body(at_ref, w_in_hbm, w_out_hbm, pack_hbm, pack_ref, sems):
+def weights_body(at_ref, w_in_hbm, w_out_hbm, pack_hbm, w_in_ref, w_out_ref, pack_ref, sems):
     rows, hid = w_in_hbm.shape
-    half = hid // 2
-    bot = w_out_hbm.shape[1]
-    lines = w_out_hbm.shape[0] * bot // half
-    column = pl.multiple_of(at_ref[0] * half, half)
-    pairs = [(w_in_hbm.at[:, pl.ds(column, half)], pack_ref.at[0:rows, :])]
-    for q in range(half // bot):
-        source = w_out_hbm.at[q * lines : (q + 1) * lines, :]
-        pairs.append((source, pack_ref.at[rows : rows + lines, q * bot : (q + 1) * bot]))
-    loads = copies(pairs, sems)
+    block, bot = w_out_hbm.shape
+    half = block // 2
+    loads = copies([(w_in_hbm, w_in_ref), (w_out_hbm, w_out_ref)], sems)
     for load in loads:
         load.start()
+    core = at_ref[0]
+    row = iota((2 * block, block), 0)
+    col = iota((2 * block, block), 1)
+    pick = (row == (col // half) * block + core * half + col % half).astype(f32).astype(bf16)
     for load in loads:
         load.wait()
+    for p in range(hid // (2 * block)):
+        two = w_in_ref[:, p * 2 * block : (p + 1) * 2 * block]
+        pack_ref[0:rows, p * block : (p + 1) * block] = mm(two, pick).astype(bf16)
+    lines = pack_ref.shape[0] - rows
+    for q in range(half // lines):
+        at = pl.multiple_of(core * half + q * lines, lines)
+        pack_ref[rows : rows + lines, q * bot : (q + 1) * bot] = w_out_ref[pl.ds(at, lines), :]
     store = pltpu.make_async_copy(pack_ref, pack_hbm, sems.at[0])
     store.start()
     store.wait()
 
 
-def w_in_loads(w_hbm, w_in_ref, sems):
-    peers = w_hbm.shape[0]
-    rows = w_in_ref.shape[0] // peers
-    return copies([(w_hbm.at[g, 0:rows, :], w_in_ref.at[g * rows : (g + 1) * rows, :]) for g in range(peers)], sems)
-
-
-def w_out_loads(at_ref, w_hbm, w_out_ref, sems):
-    peers = w_hbm.shape[0]
-    bot = w_out_ref.shape[1]
-    quarters = w_hbm.shape[2] // bot
-    lines = w_out_ref.shape[0] // (peers // 2 * quarters)
-    rows = w_hbm.shape[1] - lines
-    pairs = []
-    for i in range(peers // 2):
-        for q in range(quarters):
-            source = w_hbm.at[at_ref[0] * (peers // 2) + i, rows : rows + lines, q * bot : (q + 1) * bot]
-            at = (i * quarters + q) * lines
-            pairs.append((source, w_out_ref.at[at : at + lines, :]))
-    return copies(pairs, sems)
+def w_in_load(w_hbm, w_in_ref, at):
+    return pltpu.make_async_copy(w_hbm.at[:, 0 : w_in_ref.shape[1], :], w_in_ref, at)
+
+
+def w_in_of(w_in_ref, part):
+    peers, rows, _ = w_in_ref.shape
+    return w_in_ref[:, :, part].reshape(peers * rows, part.stop - part.start)
 
 
 def tokens_body(sel_ref, tokens_hbm, rows_hbm, tokens_ref, rows_ref, sems):
@@ -208,24 +201,34 @@
 
 
 def forward_body(
-    at_ref, rows_hbm, w_hbm, hidden_hbm, slope_hbm, feats_ref, w_out_hbm,
-    rows_ref, hidden_ref, slope_ref, w_in_ref, w_out_ref, sems, out_sems, own_sems,
+    rows_hbm, w_hbm, hidden_hbm, slope_hbm, feats_ref, w_out_hbm,
+    rows_ref, hidden_ref, slope_ref, w_in_ref, lines_ref, w_out_ref, own_sems,
 ):
     first = pltpu.make_async_copy(rows_hbm, rows_ref, own_sems.at[0])
     first.start()
-    loads = w_in_loads(w_hbm, w_in_ref, sems) + w_out_loads(at_ref, w_hbm, w_out_ref, out_sems)
+    per, lines = (w_in_ref.shape[1], lines_ref.shape[1])
+    loads = [
+        pltpu.make_async_copy(w_hbm.at[:, per : per + lines, :], lines_ref, own_sems.at[1]),
+        w_in_load(w_hbm, w_in_ref, own_sems.at[2]),
+    ]
     for load in loads:
         load.start()
     first.wait()
-    for load in loads:
-        load.wait()
-    keeps = copies([(w_out_ref, w_out_hbm)], sems)
+    loads[0].wait()
+    bot = w_out_ref.shape[1]
+    quarters = lines_ref.shape[2] // bot
+    for g in range(lines_ref.shape[0]):
+        for q in range(quarters):
+            at = (g * quarters + q) * lines
+            w_out_ref[at : at + lines, :] = lines_ref[g, :, q * bot : (q + 1) * bot]
+    loads[1].wait()
+    keeps = [pltpu.make_async_copy(w_out_ref, w_out_hbm, own_sems.at[2])]
     for keep in keeps:
         keep.start()
     rows = rows_ref[...]
     feats = jnp.zeros(feats_ref.shape, f32)
     for part in chunks_of(hidden_ref.shape[1]):
-        pre = mm(rows, w_in_ref[:, part])
+        pre = mm(rows, w_in_of(w_in_ref, part))
         cdf = 0.5 * (1.0 + lax.erf(pre * 0.7071067811865476))
         slope_ref[:, part] = cdf + pre * (jnp.exp(-0.5 * pre * pre) * 0.3989422804014327)
         hidden = (pre * cdf).astype(bf16)
@@ -538,11 +541,11 @@
     loads[3].wait()
     for part in chunks_of(hidden_ref.shape[1]):
         out_ref[part, :] = mm(hidden_ref[:, part], grad_feats, TN).astype(bf16)
-    core, level = (at_ref[0], at_ref[1])
+    level = at_ref[1]
     own = pre_ref[:, pl.ds(pl.multiple_of(level * width, width), width)]
     grad_in = mm(rows_ref[...], own, TN).astype(bf16)
     per = grad_in.shape[0] // peers
-    block = out_ref.shape[0] // (peers // 2)
+    block = out_ref.shape[0] // peers
     share = block // 4
     at = iota((EXTRA, CAP), 0)
     rows = jnp.zeros((EXTRA, CAP), f32)
@@ -552,22 +555,20 @@
     store = lambda g: pltpu.make_async_copy(send_ref.at[g], send_hbm.at[g], send_sems.at[g])
     for g in range(peers):
         send_ref[g, 0:per, :] = grad_in[g * per : (g + 1) * per, :]
-        start = pl.multiple_of((g % (peers // 2)) * block + level * share, share)
-        out = out_ref[pl.ds(start, share), :]
-        send_ref[g, per : per + share, :] = jnp.where(core == g // (peers // 2), out, jnp.zeros_like(out))
+        start = pl.multiple_of(g * block + level * share, share)
+        send_ref[g, per : per + share, :] = out_ref[pl.ds(start, share), :]
         send_ref[g, per + share : per + share + EXTRA, :] = rows
         store(g).start()
     pre_out.wait()
     wait_all(peers, store)
 
 
-def backward_rows_body(pre_ref, w_hbm, out_hbm, w_in_ref, out_ref, sems, out_sem):
-    loads = w_in_loads(w_hbm, w_in_ref, sems)
-    for load in loads:
-        load.start()
-    for load in loads:
-        load.wait()
-    out_ref[...] = mm(pre_ref[...], w_in_ref[...], NT).astype(bf16)
+def backward_rows_body(pre_ref, w_hbm, out_hbm, w_in_ref, out_ref, sem, out_sem):
+    load = w_in_load(w_hbm, w_in_ref, sem.at[0])
+    load.start()
+    load.wait()
+    w_in = w_in_of(w_in_ref, slice(0, w_in_ref.shape[2]))
+    out_ref[...] = mm(pre_ref[...], w_in, NT).astype(bf16)
     store = pltpu.make_async_copy(out_ref, out_hbm, out_sem.at[0])
     store.start()
     store.wait()
@@ -601,15 +602,22 @@
     wait_all(send_hbm.shape[0], store)
 
 
-def weight_grads_body(at_ref, parts_ref, grad_in_ref, grad_out_ref):
+def weight_grads_body(parts_ref, grad_in_ref, grad_out_ref):
     peers, lines, width = parts_ref.shape
     per = grad_in_ref.shape[0]
     share = lines - per
-    for t in range(peers):
-        to = ((t % 2) * (peers // 2) + t // 2) * width
-        grad_in_ref[:, to : to + width] = parts_ref[t, 0:per, :].astype(f32)
+    block = 2 * (width // 4)
+    row = iota((2 * width, 2 * width), 0)
+    col = iota((2 * width, 2 * width), 1)
+    half = block // 2
+    from_row = ((col % block) // half) * width + (col // block) * half + col % half
+    order = (row == from_row).astype(f32).astype(bf16)
     for z in range(peers // 2):
-        grad_out_ref[z * share : (z + 1) * share, :] = parts_ref[2 * z + at_ref[2], per:lines, :].astype(f32)
+        both = jnp.concatenate([parts_ref[2 * z, 0:per, :], parts_ref[2 * z + 1, 0:per, :]], axis=1)
+        grad_in_ref[:, z * 2 * width : (z + 1) * 2 * width] = mm(both, order)
+        for c in range(2):
+            at = c * half + z * share
+            grad_out_ref[at : at + share, :] = parts_ref[2 * z + c, per:lines, :].astype(f32)
 
 
 def sem(number):
@@ -776,13 +784,19 @@
     dp, tensor = (lax.axis_size("dp"), lax.axis_size("tensor"))
     per = w_in.shape[0]
     half = hid // 2
-    share = w_out.shape[0] // 4
+    share = w_out.shape[0] // 8
     t = lax.axis_index("tensor").astype(jnp.int32)
-    g = lax.axis_index("dp").astype(jnp.int32)
-    at = jnp.stack([t % 2, t // 2, g // (dp // 2)])
-
-    lines = per + w_out.shape[0] * bot // half
-    (w_pack,) = call(weights_body, [((lines, half), bf16)], (at, w_in, w_out), in_specs=[SMEM, HBM, HBM], out_specs=[HBM], scratch=[pltpu.VMEM((lines, half), bf16), sem(1 + half // bot)])
+    at = jnp.stack([t % 2, t // 2])
+
+    lines = per + w_out.shape[0] // 2 * bot // half
+    (w_pack,) = call(
+        weights_body,
+        [((lines, half), bf16)],
+        (at, w_in, w_out),
+        in_specs=[SMEM, HBM, HBM],
+        out_specs=[HBM],
+        scratch=[pltpu.VMEM(w_in.shape, bf16), pltpu.VMEM(w_out.shape, bf16), pltpu.VMEM((lines, half), bf16), sem(2)],
+    )
     w_all = lax.all_gather(w_pack, "dp", axis=0, tiled=True).reshape(dp, lines, half)
     dma = pltpu.SemaphoreType.DMA
     sems = dma((dp,))
@@ -817,7 +831,6 @@
         ],
     )
     expo, part, live = run_expo(at, teacher_t, packs, others)
-    w_held = [pltpu.VMEM((dim, half), bf16), pltpu.VMEM((half, bot), bf16)]
     (rows,) = call(
         tokens_body,
         [((CAP, dim), bf16)],
@@ -829,17 +842,17 @@
     hidden, slope, feats, w_out_half = call(
         forward_body,
         [((CAP, half), bf16), ((CAP, half), f32), ((CAP, bot), f32), ((half, bot), bf16)],
-        (at, rows, after(w_all, part)),
-        in_specs=[SMEM, HBM, HBM],
+        (rows, after(w_all, part)),
+        in_specs=[HBM, HBM],
         out_specs=[HBM, HBM, VMEM, HBM],
         scratch=[
             pltpu.VMEM((CAP, dim), bf16),
             pltpu.VMEM((CAP, half), bf16),
             pltpu.VMEM((CAP, half), f32),
-            *w_held,
-            sems,
-            sem(2 * dp),
-            sem(2),
+            pltpu.VMEM((dp, per, half), bf16),
+            pltpu.VMEM((dp, share, half), bf16),
+            pltpu.VMEM((half, bot), bf16),
+            sem(3),
         ],
     )
     feats_other = sibling(feats)
@@ -885,7 +898,7 @@
         (grad_pre, w_all),
         in_specs=[VMEM, HBM],
         out_specs=[HBM],
-        scratch=[pltpu.VMEM((dim, half), bf16), pltpu.VMEM((CAP, dim), bf16), sems, sem(1)],
+        scratch=[pltpu.VMEM((dp, per, half), bf16), pltpu.VMEM((CAP, dim), bf16), sem(1), sem(1)],
     )
     pieces = 4
     d_shape = (pieces, tokens.shape[0] // pieces, dim)
@@ -907,9 +920,7 @@
     )
     parts = exchange(sent, "tensor")
     grad_proto = run_columns_grad(expo, raised, scale, got, all_rows, proto_student, norm)
-    grad_in, grad_out = call(
-        weight_grads_body, [((per, hid), f32), ((w_out.shape[0], bot), f32)], (at, parts), in_specs=[SMEM, VMEM]
-    )
+    grad_in, grad_out = call(weight_grads_body, [((per, hid), f32), ((w_out.shape[0], bot), f32)], (parts,))
     return (d_tokens.reshape(tokens.shape), grad_in, grad_out, grad_proto, loss.reshape(masks.shape[0]))
 
 

time: 260 us -> 254 us (0.977)
  waiting for transfers between devices: 65.6 us -> 62 us
  transfers between devices with their start and end apart: 27 -> 27, of which waited for: 14 -> 14; matrix products, arithmetic and copies ran while one was open for 2% -> 2% of each run, Pallas kernels for 18% -> 19%
where the time goes in v5:
time: 254 us; the launch traced here: 253 us
  Pallas kernels  72.1 us (28%)
  waiting for transfers between devices  62 us (24%)
  blocking collectives  50.5 us (20%)
  starting transfers between devices  47.7 us (19%)
  between operations  14.4 us (6%)
  other arithmetic  4.86 us (2%)
    pallas_call x20, Pallas kernels, call(): pl.pallas_call(body, out_shape=outs, in_specs=in_specs, out_specs=tuple(s...  72.1 us
    all_to_all x3, blocking collectives, exchange(): return lax.all_to_all(x, axis, split_axis=0, concat_axis=0, tiled=True)  50.5 us
    all_to_all x4, waiting for transfers between devices, exchange(): return lax.all_to_all(x, axis, split_axis=0, concat_axis=0, tiled=True)  36.2 us
    ppermute x9, starting transfers between devices, sibling(): return lax.ppermute(x, 'tensor', [(i, i ^ 1) for i in range(peers)])  18 us
    all_to_all x4, starting transfers between devices, exchange(): return lax.all_to_all(x, axis, split_axis=0, concat_axis=0, tiled=True)  16.4 us
    ppermute x12, starting transfers between devices, levels(): return lax.ppermute(x, 'tensor', [(i, i ^ 2 * by) for i in range(peers)])  13.2 us
    all_gather x1, waiting for transfers between devices, parts_of(): lax.all_gather(w_pack, 'dp', axis=0, tiled=True).reshape(dp, lines, half)  12 us
    ppermute x9, waiting for transfers between devices, sibling(): return lax.ppermute(x, 'tensor', [(i, i ^ 1) for i in range(peers)])  8.35 us
  transfers between devices with their start and end apart: 27, of which 14 were waited for; matrix products, arithmetic and copies ran while one was open for 2% of the time, Pallas kernels for 19%

profile of v5, /device:TPU:1, one launch (start us, length us, event | category | flops | bytes accessed | tf_op | source)
XLA Modules:
  0.0 253.5 jit_solution(6138486788298368226)
XLA Ops:
  7.3 2.5 shard_map.119
  10.6 2.4 shard_map.111
  13.0 28.7 %all_to_all.35.own_hbm = bf16[16,144,256]{2,1,0:T(8,128)(2,1)S(1)} all-to-all(bf16[16,144,256]{2,1,0:T(8,128)(2,1)} %get-tuple-element.36), channel_id=1, replica_groups=mesh['dp'=16,'tensor'=8] {'dp'}, dimensions={0} | all-to-all | bytes 2359296 | tf_op jit(solution)/shard_map/all_to_all | solution.py:719
  41.7 2.2 collective-permute-start
  45.5 3.8 %shard_map.118.rows_hbm = bf16[256,1536]{1,0:T(8,128)(2,1)} custom-call(bf16[256,1024]{1,0:T(8,128)(2,1)S(1)} %get-tuple-element.44.sel_ref, bf16[1024,1536]{1,0:T(8,128)(2,1)} %tokens_hbm.1), custom_call_target="tpu_custom_call" | custom-call | tf_op jit(solution)/shard_map/pallas_call | solution.py:37
  49.3 7.8 %shard_map.112 = (bf16[16,1024,256]{2,1,0:T(8,128)(2,1)}, f32[16,256]{1,0:T(8,128)S(1)}, f32[16,256]{1,0:T(8,128)S(1)}) custom-call(s32[2]{0:T(128)S(1)} %pad_add_fusion.at_ref, bf16[1024,256]{1,0:T(8,128)(2,1)} %get-tuple-element.35.cols_hbm, bf16[16,144,256]{2,1,0:T(8,128)(2,1)S(1)} %all_to_all.35.own_hbm, ...), custom_call_target="tpu_custom_call" | custom-call | tf_op jit(solution)/shard_map/pallas_call | solution.py:37
  57.1 12.0 %all-gather.3.cloned.1.call-done = bf16[1792,1024]{1,0:T(8,128)(2,1)} async-done(((bf16[112,1024]{1,0:T(8,128)(2,1)}), bf16[1792,1024]{1,0:T(8,128)(2,1)}) %all-gather.3.cloned.1.call-update) | async-done | bytes 3670032 | tf_op jit(solution)/shard_map/all_gather | solution.py:800
  69.1 5.2 %shard_map.120 = (bf16[256,1024]{1,0:T(8,128)(2,1)}, f32[256,1024]{1,0:T(8,128)}, f32[256,256]{1,0:T(8,128)S(1)}, bf16[1024,256]{1,0:T(8,128)(2,1)}) custom-call(bf16[256,1536]{1,0:T(8,128)(2,1)} %shard_map.118.rows_hbm, bf16[16,112,1024]{2,1,0:T(8,128)(2,1)} %bitcast.6), custom_call_target="tpu_custom_call" | custom-call | tf_op jit(solution)/shard_map/pallas_call | solution.py:37
  78.8 2.7 %collective-permute-start.4 = (f32[16,256]{1,0:T(8,128)S(1)}, f32[16,256]{1,0:T(8,128)S(1)}, u32[]{:S(2)}, u32[]{:S(2)}) collective-permute-start(f32[16,256]{1,0:T(8,128)S(1)} %add.36.own_ref), channel_id=1, source_target_pairs={{0,6},{1,7},{2,4},{3,5},{4,2},{5,3},{6,0},{7,1},{8,14},{9,15},{10,... | collective-permute-start | bytes 49160 | tf_op jit(solution)/shard_map/ppermute | solution.py:736
  82.6 3.0 %collective-permute-done.3.far_ref = f32[16,256]{1,0:T(8,128)S(1)} collective-permute-done((f32[16,256]{1,0:T(8,128)S(1)}, f32[16,256]{1,0:T(8,128)S(1)}, u32[]{:S(2)}, u32[]{:S(2)}) %collective-permute-start.3) | collective-permute-done | bytes 16416 | tf_op jit(solution)/shard_map/ppermute | solution.py:736
  85.6 11.4 %all_to_all.36.parts_ref = bf16[16,16,256]{2,1,0:T(8,128)(2,1)S(1)} all-to-all(bf16[16,16,256]{2,1,0:T(8,128)(2,1)S(1)} %shard_map.113), channel_id=1, replica_groups=mesh['dp'=16,'tensor'=8] {'dp'}, dimensions={0} | all-to-all | bytes 262144 | tf_op jit(solution)/shard_map/all_to_all | solution.py:719
  97.0 6.0 %shard_map.114 = f32[16,256]{1,0:T(8,128)S(1)} custom-call(bf16[16,1024,256]{2,1,0:T(8,128)(2,1)} %get-tuple-element.37.expo_hbm, bf16[16,16,256]{2,1,0:T(8,128)(2,1)S(1)} %all_to_all.36.parts_ref, f32[16,256]{1,0:T(8,128)S(1)} %get-tuple-element.39.live_ref), custom_call_target="tpu_custom_call" | custom-call | tf_op jit(solution)/shard_map/pallas_call | solution.py:37
  103.0 2.9 %collective-permute-start.5 = (f32[16,256]{1,0:T(8,128)S(1)}, f32[16,256]{1,0:T(8,128)S(1)}, u32[]{:S(2)}, u32[]{:S(2)}) collective-permute-start(f32[16,256]{1,0:T(8,128)S(1)} %shard_map.114), channel_id=1, source_target_pairs={{0,1},{1,0},{2,3},{3,2},{4,5},{5,4},{6,7},{7,6},{8,9},{9,8},{10,11... | collective-permute-start | bytes 49160 | tf_op jit(solution)/shard_map/ppermute | solution.py:724
  112.0 10.4 %all_to_all.37.parts_ref = bf16[16,16,256]{2,1,0:T(8,128)(2,1)S(1)} all-to-all(bf16[16,16,256]{2,1,0:T(8,128)(2,1)S(1)} %shard_map.115), channel_id=1, replica_groups=mesh['dp'=16,'tensor'=8] {'dp'}, dimensions={0} | all-to-all | bytes 262144 | tf_op jit(solution)/shard_map/all_to_all | solution.py:719
  122.4 8.2 %shard_map.116 = (bf16[16,272,128]{2,1,0:T(8,128)(2,1)S(1)}, bf16[16,272,128]{2,1,0:T(8,128)(2,1)S(1)}, f32[1024,128]{1,0:T(8,128)}) custom-call(s32[2]{0:T(128)S(1)} %pad_add_fusion.at_ref, bf16[16,1024,256]{2,1,0:T(8,128)(2,1)} %get-tuple-element.37.expo_hbm, bf16[16,16,256]{2,1,0:T(8,128)(2,1)S(1)} %all_to_all.37.parts_ref, ...), custom_call_target="tpu_custom_call" | custom-call | tf_op jit(solution)/shard_map/pallas_call | solution.py:37
  130.6 2.7 %collective-permute-start.9 = (bf16[16,272,128]{2,1,0:T(8,128)(2,1)S(1)}, bf16[16,272,128]{2,1,0:T(8,128)(2,1)S(1)}, u32[]{:S(2)}, u32[]{:S(2)}) collective-permute-start(bf16[16,272,128]{2,1,0:T(8,128)(2,1)S(1)} %get-tuple-element.42), channel_id=1, source_target_pairs={{0,1},{1,0},{2,3},{3,2},{4,5},{5,4},{6,7},{7,6},{8,9},{9,8},{10,11... | collective-permute-start | bytes 3342344 | tf_op jit(solution)/shard_map/ppermute | solution.py:724
  133.3 2.4 collective-permute-done.9
  137.0 9.2 %shard_map.122 = (bf16[16,1024,256]{2,1,0:T(8,128)(2,1)}, bf16[16,272,128]{2,1,0:T(8,128)(2,1)S(1)}, bf16[16,272,128]{2,1,0:T(8,128)(2,1)}) custom-call(s32[2]{0:T(128)S(1)} %pad_add_fusion.at_ref, bf16[1024,256]{1,0:T(8,128)(2,1)S(1)} %copy-done.6, bf16[256,1024]{1,0:T(8,128)(2,1)S(1)} %copy-done.2, bf16[16,256,256]{2,1,0:T(8,128)(2,1)} %bitcast.8), custom_call_target="tpu_custom_call" | custom-call | tf_op jit(solution)/shard_map/pallas_call | solution.py:37
  146.6 3.7 %all-to-all-start.3 = ((bf16[16,272,128]{2,1,0:T(8,128)(2,1)}), bf16[16,272,128]{2,1,0:T(8,128)(2,1)S(1)}, u32[]{:S(2)}, u32[]{:S(2)}) async-start(bf16[16,272,128]{2,1,0:T(8,128)(2,1)} %add_convert_fusion.1), calls=%async_computation.3 | async-start | bytes 2228224 | tf_op jit(solution)/shard_map/all_to_all | solution.py:719
  150.4 2.5 %add_convert_fusion = bf16[16,272,128]{2,1,0:T(8,128)(2,1)} fusion(bf16[16,272,128]{2,1,0:T(8,128)(2,1)} %collective-permute-done.15, bf16[16,272,128]{2,1,0:T(8,128)(2,1)S(1)} %get-tuple-element.48), kind=kLoop, calls=%fused_computation | loop fusion | flops 2228224 | bytes 3342336 | tf_op jit(solution)/shard_map/convert_element_type | solution.py:746
  152.9 16.8 %all-to-all-done.3.parts_hbm = bf16[16,272,128]{2,1,0:T(8,128)(2,1)S(1)} async-done(((bf16[16,272,128]{2,1,0:T(8,128)(2,1)}), bf16[16,272,128]{2,1,0:T(8,128)(2,1)S(1)}, u32[]{:S(2)}, u32[]{:S(2)}) %all-to-all-start.3) | async-done | bytes 1114144 | tf_op jit(solution)/shard_map/all_to_all | solution.py:719
  169.7 3.7 %all-to-all-start.4 = ((bf16[16,272,128]{2,1,0:T(8,128)(2,1)}), bf16[16,272,128]{2,1,0:T(8,128)(2,1)S(1)}, u32[]{:S(2)}, u32[]{:S(2)}) async-start(bf16[16,272,128]{2,1,0:T(8,128)(2,1)} %add_convert_fusion), calls=%async_computation.4 | async-start | bytes 2228224 | tf_op jit(solution)/shard_map/all_to_all | solution.py:719
  177.8 12.3 %all-to-all-done.4.parts_hbm = bf16[16,272,128]{2,1,0:T(8,128)(2,1)S(1)} async-done(((bf16[16,272,128]{2,1,0:T(8,128)(2,1)}), bf16[16,272,128]{2,1,0:T(8,128)(2,1)S(1)}, u32[]{:S(2)}, u32[]{:S(2)}) %all-to-all-start.4) | async-done | bytes 1114144 | tf_op jit(solution)/shard_map/all_to_all | solution.py:719
  194.5 3.6 %collective-permute-start.13 = (f32[1,272,128]{2,1,0:T(8,128)S(1)}, f32[1,272,128]{2,1,0:T(8,128)S(1)}, u32[]{:S(2)}, u32[]{:S(2)}) collective-permute-start(f32[1,272,128]{2,1,0:T(8,128)S(1)} %add_add_fusion.1.pull_ref), channel_id=1, source_target_pairs={{0,1},{1,0},{2,3},{3,2},{4,5},{5,4},{6,7},{7,6},{8,9},{9,8},{10,11... | collective-permute-start | bytes 417800 | tf_op jit(solution)/shard_map/ppermute | solution.py:724
  199.0 3.9 %collective-permute-start.19 = (f32[1,272,128]{2,1,0:T(8,128)S(1)}, f32[1,272,128]{2,1,0:T(8,128)S(1)}, u32[]{:S(2)}, u32[]{:S(2)}) collective-permute-start(f32[1,272,128]{2,1,0:T(8,128)S(1)} %add_add_fusion.push_ref), channel_id=1, source_target_pairs={{0,1},{1,0},{2,3},{3,2},{4,5},{5,4},{6,7},{7,6},{8,9},{9,8},{10,11... | collective-permute-start | bytes 417800 | tf_op jit(solution)/shard_map/ppermute | solution.py:724
  203.9 4.6 %shard_map.124 = (bf16[16,128,256]{2,1,0:T(8,128)(2,1)}, bf16[256,1024]{1,0:T(8,128)(2,1)}, f32[1,4]{1,0:T(1,128)}) custom-call(s32[2]{0:T(128)S(1)} %pad_add_fusion.at_ref, f32[1,272,128]{2,1,0:T(8,128)S(1)} %add_add_fusion.1.pull_ref, f32[1,272,128]{2,1,0:T(8,128)S(1)} %collective-permute-done.13.pull_other_ref, f32[1,272,128]{2,1,0:T(8,128)S(1)} %add_add_fusion.push_ref, ...), custom_call_target="tpu_custom_call" | custom-call | tf_op jit(solution)/shard_map/pallas_call | solution.py:37
  208.6 3.8 %all-to-all-start.5 = ((bf16[16,128,256]{2,1,0:T(8,128)(2,1)}), bf16[16,128,256]{2,1,0:T(8,128)(2,1)S(1)}, u32[]{:S(2)}, u32[]{:S(2)}) async-start(bf16[16,128,256]{2,1,0:T(8,128)(2,1)} %get-tuple-element.55), calls=%async_computation.5 | async-start | bytes 2097152 | tf_op jit(solution)/shard_map/all_to_all | solution.py:719
  212.4 3.8 %shard_map.125.rows_ref = bf16[256,1536]{1,0:T(8,128)(2,1)} custom-call(bf16[256,1024]{1,0:T(8,128)(2,1)S(1)} %copy-done.3, bf16[16,112,1024]{2,1,0:T(8,128)(2,1)} %bitcast.7), custom_call_target="tpu_custom_call" | custom-call | tf_op jit(solution)/shard_map/pallas_call | solution.py:37
  216.7 2.1 collective-permute-done.20.other_ref
  222.1 7.2 %all-to-all-done.5.got_hbm = bf16[16,128,256]{2,1,0:T(8,128)(2,1)S(1)} async-done(((bf16[16,128,256]{2,1,0:T(8,128)(2,1)}), bf16[16,128,256]{2,1,0:T(8,128)(2,1)S(1)}, u32[]{:S(2)}, u32[]{:S(2)}) %all-to-all-start.5) | async-done | bytes 1048608 | tf_op jit(solution)/shard_map/all_to_all | solution.py:719
  230.7 5.2 %all-to-all-start.6 = ((bf16[8,112,256]{2,1,0:T(8,128)(2,1)}), bf16[8,112,256]{2,1,0:T(8,128)(2,1)S(1)}, u32[]{:S(2)}, u32[]{:S(2)}) async-start(bf16[8,112,256]{2,1,0:T(8,128)(2,1)} %shard_map.127), calls=%async_computation.6 | async-start | bytes 917504 | tf_op jit(solution)/shard_map/all_to_all | solution.py:719
  235.9 9.3 %shard_map.129 = f32[256,1024]{1,0:T(8,128)} custom-call(bf16[16,1024,256]{2,1,0:T(8,128)(2,1)} %get-tuple-element.37.expo_hbm, bf16[16,1024,256]{2,1,0:T(8,128)(2,1)} %get-tuple-element.61.raised_hbm, f32[1024,128]{1,0:T(8,128)} %get-tuple-element.62.scale_hbm, bf16[16,128,256]{2,1,0:T(8,128)(2,1)S(1)} %all-to-all-done.5.got_hbm, ...), custom_call_target="tpu_custom_call" | custom-call | tf_op jit(solution)/shard_map/pallas_call | solution.py:37
  (76 shorter events, 33.0 us)
Async XLA Ops:
  7.2 61.9 %all-gather.3.cloned.1.call-start = ((), (), s32[]{:S(2)}) async-start(), calls=%async_computation.7 | async-start | bytes 3899392 | tf_op jit(solution)/shard_map/all_gather | solution.py:800
  9.9 127.1 %all-gather.5.cloned.1.call-start = ((), (), s32[]{:S(2)}) async-start(), calls=%async_computation.8 | async-start | bytes 2228224 | tf_op jit(solution)/shard_map/all_gather | solution.py:860
  13.0 30.9 %copy-start.1 = (bf16[256,1024]{1,0:T(8,128)(2,1)S(1)}, bf16[256,1024]{1,0:T(8,128)(2,1)}, u32[]{:S(2)}) copy-start(bf16[256,1024]{1,0:T(8,128)(2,1)} %proto_hbm.1) | copy-start | bytes 1572868
  13.0 30.9 %copy-start.5 = (bf16[256,1024]{1,0:T(8,128)(2,1)S(1)}, bf16[256,1024]{1,0:T(8,128)(2,1)}, u32[]{:S(2)}) copy-start(bf16[256,1024]{1,0:T(8,128)(2,1)} %teacher_ref.1) | copy-start | bytes 1572868
  41.7 7.5 %collective-permute-start = (bf16[16,144,256]{2,1,0:T(8,128)(2,1)S(1)}, bf16[16,144,256]{2,1,0:T(8,128)(2,1)S(1)}, u32[]{:S(2)}, u32[]{:S(2)}) collective-permute-start(bf16[16,144,256]{2,1,0:T(8,128)(2,1)S(1)} %all_to_all.35.own_hbm), channel_id=1, source_target_pairs={{0,1},{1,0},{2,3},{3,2},{4,5},{5,4},{6,7},{7,6},{8,9},{9,8},{10,11... | collective-permute-start | bytes 3538952 | tf_op jit(solution)/shard_map/ppermute | solution.py:724
  74.3 2.4 collective-permute-start.14
  77.5 1.3 collective-permute-start.1
  78.8 3.8 %collective-permute-start.4 = (f32[16,256]{1,0:T(8,128)S(1)}, f32[16,256]{1,0:T(8,128)S(1)}, u32[]{:S(2)}, u32[]{:S(2)}) collective-permute-start(f32[16,256]{1,0:T(8,128)S(1)} %add.36.own_ref), channel_id=1, source_target_pairs={{0,6},{1,7},{2,4},{3,5},{4,2},{5,3},{6,0},{7,1},{8,14},{9,15},{10,... | collective-permute-start | bytes 49160 | tf_op jit(solution)/shard_map/ppermute | solution.py:736
  81.5 4.1 %collective-permute-start.3 = (f32[16,256]{1,0:T(8,128)S(1)}, f32[16,256]{1,0:T(8,128)S(1)}, u32[]{:S(2)}, u32[]{:S(2)}) collective-permute-start(f32[16,256]{1,0:T(8,128)S(1)} %add.36.own_ref), channel_id=1, source_target_pairs={{0,4},{1,5},{2,6},{3,7},{4,0},{5,1},{6,2},{7,3},{8,12},{9,13},{10,... | collective-permute-start | bytes 49160 | tf_op jit(solution)/shard_map/ppermute | solution.py:736
  81.9 3.7 %collective-permute-start.2 = (f32[16,256]{1,0:T(8,128)S(1)}, f32[16,256]{1,0:T(8,128)S(1)}, u32[]{:S(2)}, u32[]{:S(2)}) collective-permute-start(f32[16,256]{1,0:T(8,128)S(1)} %add.36.own_ref), channel_id=1, source_target_pairs={{0,2},{1,3},{2,0},{3,1},{4,6},{5,7},{6,4},{7,5},{8,10},{9,11},{10,... | collective-permute-start | bytes 49160 | tf_op jit(solution)/shard_map/ppermute | solution.py:736
  97.0 25.4 %copy-start.2 = (bf16[256,1024]{1,0:T(8,128)(2,1)S(1)}, bf16[256,1024]{1,0:T(8,128)(2,1)}, u32[]{:S(2)}) copy-start(bf16[256,1024]{1,0:T(8,128)(2,1)} %get-tuple-element.40.cols_ref) | copy-start | bytes 1572868
  103.0 3.8 %collective-permute-start.5 = (f32[16,256]{1,0:T(8,128)S(1)}, f32[16,256]{1,0:T(8,128)S(1)}, u32[]{:S(2)}, u32[]{:S(2)}) collective-permute-start(f32[16,256]{1,0:T(8,128)S(1)} %shard_map.114), channel_id=1, source_target_pairs={{0,1},{1,0},{2,3},{3,2},{4,5},{5,4},{6,7},{7,6},{8,9},{9,8},{10,11... | collective-permute-start | bytes 49160 | tf_op jit(solution)/shard_map/ppermute | solution.py:724
  106.8 4.2 %collective-permute-start.8 = (f32[16,256]{1,0:T(8,128)S(1)}, f32[16,256]{1,0:T(8,128)S(1)}, u32[]{:S(2)}, u32[]{:S(2)}) collective-permute-start(f32[16,256]{1,0:T(8,128)S(1)} %add.37.own_ref), channel_id=1, source_target_pairs={{0,6},{1,7},{2,4},{3,5},{4,2},{5,3},{6,0},{7,1},{8,14},{9,15},{10,... | collective-permute-start | bytes 49160 | tf_op jit(solution)/shard_map/ppermute | solution.py:736
  107.8 4.1 %collective-permute-start.7 = (f32[16,256]{1,0:T(8,128)S(1)}, f32[16,256]{1,0:T(8,128)S(1)}, u32[]{:S(2)}, u32[]{:S(2)}) collective-permute-start(f32[16,256]{1,0:T(8,128)S(1)} %add.37.own_ref), channel_id=1, source_target_pairs={{0,4},{1,5},{2,6},{3,7},{4,0},{5,1},{6,2},{7,3},{8,12},{9,13},{10,... | collective-permute-start | bytes 49160 | tf_op jit(solution)/shard_map/ppermute | solution.py:736
  108.5 3.4 %collective-permute-start.6 = (f32[16,256]{1,0:T(8,128)S(1)}, f32[16,256]{1,0:T(8,128)S(1)}, u32[]{:S(2)}, u32[]{:S(2)}) collective-permute-start(f32[16,256]{1,0:T(8,128)S(1)} %add.37.own_ref), channel_id=1, source_target_pairs={{0,2},{1,3},{2,0},{3,1},{4,6},{5,7},{6,4},{7,5},{8,10},{9,11},{10,... | collective-permute-start | bytes 49160 | tf_op jit(solution)/shard_map/ppermute | solution.py:736
  130.6 5.1 %collective-permute-start.9 = (bf16[16,272,128]{2,1,0:T(8,128)(2,1)S(1)}, bf16[16,272,128]{2,1,0:T(8,128)(2,1)S(1)}, u32[]{:S(2)}, u32[]{:S(2)}) collective-permute-start(bf16[16,272,128]{2,1,0:T(8,128)(2,1)S(1)} %get-tuple-element.42), channel_id=1, source_target_pairs={{0,1},{1,0},{2,3},{3,2},{4,5},{5,4},{6,7},{7,6},{8,9},{9,8},{10,11... | collective-permute-start | bytes 3342344 | tf_op jit(solution)/shard_map/ppermute | solution.py:724
  146.2 4.2 %collective-permute-start.15 = (bf16[16,272,128]{2,1,0:T(8,128)(2,1)}, bf16[16,272,128]{2,1,0:T(8,128)(2,1)}, u32[]{:S(2)}, u32[]{:S(2)}) collective-permute-start(bf16[16,272,128]{2,1,0:T(8,128)(2,1)} %get-tuple-element.49), channel_id=1, source_target_pairs={{0,1},{1,0},{2,3},{3,2},{4,5},{5,4},{6,7},{7,6},{8,9},{9,8},{10,11... | collective-permute-start | bytes 3342344 | tf_op jit(solution)/shard_map/ppermute | solution.py:724
  146.6 23.0 %all-to-all-start.3 = ((bf16[16,272,128]{2,1,0:T(8,128)(2,1)}), bf16[16,272,128]{2,1,0:T(8,128)(2,1)S(1)}, u32[]{:S(2)}, u32[]{:S(2)}) async-start(bf16[16,272,128]{2,1,0:T(8,128)(2,1)} %add_convert_fusion.1), calls=%async_computation.3 | async-start | bytes 2228224 | tf_op jit(solution)/shard_map/all_to_all | solution.py:719
  169.7 20.4 %all-to-all-start.4 = ((bf16[16,272,128]{2,1,0:T(8,128)(2,1)}), bf16[16,272,128]{2,1,0:T(8,128)(2,1)S(1)}, u32[]{:S(2)}, u32[]{:S(2)}) async-start(bf16[16,272,128]{2,1,0:T(8,128)(2,1)} %add_convert_fusion), calls=%async_computation.4 | async-start | bytes 2228224 | tf_op jit(solution)/shard_map/all_to_all | solution.py:719
  174.4 29.5 %copy-start.7 = (f32[8,256]{1,0:T(8,128)S(1)}, f32[8,256]{1,0:T(8,128)}, u32[]{:S(2)}) copy-start(f32[8,256]{1,0:T(8,128)} %get-tuple-element.51.member_ref) | copy-start | bytes 24580
  174.4 29.5 %copy-start.8 = (bf16[16,256]{1,0:T(8,128)(2,1)S(1)}, bf16[16,256]{1,0:T(8,128)(2,1)}, u32[]{:S(2)}) copy-start(bf16[16,256]{1,0:T(8,128)(2,1)} %get-tuple-element.50.mine_ref) | copy-start | bytes 24580
  174.4 19.4 %collective-permute-start.12 = (bf16[1,272,128]{2,1,0:T(8,128)(2,1)}, bf16[1,272,128]{2,1,0:T(8,128)(2,1)S(1)}, u32[]{:S(2)}, u32[]{:S(2)}) collective-permute-start(bf16[1,272,128]{2,1,0:T(8,128)(2,1)} %shard_map.117), channel_id=1, source_target_pairs={{0,6},{1,7},{2,4},{3,5},{4,2},{5,3},{6,0},{7,1},{8,14},{9,15},{10,... | collective-permute-start | bytes 208904 | tf_op jit(solution)/shard_map/ppermute | solution.py:736
  176.3 18.1 %collective-permute-start.11 = (bf16[1,272,128]{2,1,0:T(8,128)(2,1)}, bf16[1,272,128]{2,1,0:T(8,128)(2,1)S(1)}, u32[]{:S(2)}, u32[]{:S(2)}) collective-permute-start(bf16[1,272,128]{2,1,0:T(8,128)(2,1)} %shard_map.117), channel_id=1, source_target_pairs={{0,4},{1,5},{2,6},{3,7},{4,0},{5,1},{6,2},{7,3},{8,12},{9,13},{10,... | collective-permute-start | bytes 208904 | tf_op jit(solution)/shard_map/ppermute | solution.py:736
  177.2 17.2 %collective-permute-start.10 = (bf16[1,272,128]{2,1,0:T(8,128)(2,1)}, bf16[1,272,128]{2,1,0:T(8,128)(2,1)S(1)}, u32[]{:S(2)}, u32[]{:S(2)}) collective-permute-start(bf16[1,272,128]{2,1,0:T(8,128)(2,1)} %shard_map.117), channel_id=1, source_target_pairs={{0,2},{1,3},{2,0},{3,1},{4,6},{5,7},{6,4},{7,5},{8,10},{9,11},{10,... | collective-permute-start | bytes 208904 | tf_op jit(solution)/shard_map/ppermute | solution.py:736
  191.1 7.0 %collective-permute-start.18 = (bf16[1,272,128]{2,1,0:T(8,128)(2,1)}, bf16[1,272,128]{2,1,0:T(8,128)(2,1)S(1)}, u32[]{:S(2)}, u32[]{:S(2)}) collective-permute-start(bf16[1,272,128]{2,1,0:T(8,128)(2,1)} %shard_map.123), channel_id=1, source_target_pairs={{0,6},{1,7},{2,4},{3,5},{4,2},{5,3},{6,0},{7,1},{8,14},{9,15},{10,... | collective-permute-start | bytes 208904 | tf_op jit(solution)/shard_map/ppermute | solution.py:736
  192.9 5.2 %collective-permute-start.17 = (bf16[1,272,128]{2,1,0:T(8,128)(2,1)}, bf16[1,272,128]{2,1,0:T(8,128)(2,1)S(1)}, u32[]{:S(2)}, u32[]{:S(2)}) collective-permute-start(bf16[1,272,128]{2,1,0:T(8,128)(2,1)} %shard_map.123), channel_id=1, source_target_pairs={{0,4},{1,5},{2,6},{3,7},{4,0},{5,1},{6,2},{7,3},{8,12},{9,13},{10,... | collective-permute-start | bytes 208904 | tf_op jit(solution)/shard_map/ppermute | solution.py:736
  193.8 4.3 %collective-permute-start.16 = (bf16[1,272,128]{2,1,0:T(8,128)(2,1)}, bf16[1,272,128]{2,1,0:T(8,128)(2,1)S(1)}, u32[]{:S(2)}, u32[]{:S(2)}) collective-permute-start(bf16[1,272,128]{2,1,0:T(8,128)(2,1)} %shard_map.123), channel_id=1, source_target_pairs={{0,2},{1,3},{2,0},{3,1},{4,6},{5,7},{6,4},{7,5},{8,10},{9,11},{10,... | collective-permute-start | bytes 208904 | tf_op jit(solution)/shard_map/ppermute | solution.py:736
  194.5 8.5 %collective-permute-start.13 = (f32[1,272,128]{2,1,0:T(8,128)S(1)}, f32[1,272,128]{2,1,0:T(8,128)S(1)}, u32[]{:S(2)}, u32[]{:S(2)}) collective-permute-start(f32[1,272,128]{2,1,0:T(8,128)S(1)} %add_add_fusion.1.pull_ref), channel_id=1, source_target_pairs={{0,1},{1,0},{2,3},{3,2},{4,5},{5,4},{6,7},{7,6},{8,9},{9,8},{10,11... | collective-permute-start | bytes 417800 | tf_op jit(solution)/shard_map/ppermute | solution.py:724
  199.0 4.9 %collective-permute-start.19 = (f32[1,272,128]{2,1,0:T(8,128)S(1)}, f32[1,272,128]{2,1,0:T(8,128)S(1)}, u32[]{:S(2)}, u32[]{:S(2)}) collective-permute-start(f32[1,272,128]{2,1,0:T(8,128)S(1)} %add_add_fusion.push_ref), channel_id=1, source_target_pairs={{0,1},{1,0},{2,3},{3,2},{4,5},{5,4},{6,7},{7,6},{8,9},{9,8},{10,11... | collective-permute-start | bytes 417800 | tf_op jit(solution)/shard_map/ppermute | solution.py:724
  208.6 20.7 %all-to-all-start.5 = ((bf16[16,128,256]{2,1,0:T(8,128)(2,1)}), bf16[16,128,256]{2,1,0:T(8,128)(2,1)S(1)}, u32[]{:S(2)}, u32[]{:S(2)}) async-start(bf16[16,128,256]{2,1,0:T(8,128)(2,1)} %get-tuple-element.55), calls=%async_computation.5 | async-start | bytes 2097152 | tf_op jit(solution)/shard_map/all_to_all | solution.py:719
  216.2 2.6 %collective-permute-start.20 = (bf16[256,1536]{1,0:T(8,128)(2,1)}, bf16[256,1536]{1,0:T(8,128)(2,1)S(1)}, u32[]{:S(2)}, u32[]{:S(2)}) collective-permute-start(bf16[256,1536]{1,0:T(8,128)(2,1)} %shard_map.125.rows_ref), channel_id=1, source_target_pairs={{0,1},{1,0},{2,3},{3,2},{4,5},{5,4},{6,7},{7,6},{8,9},{9,8},{10,11... | collective-permute-start | bytes 2359304 | tf_op jit(solution)/shard_map/ppermute | solution.py:724
  230.7 14.6 %all-to-all-start.6 = ((bf16[8,112,256]{2,1,0:T(8,128)(2,1)}), bf16[8,112,256]{2,1,0:T(8,128)(2,1)S(1)}, u32[]{:S(2)}, u32[]{:S(2)}) async-start(bf16[8,112,256]{2,1,0:T(8,128)(2,1)} %shard_map.127), calls=%async_computation.6 | async-start | bytes 917504 | tf_op jit(solution)/shard_map/all_to_all | solution.py:719
  (6 other events, 29.7 us)
Sparse Core Ops, SparseCore 0:
  10.1 58.8 all-gather.2
  77.6 42.7 all-gather.4

commit v6 on v5

--- a/solution.py
+++ b/solution.py
@@ -21,6 +21,8 @@
 EXTRA = 16
 HALF = CAP // 2
 LINES = CAP + EXTRA
+DEAD = 2.0
+LOG2E = 1.4426950408889634
 
 
 def mm(a, b, dims=None):
@@ -118,15 +120,16 @@
     live = jnp.where(lane < total, 1.0, 0.0)
     picked = mm(sel_ref[...], feats_ref[...])
     scale = lax.rsqrt(jnp.sum(picked * picked, axis=1, keepdims=True) + EPS)
-    unit_ref[...] = (picked * scale).astype(bf16)
+    dead = iota(picked.shape, 0).astype(f32) >= total
+    mark = jnp.where(iota(picked.shape, 1) == 0, DEAD, 0.0)
+    unit_ref[...] = jnp.where(dead, mark, picked * scale).astype(bf16)
     at = iota((EXTRA, CAP), 0)
     tail = jnp.where(at == 0, live, jnp.where(at == 1, weight * GRAD_SCALE, 0.0)).astype(bf16)
     mine_ref[...] = tail
     late = copies([(member_ref, member_hbm), (mine_ref, mine_hbm)], late_sems)
     for copy in late:
         copy.start()
-    pack_ref[0:HALF, :] = unit_ref[pl.ds(pl.multiple_of(at_ref[0] * HALF, HALF), HALF), :]
-    pack_ref[HALF : HALF + EXTRA, :] = tail
+    pack_ref[...] = unit_ref[pl.ds(pl.multiple_of(at_ref[0] * HALF, HALF), HALF), :]
     peers = send_hbm.shape[0]
     make = lambda g: pltpu.make_async_copy(pack_ref, send_hbm.at[g], sems.at[g])
     start_all(peers, make)
@@ -209,8 +212,11 @@
     per, lines = (w_in_ref.shape[1], lines_ref.shape[1])
     loads = [
         pltpu.make_async_copy(w_hbm.at[:, per : per + lines, :], lines_ref, own_sems.at[1]),
-        w_in_load(w_hbm, w_in_ref, own_sems.at[2]),
     ]
+    parts = chunks_of(hidden_ref.shape[1])
+    for i, part in enumerate(parts):
+        source = w_hbm.at[:, 0:per, part]
+        loads.append(pltpu.make_async_copy(source, w_in_ref.at[:, :, part], own_sems.at[2 + i]))
     for load in loads:
         load.start()
     first.wait()
@@ -221,13 +227,13 @@
         for q in range(quarters):
             at = (g * quarters + q) * lines
             w_out_ref[at : at + lines, :] = lines_ref[g, :, q * bot : (q + 1) * bot]
-    loads[1].wait()
-    keeps = [pltpu.make_async_copy(w_out_ref, w_out_hbm, own_sems.at[2])]
+    keeps = [pltpu.make_async_copy(w_out_ref, w_out_hbm, own_sems.at[0])]
     for keep in keeps:
         keep.start()
     rows = rows_ref[...]
     feats = jnp.zeros(feats_ref.shape, f32)
-    for part in chunks_of(hidden_ref.shape[1]):
+    for load, part in zip(loads[1:], parts):
+        load.wait()
         pre = mm(rows, w_in_of(w_in_ref, part))
         cdf = 0.5 * (1.0 + lax.erf(pre * 0.7071067811865476))
         slope_ref[:, part] = cdf + pre * (jnp.exp(-0.5 * pre * pre) * 0.3989422804014327)
@@ -235,7 +241,8 @@
         hidden_ref[:, part] = hidden
         feats = feats + mm(hidden, w_out_ref[part, :])
     feats_ref[...] = feats
-    stores = copies([(hidden_ref, hidden_hbm), (slope_ref, slope_hbm)], own_sems)
+    pairs = [(hidden_ref, hidden_hbm), (slope_ref, slope_hbm)]
+    stores = [pltpu.make_async_copy(a, b, own_sems.at[1 + i]) for i, (a, b) in enumerate(pairs)]
     for store in stores:
         store.start()
     for store in keeps + stores:
@@ -267,35 +274,31 @@
 
 def expo_body(
     at_ref, cols_hbm, own_hbm, other_hbm, expo_hbm, part_ref, live_ref,
-    cols_ref, rows_ref, tail_ref, expo_ref, total_ref, sems, own_sems, other_sems, tail_sems,
+    cols_ref, rows_ref, expo_ref, total_ref, sems, own_sems, other_sems, cols_sem,
 ):
     peers = own_hbm.shape[0]
     width = cols_ref.shape[0]
     core = at_ref[0]
     number = peers // GROUP
-    rows_of = lambda ref, q: ref.at[pl.ds(q * GROUP, GROUP), 0:HALF, :]
     rows_at = lambda q, c: rows_ref.at[pl.ds(q * GROUP, GROUP), c]
-    load_own = lambda q: pltpu.make_async_copy(rows_of(own_hbm, q), rows_at(q, core), own_sems.at[q])
-    load_other = lambda q: pltpu.make_async_copy(rows_of(other_hbm, q), rows_at(q, 1 - core), other_sems.at[q])
-    load_tail = pltpu.make_async_copy(own_hbm.at[:, HALF : HALF + EXTRA, :], tail_ref, tail_sems.at[0])
+    load_own = lambda q: pltpu.make_async_copy(group(own_hbm, q), rows_at(q, core), own_sems.at[q])
+    load_other = lambda q: pltpu.make_async_copy(group(other_hbm, q), rows_at(q, 1 - core), other_sems.at[q])
     store = lambda q: pltpu.make_async_copy(group(expo_ref, q), group(expo_hbm, q), sems.at[q])
-    load_cols = pltpu.make_async_copy(cols_hbm, cols_ref, tail_sems.at[1])
+    load_cols = pltpu.make_async_copy(cols_hbm, cols_ref, cols_sem.at[0])
     load_cols.start()
-    load_tail.start()
     start_all(number, load_own)
     start_all(number, load_other)
     total_ref[...] = jnp.zeros_like(total_ref)
-    load_tail.wait()
+    lead = ((iota((EXTRA, cols_ref.shape[1]), 0) == 0) & (iota((EXTRA, cols_ref.shape[1]), 1) == 0)).astype(f32).astype(bf16)
     load_cols.wait()
 
     def first(g):
         rows = rows_ref[g].reshape(CAP, rows_ref.shape[3])
-        tail = tail_ref[g].astype(f32)
-        live = tail[0:1]
+        live = jnp.where(mm(lead, rows, NT)[0:1] < 0.75 * DEAD, 1.0, 0.0)
         live_ref[pl.ds(g, 1), :] = live
         for part in chunks_of(width):
             cos = mm(cols_ref[part, :], rows, NT)
-            expo = jnp.exp(cos * (1.0 / TEACHER_TEMP)) * live
+            expo = jnp.exp2(cos * (LOG2E / TEACHER_TEMP)) * live
             expo_ref[g, part, :] = expo.astype(bf16)
             total_ref[part, :] += expo[:, 0:128] + expo[:, 128:256]
         return 0
@@ -426,7 +429,7 @@
         acc = jnp.zeros((8, CAP), f32)
         pull = jnp.zeros((cols_ref.shape[0], CAP), f32)
         for part in chunks_of(width):
-            raised = jnp.exp(mm(cols_t_ref[part, :], rows, NT) * (1.0 / STUDENT_TEMP))
+            raised = jnp.exp2(mm(cols_t_ref[part, :], rows, NT) * (LOG2E / STUDENT_TEMP))
             acc = acc + fold(raised)
             raised = raised.astype(bf16)
             raised_ref[g, part, :] = raised
@@ -636,7 +639,6 @@
         scratch=[
             pltpu.VMEM((width, bot), bf16),
             pltpu.VMEM((dp, 2, HALF, bot), bf16),
-            pltpu.VMEM((dp, EXTRA, bot), bf16),
             pltpu.VMEM(big, bf16),
             pltpu.VMEM((width, 128), f32),
             *[sem(dp // GROUP)] * 4,
@@ -802,13 +804,13 @@
     sems = dma((dp,))
     sel, send, member, mine = call(
         select_body,
-        [((CAP, tokens.shape[0]), bf16), ((dp, HALF + EXTRA, bot), bf16), ((8, CAP), f32), ((EXTRA, CAP), bf16)],
+        [((CAP, tokens.shape[0]), bf16), ((dp, HALF, bot), bf16), ((8, CAP), f32), ((EXTRA, CAP), bf16)],
         (at, masks, teacher_feats),
         in_specs=[SMEM, VMEM, VMEM],
         out_specs=[VMEM, HBM, HBM, HBM],
         scratch=[
             pltpu.VMEM((CAP, bot), bf16),
-            pltpu.VMEM((HALF + EXTRA, bot), bf16),
+            pltpu.VMEM((HALF, bot), bf16),
             pltpu.VMEM((8, CAP), f32),
             pltpu.VMEM((EXTRA, CAP), bf16),
             sems,
@@ -852,7 +854,7 @@
             pltpu.VMEM((dp, per, half), bf16),
             pltpu.VMEM((dp, share, half), bf16),
             pltpu.VMEM((half, bot), bf16),
-            sem(3),
+            sem(2 + len(chunks_of(half))),
         ],
     )
     feats_other = sibling(feats)

time: 254 us -> 253 us (level)
  transfers between devices with their start and end apart: 27 -> 27, of which waited for: 14 -> 14; matrix products, arithmetic and copies ran while one was open for 2% -> 2% of each run, Pallas kernels for 19% -> 18%
where the time goes in v6:
time: 253 us
  Pallas kernels  71.6 us (28%)
  waiting for transfers between devices  63.1 us (25%)
  blocking collectives  48.6 us (19%)
  starting transfers between devices  48.2 us (19%)
  between operations  14.4 us (6%)
  other arithmetic  4.86 us (2%)
    pallas_call x20, Pallas kernels, call(): pl.pallas_call(body, out_shape=outs, in_specs=in_specs, out_specs=tuple(s...  71.6 us
    all_to_all x3, blocking collectives, exchange(): return lax.all_to_all(x, axis, split_axis=0, concat_axis=0, tiled=True)  48.6 us
    all_to_all x4, waiting for transfers between devices, exchange(): return lax.all_to_all(x, axis, split_axis=0, concat_axis=0, tiled=True)  36.3 us
    ppermute x9, starting transfers between devices, sibling(): return lax.ppermute(x, 'tensor', [(i, i ^ 1) for i in range(peers)])  18.5 us
    all_to_all x4, starting transfers between devices, exchange(): return lax.all_to_all(x, axis, split_axis=0, concat_axis=0, tiled=True)  16.4 us
    ppermute x12, starting transfers between devices, levels(): return lax.ppermute(x, 'tensor', [(i, i ^ 2 * by) for i in range(peers)])  13.2 us
    all_gather x1, waiting for transfers between devices, parts_of(): lax.all_gather(w_pack, 'dp', axis=0, tiled=True).reshape(dp, lines, half)  13 us
    ppermute x9, waiting for transfers between devices, sibling(): return lax.ppermute(x, 'tensor', [(i, i ^ 1) for i in range(peers)])  8.36 us
  transfers between devices with their start and end apart: 27, of which 14 were waited for; matrix products, arithmetic and copies ran while one was open for 2% of the time, Pallas kernels for 18%

profile of v6, /device:TPU:1, one launch (start us, length us, event | category | flops | bytes accessed | tf_op | source)
XLA Modules:
  0.0 252.5 jit_solution(2881586925523398578)
XLA Ops:
  7.3 2.5 shard_map.119
  10.6 2.3 shard_map.111
  13.0 26.8 %all_to_all.35.own_hbm = bf16[16,128,256]{2,1,0:T(8,128)(2,1)S(1)} all-to-all(bf16[16,128,256]{2,1,0:T(8,128)(2,1)} %get-tuple-element.36), channel_id=1, replica_groups=mesh['dp'=16,'tensor'=8] {'dp'}, dimensions={0} | all-to-all | bytes 2097152 | tf_op jit(solution)/shard_map/all_to_all | solution.py:721
  39.8 2.7 %collective-permute-start = (bf16[16,128,256]{2,1,0:T(8,128)(2,1)S(1)}, bf16[16,128,256]{2,1,0:T(8,128)(2,1)S(1)}, u32[]{:S(2)}, u32[]{:S(2)}) collective-permute-start(bf16[16,128,256]{2,1,0:T(8,128)(2,1)S(1)} %all_to_all.35.own_hbm), channel_id=1, source_target_pairs={{0,1},{1,0},{2,3},{3,2},{4,5},{5,4},{6,7},{7,6},{8,9},{9,8},{10,11... | collective-permute-start | bytes 3145736 | tf_op jit(solution)/shard_map/ppermute | solution.py:726
  44.0 3.8 %shard_map.118.rows_hbm = bf16[256,1536]{1,0:T(8,128)(2,1)} custom-call(bf16[256,1024]{1,0:T(8,128)(2,1)S(1)} %get-tuple-element.44.sel_ref, bf16[1024,1536]{1,0:T(8,128)(2,1)} %tokens_hbm.1), custom_call_target="tpu_custom_call" | custom-call | tf_op jit(solution)/shard_map/pallas_call | solution.py:39
  47.8 7.3 %shard_map.112 = (bf16[16,1024,256]{2,1,0:T(8,128)(2,1)}, f32[16,256]{1,0:T(8,128)S(1)}, f32[16,256]{1,0:T(8,128)S(1)}) custom-call(s32[2]{0:T(128)S(1)} %pad_add_fusion.at_ref, bf16[1024,256]{1,0:T(8,128)(2,1)} %get-tuple-element.35.cols_hbm, bf16[16,128,256]{2,1,0:T(8,128)(2,1)S(1)} %all_to_all.35.own_hbm, ...), custom_call_target="tpu_custom_call" | custom-call | tf_op jit(solution)/shard_map/pallas_call | solution.py:39
  55.1 13.0 %all-gather.3.cloned.1.call-done = bf16[1792,1024]{1,0:T(8,128)(2,1)} async-done(((bf16[112,1024]{1,0:T(8,128)(2,1)}), bf16[1792,1024]{1,0:T(8,128)(2,1)}) %all-gather.3.cloned.1.call-update) | async-done | bytes 3670032 | tf_op jit(solution)/shard_map/all_gather | solution.py:802
  68.2 5.2 %shard_map.120 = (bf16[256,1024]{1,0:T(8,128)(2,1)}, f32[256,1024]{1,0:T(8,128)}, f32[256,256]{1,0:T(8,128)S(1)}, bf16[1024,256]{1,0:T(8,128)(2,1)}) custom-call(bf16[256,1536]{1,0:T(8,128)(2,1)} %shard_map.118.rows_hbm, bf16[16,112,1024]{2,1,0:T(8,128)(2,1)} %bitcast.6), custom_call_target="tpu_custom_call" | custom-call | tf_op jit(solution)/shard_map/pallas_call | solution.py:39
  77.8 2.7 %collective-permute-start.4 = (f32[16,256]{1,0:T(8,128)S(1)}, f32[16,256]{1,0:T(8,128)S(1)}, u32[]{:S(2)}, u32[]{:S(2)}) collective-permute-start(f32[16,256]{1,0:T(8,128)S(1)} %add.36.own_ref), channel_id=1, source_target_pairs={{0,6},{1,7},{2,4},{3,5},{4,2},{5,3},{6,0},{7,1},{8,14},{9,15},{10,... | collective-permute-start | bytes 49160 | tf_op jit(solution)/shard_map/ppermute | solution.py:738
  81.6 3.0 %collective-permute-done.3.far_ref = f32[16,256]{1,0:T(8,128)S(1)} collective-permute-done((f32[16,256]{1,0:T(8,128)S(1)}, f32[16,256]{1,0:T(8,128)S(1)}, u32[]{:S(2)}, u32[]{:S(2)}) %collective-permute-start.3) | collective-permute-done | bytes 16416 | tf_op jit(solution)/shard_map/ppermute | solution.py:738
  84.6 11.4 %all_to_all.36.parts_ref = bf16[16,16,256]{2,1,0:T(8,128)(2,1)S(1)} all-to-all(bf16[16,16,256]{2,1,0:T(8,128)(2,1)S(1)} %shard_map.113), channel_id=1, replica_groups=mesh['dp'=16,'tensor'=8] {'dp'}, dimensions={0} | all-to-all | bytes 262144 | tf_op jit(solution)/shard_map/all_to_all | solution.py:721
  96.0 6.0 %shard_map.114 = f32[16,256]{1,0:T(8,128)S(1)} custom-call(bf16[16,1024,256]{2,1,0:T(8,128)(2,1)} %get-tuple-element.37.expo_hbm, bf16[16,16,256]{2,1,0:T(8,128)(2,1)S(1)} %all_to_all.36.parts_ref, f32[16,256]{1,0:T(8,128)S(1)} %get-tuple-element.39.live_ref), custom_call_target="tpu_custom_call" | custom-call | tf_op jit(solution)/shard_map/pallas_call | solution.py:39
  102.0 2.9 %collective-permute-start.5 = (f32[16,256]{1,0:T(8,128)S(1)}, f32[16,256]{1,0:T(8,128)S(1)}, u32[]{:S(2)}, u32[]{:S(2)}) collective-permute-start(f32[16,256]{1,0:T(8,128)S(1)} %shard_map.114), channel_id=1, source_target_pairs={{0,1},{1,0},{2,3},{3,2},{4,5},{5,4},{6,7},{7,6},{8,9},{9,8},{10,11... | collective-permute-start | bytes 49160 | tf_op jit(solution)/shard_map/ppermute | solution.py:726
  111.0 10.4 %all_to_all.37.parts_ref = bf16[16,16,256]{2,1,0:T(8,128)(2,1)S(1)} all-to-all(bf16[16,16,256]{2,1,0:T(8,128)(2,1)S(1)} %shard_map.115), channel_id=1, replica_groups=mesh['dp'=16,'tensor'=8] {'dp'}, dimensions={0} | all-to-all | bytes 262144 | tf_op jit(solution)/shard_map/all_to_all | solution.py:721
  121.4 8.2 %shard_map.116 = (bf16[16,272,128]{2,1,0:T(8,128)(2,1)S(1)}, bf16[16,272,128]{2,1,0:T(8,128)(2,1)S(1)}, f32[1024,128]{1,0:T(8,128)}) custom-call(s32[2]{0:T(128)S(1)} %pad_add_fusion.at_ref, bf16[16,1024,256]{2,1,0:T(8,128)(2,1)} %get-tuple-element.37.expo_hbm, bf16[16,16,256]{2,1,0:T(8,128)(2,1)S(1)} %all_to_all.37.parts_ref, ...), custom_call_target="tpu_custom_call" | custom-call | tf_op jit(solution)/shard_map/pallas_call | solution.py:39
  129.6 2.7 %collective-permute-start.9 = (bf16[16,272,128]{2,1,0:T(8,128)(2,1)S(1)}, bf16[16,272,128]{2,1,0:T(8,128)(2,1)S(1)}, u32[]{:S(2)}, u32[]{:S(2)}) collective-permute-start(bf16[16,272,128]{2,1,0:T(8,128)(2,1)S(1)} %get-tuple-element.42), channel_id=1, source_target_pairs={{0,1},{1,0},{2,3},{3,2},{4,5},{5,4},{6,7},{7,6},{8,9},{9,8},{10,11... | collective-permute-start | bytes 3342344 | tf_op jit(solution)/shard_map/ppermute | solution.py:726
  132.3 2.4 collective-permute-done.9
  136.0 9.2 %shard_map.122 = (bf16[16,1024,256]{2,1,0:T(8,128)(2,1)}, bf16[16,272,128]{2,1,0:T(8,128)(2,1)S(1)}, bf16[16,272,128]{2,1,0:T(8,128)(2,1)}) custom-call(s32[2]{0:T(128)S(1)} %pad_add_fusion.at_ref, bf16[1024,256]{1,0:T(8,128)(2,1)S(1)} %copy-done.6, bf16[256,1024]{1,0:T(8,128)(2,1)S(1)} %copy-done.2, bf16[16,256,256]{2,1,0:T(8,128)(2,1)} %bitcast.8), custom_call_target="tpu_custom_call" | custom-call | tf_op jit(solution)/shard_map/pallas_call | solution.py:39
  145.7 3.7 %all-to-all-start.3 = ((bf16[16,272,128]{2,1,0:T(8,128)(2,1)}), bf16[16,272,128]{2,1,0:T(8,128)(2,1)S(1)}, u32[]{:S(2)}, u32[]{:S(2)}) async-start(bf16[16,272,128]{2,1,0:T(8,128)(2,1)} %add_convert_fusion.1), calls=%async_computation.3 | async-start | bytes 2228224 | tf_op jit(solution)/shard_map/all_to_all | solution.py:721
  149.4 2.5 %add_convert_fusion = bf16[16,272,128]{2,1,0:T(8,128)(2,1)} fusion(bf16[16,272,128]{2,1,0:T(8,128)(2,1)} %collective-permute-done.15, bf16[16,272,128]{2,1,0:T(8,128)(2,1)S(1)} %get-tuple-element.48), kind=kLoop, calls=%fused_computation | loop fusion | flops 2228224 | bytes 3342336 | tf_op jit(solution)/shard_map/convert_element_type | solution.py:748
  151.9 16.7 %all-to-all-done.3.parts_hbm = bf16[16,272,128]{2,1,0:T(8,128)(2,1)S(1)} async-done(((bf16[16,272,128]{2,1,0:T(8,128)(2,1)}), bf16[16,272,128]{2,1,0:T(8,128)(2,1)S(1)}, u32[]{:S(2)}, u32[]{:S(2)}) %all-to-all-start.3) | async-done | bytes 1114144 | tf_op jit(solution)/shard_map/all_to_all | solution.py:721
  168.7 3.7 %all-to-all-start.4 = ((bf16[16,272,128]{2,1,0:T(8,128)(2,1)}), bf16[16,272,128]{2,1,0:T(8,128)(2,1)S(1)}, u32[]{:S(2)}, u32[]{:S(2)}) async-start(bf16[16,272,128]{2,1,0:T(8,128)(2,1)} %add_convert_fusion), calls=%async_computation.4 | async-start | bytes 2228224 | tf_op jit(solution)/shard_map/all_to_all | solution.py:721
  176.8 12.3 %all-to-all-done.4.parts_hbm = bf16[16,272,128]{2,1,0:T(8,128)(2,1)S(1)} async-done(((bf16[16,272,128]{2,1,0:T(8,128)(2,1)}), bf16[16,272,128]{2,1,0:T(8,128)(2,1)S(1)}, u32[]{:S(2)}, u32[]{:S(2)}) %all-to-all-start.4) | async-done | bytes 1114144 | tf_op jit(solution)/shard_map/all_to_all | solution.py:721
  193.5 3.6 %collective-permute-start.13 = (f32[1,272,128]{2,1,0:T(8,128)S(1)}, f32[1,272,128]{2,1,0:T(8,128)S(1)}, u32[]{:S(2)}, u32[]{:S(2)}) collective-permute-start(f32[1,272,128]{2,1,0:T(8,128)S(1)} %add_add_fusion.1.pull_ref), channel_id=1, source_target_pairs={{0,1},{1,0},{2,3},{3,2},{4,5},{5,4},{6,7},{7,6},{8,9},{9,8},{10,11... | collective-permute-start | bytes 417800 | tf_op jit(solution)/shard_map/ppermute | solution.py:726
  198.0 3.9 %collective-permute-start.19 = (f32[1,272,128]{2,1,0:T(8,128)S(1)}, f32[1,272,128]{2,1,0:T(8,128)S(1)}, u32[]{:S(2)}, u32[]{:S(2)}) collective-permute-start(f32[1,272,128]{2,1,0:T(8,128)S(1)} %add_add_fusion.push_ref), channel_id=1, source_target_pairs={{0,1},{1,0},{2,3},{3,2},{4,5},{5,4},{6,7},{7,6},{8,9},{9,8},{10,11... | collective-permute-start | bytes 417800 | tf_op jit(solution)/shard_map/ppermute | solution.py:726
  203.0 4.6 %shard_map.124 = (bf16[16,128,256]{2,1,0:T(8,128)(2,1)}, bf16[256,1024]{1,0:T(8,128)(2,1)}, f32[1,4]{1,0:T(1,128)}) custom-call(s32[2]{0:T(128)S(1)} %pad_add_fusion.at_ref, f32[1,272,128]{2,1,0:T(8,128)S(1)} %add_add_fusion.1.pull_ref, f32[1,272,128]{2,1,0:T(8,128)S(1)} %collective-permute-done.13.pull_other_ref, f32[1,272,128]{2,1,0:T(8,128)S(1)} %add_add_fusion.push_ref, ...), custom_call_target="tpu_custom_call" | custom-call | tf_op jit(solution)/shard_map/pallas_call | solution.py:39
  207.6 3.8 %all-to-all-start.5 = ((bf16[16,128,256]{2,1,0:T(8,128)(2,1)}), bf16[16,128,256]{2,1,0:T(8,128)(2,1)S(1)}, u32[]{:S(2)}, u32[]{:S(2)}) async-start(bf16[16,128,256]{2,1,0:T(8,128)(2,1)} %get-tuple-element.55), calls=%async_computation.5 | async-start | bytes 2097152 | tf_op jit(solution)/shard_map/all_to_all | solution.py:721
  211.4 3.8 %shard_map.125.rows_ref = bf16[256,1536]{1,0:T(8,128)(2,1)} custom-call(bf16[256,1024]{1,0:T(8,128)(2,1)S(1)} %copy-done.3, bf16[16,112,1024]{2,1,0:T(8,128)(2,1)} %bitcast.7), custom_call_target="tpu_custom_call" | custom-call | tf_op jit(solution)/shard_map/pallas_call | solution.py:39
  215.7 2.1 collective-permute-done.20.other_ref
  221.1 7.2 %all-to-all-done.5.got_hbm = bf16[16,128,256]{2,1,0:T(8,128)(2,1)S(1)} async-done(((bf16[16,128,256]{2,1,0:T(8,128)(2,1)}), bf16[16,128,256]{2,1,0:T(8,128)(2,1)S(1)}, u32[]{:S(2)}, u32[]{:S(2)}) %all-to-all-start.5) | async-done | bytes 1048608 | tf_op jit(solution)/shard_map/all_to_all | solution.py:721
  229.8 5.2 %all-to-all-start.6 = ((bf16[8,112,256]{2,1,0:T(8,128)(2,1)}), bf16[8,112,256]{2,1,0:T(8,128)(2,1)S(1)}, u32[]{:S(2)}, u32[]{:S(2)}) async-start(bf16[8,112,256]{2,1,0:T(8,128)(2,1)} %shard_map.127), calls=%async_computation.6 | async-start | bytes 917504 | tf_op jit(solution)/shard_map/all_to_all | solution.py:721
  235.0 9.3 %shard_map.129 = f32[256,1024]{1,0:T(8,128)} custom-call(bf16[16,1024,256]{2,1,0:T(8,128)(2,1)} %get-tuple-element.37.expo_hbm, bf16[16,1024,256]{2,1,0:T(8,128)(2,1)} %get-tuple-element.61.raised_hbm, f32[1024,128]{1,0:T(8,128)} %get-tuple-element.62.scale_hbm, bf16[16,128,256]{2,1,0:T(8,128)(2,1)S(1)} %all-to-all-done.5.got_hbm, ...), custom_call_target="tpu_custom_call" | custom-call | tf_op jit(solution)/shard_map/pallas_call | solution.py:39
  (76 shorter events, 33.0 us)
Async XLA Ops:
  7.2 61.0 %all-gather.3.cloned.1.call-start = ((), (), s32[]{:S(2)}) async-start(), calls=%async_computation.7 | async-start | bytes 3899392 | tf_op jit(solution)/shard_map/all_gather | solution.py:802
  9.9 126.2 %all-gather.5.cloned.1.call-start = ((), (), s32[]{:S(2)}) async-start(), calls=%async_computation.8 | async-start | bytes 2228224 | tf_op jit(solution)/shard_map/all_gather | solution.py:862
  12.9 29.5 %copy-start.1 = (bf16[256,1024]{1,0:T(8,128)(2,1)S(1)}, bf16[256,1024]{1,0:T(8,128)(2,1)}, u32[]{:S(2)}) copy-start(bf16[256,1024]{1,0:T(8,128)(2,1)} %proto_hbm.1) | copy-start | bytes 1572868
  12.9 29.5 %copy-start.5 = (bf16[256,1024]{1,0:T(8,128)(2,1)S(1)}, bf16[256,1024]{1,0:T(8,128)(2,1)}, u32[]{:S(2)}) copy-start(bf16[256,1024]{1,0:T(8,128)(2,1)} %teacher_ref.1) | copy-start | bytes 1572868
  39.8 8.0 %collective-permute-start = (bf16[16,128,256]{2,1,0:T(8,128)(2,1)S(1)}, bf16[16,128,256]{2,1,0:T(8,128)(2,1)S(1)}, u32[]{:S(2)}, u32[]{:S(2)}) collective-permute-start(bf16[16,128,256]{2,1,0:T(8,128)(2,1)S(1)} %all_to_all.35.own_hbm), channel_id=1, source_target_pairs={{0,1},{1,0},{2,3},{3,2},{4,5},{5,4},{6,7},{7,6},{8,9},{9,8},{10,11... | collective-permute-start | bytes 3145736 | tf_op jit(solution)/shard_map/ppermute | solution.py:726
  73.3 2.4 collective-permute-start.14
  76.5 1.3 collective-permute-start.1
  77.8 3.8 %collective-permute-start.4 = (f32[16,256]{1,0:T(8,128)S(1)}, f32[16,256]{1,0:T(8,128)S(1)}, u32[]{:S(2)}, u32[]{:S(2)}) collective-permute-start(f32[16,256]{1,0:T(8,128)S(1)} %add.36.own_ref), channel_id=1, source_target_pairs={{0,6},{1,7},{2,4},{3,5},{4,2},{5,3},{6,0},{7,1},{8,14},{9,15},{10,... | collective-permute-start | bytes 49160 | tf_op jit(solution)/shard_map/ppermute | solution.py:738
  80.5 4.1 %collective-permute-start.3 = (f32[16,256]{1,0:T(8,128)S(1)}, f32[16,256]{1,0:T(8,128)S(1)}, u32[]{:S(2)}, u32[]{:S(2)}) collective-permute-start(f32[16,256]{1,0:T(8,128)S(1)} %add.36.own_ref), channel_id=1, source_target_pairs={{0,4},{1,5},{2,6},{3,7},{4,0},{5,1},{6,2},{7,3},{8,12},{9,13},{10,... | collective-permute-start | bytes 49160 | tf_op jit(solution)/shard_map/ppermute | solution.py:738
  80.9 3.7 %collective-permute-start.2 = (f32[16,256]{1,0:T(8,128)S(1)}, f32[16,256]{1,0:T(8,128)S(1)}, u32[]{:S(2)}, u32[]{:S(2)}) collective-permute-start(f32[16,256]{1,0:T(8,128)S(1)} %add.36.own_ref), channel_id=1, source_target_pairs={{0,2},{1,3},{2,0},{3,1},{4,6},{5,7},{6,4},{7,5},{8,10},{9,11},{10,... | collective-permute-start | bytes 49160 | tf_op jit(solution)/shard_map/ppermute | solution.py:738
  96.0 25.4 %copy-start.2 = (bf16[256,1024]{1,0:T(8,128)(2,1)S(1)}, bf16[256,1024]{1,0:T(8,128)(2,1)}, u32[]{:S(2)}) copy-start(bf16[256,1024]{1,0:T(8,128)(2,1)} %get-tuple-element.40.cols_ref) | copy-start | bytes 1572868
  102.0 3.8 %collective-permute-start.5 = (f32[16,256]{1,0:T(8,128)S(1)}, f32[16,256]{1,0:T(8,128)S(1)}, u32[]{:S(2)}, u32[]{:S(2)}) collective-permute-start(f32[16,256]{1,0:T(8,128)S(1)} %shard_map.114), channel_id=1, source_target_pairs={{0,1},{1,0},{2,3},{3,2},{4,5},{5,4},{6,7},{7,6},{8,9},{9,8},{10,11... | collective-permute-start | bytes 49160 | tf_op jit(solution)/shard_map/ppermute | solution.py:726
  105.8 4.2 %collective-permute-start.8 = (f32[16,256]{1,0:T(8,128)S(1)}, f32[16,256]{1,0:T(8,128)S(1)}, u32[]{:S(2)}, u32[]{:S(2)}) collective-permute-start(f32[16,256]{1,0:T(8,128)S(1)} %add.37.own_ref), channel_id=1, source_target_pairs={{0,6},{1,7},{2,4},{3,5},{4,2},{5,3},{6,0},{7,1},{8,14},{9,15},{10,... | collective-permute-start | bytes 49160 | tf_op jit(solution)/shard_map/ppermute | solution.py:738
  106.8 4.1 %collective-permute-start.7 = (f32[16,256]{1,0:T(8,128)S(1)}, f32[16,256]{1,0:T(8,128)S(1)}, u32[]{:S(2)}, u32[]{:S(2)}) collective-permute-start(f32[16,256]{1,0:T(8,128)S(1)} %add.37.own_ref), channel_id=1, source_target_pairs={{0,4},{1,5},{2,6},{3,7},{4,0},{5,1},{6,2},{7,3},{8,12},{9,13},{10,... | collective-permute-start | bytes 49160 | tf_op jit(solution)/shard_map/ppermute | solution.py:738
  107.5 3.4 %collective-permute-start.6 = (f32[16,256]{1,0:T(8,128)S(1)}, f32[16,256]{1,0:T(8,128)S(1)}, u32[]{:S(2)}, u32[]{:S(2)}) collective-permute-start(f32[16,256]{1,0:T(8,128)S(1)} %add.37.own_ref), channel_id=1, source_target_pairs={{0,2},{1,3},{2,0},{3,1},{4,6},{5,7},{6,4},{7,5},{8,10},{9,11},{10,... | collective-permute-start | bytes 49160 | tf_op jit(solution)/shard_map/ppermute | solution.py:738
  129.6 5.1 %collective-permute-start.9 = (bf16[16,272,128]{2,1,0:T(8,128)(2,1)S(1)}, bf16[16,272,128]{2,1,0:T(8,128)(2,1)S(1)}, u32[]{:S(2)}, u32[]{:S(2)}) collective-permute-start(bf16[16,272,128]{2,1,0:T(8,128)(2,1)S(1)} %get-tuple-element.42), channel_id=1, source_target_pairs={{0,1},{1,0},{2,3},{3,2},{4,5},{5,4},{6,7},{7,6},{8,9},{9,8},{10,11... | collective-permute-start | bytes 3342344 | tf_op jit(solution)/shard_map/ppermute | solution.py:726
  145.2 4.2 %collective-permute-start.15 = (bf16[16,272,128]{2,1,0:T(8,128)(2,1)}, bf16[16,272,128]{2,1,0:T(8,128)(2,1)}, u32[]{:S(2)}, u32[]{:S(2)}) collective-permute-start(bf16[16,272,128]{2,1,0:T(8,128)(2,1)} %get-tuple-element.49), channel_id=1, source_target_pairs={{0,1},{1,0},{2,3},{3,2},{4,5},{5,4},{6,7},{7,6},{8,9},{9,8},{10,11... | collective-permute-start | bytes 3342344 | tf_op jit(solution)/shard_map/ppermute | solution.py:726
  145.7 23.0 %all-to-all-start.3 = ((bf16[16,272,128]{2,1,0:T(8,128)(2,1)}), bf16[16,272,128]{2,1,0:T(8,128)(2,1)S(1)}, u32[]{:S(2)}, u32[]{:S(2)}) async-start(bf16[16,272,128]{2,1,0:T(8,128)(2,1)} %add_convert_fusion.1), calls=%async_computation.3 | async-start | bytes 2228224 | tf_op jit(solution)/shard_map/all_to_all | solution.py:721
  168.7 20.4 %all-to-all-start.4 = ((bf16[16,272,128]{2,1,0:T(8,128)(2,1)}), bf16[16,272,128]{2,1,0:T(8,128)(2,1)S(1)}, u32[]{:S(2)}, u32[]{:S(2)}) async-start(bf16[16,272,128]{2,1,0:T(8,128)(2,1)} %add_convert_fusion), calls=%async_computation.4 | async-start | bytes 2228224 | tf_op jit(solution)/shard_map/all_to_all | solution.py:721
  173.4 29.5 %copy-start.7 = (f32[8,256]{1,0:T(8,128)S(1)}, f32[8,256]{1,0:T(8,128)}, u32[]{:S(2)}) copy-start(f32[8,256]{1,0:T(8,128)} %get-tuple-element.51.member_ref) | copy-start | bytes 24580
  173.4 29.5 %copy-start.8 = (bf16[16,256]{1,0:T(8,128)(2,1)S(1)}, bf16[16,256]{1,0:T(8,128)(2,1)}, u32[]{:S(2)}) copy-start(bf16[16,256]{1,0:T(8,128)(2,1)} %get-tuple-element.50.mine_ref) | copy-start | bytes 24580
  173.4 19.4 %collective-permute-start.12 = (bf16[1,272,128]{2,1,0:T(8,128)(2,1)}, bf16[1,272,128]{2,1,0:T(8,128)(2,1)S(1)}, u32[]{:S(2)}, u32[]{:S(2)}) collective-permute-start(bf16[1,272,128]{2,1,0:T(8,128)(2,1)} %shard_map.117), channel_id=1, source_target_pairs={{0,6},{1,7},{2,4},{3,5},{4,2},{5,3},{6,0},{7,1},{8,14},{9,15},{10,... | collective-permute-start | bytes 208904 | tf_op jit(solution)/shard_map/ppermute | solution.py:738
  175.3 18.1 %collective-permute-start.11 = (bf16[1,272,128]{2,1,0:T(8,128)(2,1)}, bf16[1,272,128]{2,1,0:T(8,128)(2,1)S(1)}, u32[]{:S(2)}, u32[]{:S(2)}) collective-permute-start(bf16[1,272,128]{2,1,0:T(8,128)(2,1)} %shard_map.117), channel_id=1, source_target_pairs={{0,4},{1,5},{2,6},{3,7},{4,0},{5,1},{6,2},{7,3},{8,12},{9,13},{10,... | collective-permute-start | bytes 208904 | tf_op jit(solution)/shard_map/ppermute | solution.py:738
  176.2 17.2 %collective-permute-start.10 = (bf16[1,272,128]{2,1,0:T(8,128)(2,1)}, bf16[1,272,128]{2,1,0:T(8,128)(2,1)S(1)}, u32[]{:S(2)}, u32[]{:S(2)}) collective-permute-start(bf16[1,272,128]{2,1,0:T(8,128)(2,1)} %shard_map.117), channel_id=1, source_target_pairs={{0,2},{1,3},{2,0},{3,1},{4,6},{5,7},{6,4},{7,5},{8,10},{9,11},{10,... | collective-permute-start | bytes 208904 | tf_op jit(solution)/shard_map/ppermute | solution.py:738
  190.1 7.0 %collective-permute-start.18 = (bf16[1,272,128]{2,1,0:T(8,128)(2,1)}, bf16[1,272,128]{2,1,0:T(8,128)(2,1)S(1)}, u32[]{:S(2)}, u32[]{:S(2)}) collective-permute-start(bf16[1,272,128]{2,1,0:T(8,128)(2,1)} %shard_map.123), channel_id=1, source_target_pairs={{0,6},{1,7},{2,4},{3,5},{4,2},{5,3},{6,0},{7,1},{8,14},{9,15},{10,... | collective-permute-start | bytes 208904 | tf_op jit(solution)/shard_map/ppermute | solution.py:738
  192.0 5.2 %collective-permute-start.17 = (bf16[1,272,128]{2,1,0:T(8,128)(2,1)}, bf16[1,272,128]{2,1,0:T(8,128)(2,1)S(1)}, u32[]{:S(2)}, u32[]{:S(2)}) collective-permute-start(bf16[1,272,128]{2,1,0:T(8,128)(2,1)} %shard_map.123), channel_id=1, source_target_pairs={{0,4},{1,5},{2,6},{3,7},{4,0},{5,1},{6,2},{7,3},{8,12},{9,13},{10,... | collective-permute-start | bytes 208904 | tf_op jit(solution)/shard_map/ppermute | solution.py:738
  192.8 4.3 %collective-permute-start.16 = (bf16[1,272,128]{2,1,0:T(8,128)(2,1)}, bf16[1,272,128]{2,1,0:T(8,128)(2,1)S(1)}, u32[]{:S(2)}, u32[]{:S(2)}) collective-permute-start(bf16[1,272,128]{2,1,0:T(8,128)(2,1)} %shard_map.123), channel_id=1, source_target_pairs={{0,2},{1,3},{2,0},{3,1},{4,6},{5,7},{6,4},{7,5},{8,10},{9,11},{10,... | collective-permute-start | bytes 208904 | tf_op jit(solution)/shard_map/ppermute | solution.py:738
  193.5 8.5 %collective-permute-start.13 = (f32[1,272,128]{2,1,0:T(8,128)S(1)}, f32[1,272,128]{2,1,0:T(8,128)S(1)}, u32[]{:S(2)}, u32[]{:S(2)}) collective-permute-start(f32[1,272,128]{2,1,0:T(8,128)S(1)} %add_add_fusion.1.pull_ref), channel_id=1, source_target_pairs={{0,1},{1,0},{2,3},{3,2},{4,5},{5,4},{6,7},{7,6},{8,9},{9,8},{10,11... | collective-permute-start | bytes 417800 | tf_op jit(solution)/shard_map/ppermute | solution.py:726
  198.0 4.9 %collective-permute-start.19 = (f32[1,272,128]{2,1,0:T(8,128)S(1)}, f32[1,272,128]{2,1,0:T(8,128)S(1)}, u32[]{:S(2)}, u32[]{:S(2)}) collective-permute-start(f32[1,272,128]{2,1,0:T(8,128)S(1)} %add_add_fusion.push_ref), channel_id=1, source_target_pairs={{0,1},{1,0},{2,3},{3,2},{4,5},{5,4},{6,7},{7,6},{8,9},{9,8},{10,11... | collective-permute-start | bytes 417800 | tf_op jit(solution)/shard_map/ppermute | solution.py:726
  207.6 20.7 %all-to-all-start.5 = ((bf16[16,128,256]{2,1,0:T(8,128)(2,1)}), bf16[16,128,256]{2,1,0:T(8,128)(2,1)S(1)}, u32[]{:S(2)}, u32[]{:S(2)}) async-start(bf16[16,128,256]{2,1,0:T(8,128)(2,1)} %get-tuple-element.55), calls=%async_computation.5 | async-start | bytes 2097152 | tf_op jit(solution)/shard_map/all_to_all | solution.py:721
  215.3 2.6 %collective-permute-start.20 = (bf16[256,1536]{1,0:T(8,128)(2,1)}, bf16[256,1536]{1,0:T(8,128)(2,1)S(1)}, u32[]{:S(2)}, u32[]{:S(2)}) collective-permute-start(bf16[256,1536]{1,0:T(8,128)(2,1)} %shard_map.125.rows_ref), channel_id=1, source_target_pairs={{0,1},{1,0},{2,3},{3,2},{4,5},{5,4},{6,7},{7,6},{8,9},{9,8},{10,11... | collective-permute-start | bytes 2359304 | tf_op jit(solution)/shard_map/ppermute | solution.py:726
  229.8 14.5 %all-to-all-start.6 = ((bf16[8,112,256]{2,1,0:T(8,128)(2,1)}), bf16[8,112,256]{2,1,0:T(8,128)(2,1)S(1)}, u32[]{:S(2)}, u32[]{:S(2)}) async-start(bf16[8,112,256]{2,1,0:T(8,128)(2,1)} %shard_map.127), calls=%async_computation.6 | async-start | bytes 917504 | tf_op jit(solution)/shard_map/all_to_all | solution.py:721
  (6 other events, 29.7 us)
Sparse Core Ops, SparseCore 0:
  10.1 57.9 all-gather.2
  76.6 42.7 all-gather.4

commit v7 on v6

--- a/solution.py
+++ b/solution.py
@@ -163,25 +163,33 @@
     rows, hid = w_in_hbm.shape
     block, bot = w_out_hbm.shape
     half = block // 2
-    loads = copies([(w_in_hbm, w_in_ref), (w_out_hbm, w_out_ref)], sems)
+    parts = [slice(0, hid // 2), slice(hid // 2, hid)]
+    pairs = [(w_out_hbm, w_out_ref)] + [(w_in_hbm.at[:, part], w_in_ref.at[:, part]) for part in parts]
+    loads = copies(pairs, sems)
     for load in loads:
         load.start()
     core = at_ref[0]
     row = iota((2 * block, block), 0)
     col = iota((2 * block, block), 1)
     pick = (row == (col // half) * block + core * half + col % half).astype(f32).astype(bf16)
-    for load in loads:
-        load.wait()
-    for p in range(hid // (2 * block)):
-        two = w_in_ref[:, p * 2 * block : (p + 1) * 2 * block]
-        pack_ref[0:rows, p * block : (p + 1) * block] = mm(two, pick).astype(bf16)
+    loads[0].wait()
     lines = pack_ref.shape[0] - rows
     for q in range(half // lines):
         at = pl.multiple_of(core * half + q * lines, lines)
         pack_ref[rows : rows + lines, q * bot : (q + 1) * bot] = w_out_ref[pl.ds(at, lines), :]
-    store = pltpu.make_async_copy(pack_ref, pack_hbm, sems.at[0])
-    store.start()
-    store.wait()
+    count = hid // (4 * block)
+    stores = []
+    for i in range(2):
+        loads[1 + i].wait()
+        for p in range(i * count, (i + 1) * count):
+            two = w_in_ref[:, p * 2 * block : (p + 1) * 2 * block]
+            pack_ref[0:rows, p * block : (p + 1) * block] = mm(two, pick).astype(bf16)
+        done = slice(i * count * block, (i + 1) * count * block)
+        store = pltpu.make_async_copy(pack_ref.at[:, done], pack_hbm.at[:, done], sems.at[3 + i])
+        store.start()
+        stores.append(store)
+    for store in stores:
+        store.wait()
 
 
 def w_in_load(w_hbm, w_in_ref, at):
@@ -797,7 +805,7 @@
         (at, w_in, w_out),
         in_specs=[SMEM, HBM, HBM],
         out_specs=[HBM],
-        scratch=[pltpu.VMEM(w_in.shape, bf16), pltpu.VMEM(w_out.shape, bf16), pltpu.VMEM((lines, half), bf16), sem(2)],
+        scratch=[pltpu.VMEM(w_in.shape, bf16), pltpu.VMEM(w_out.shape, bf16), pltpu.VMEM((lines, half), bf16), sem(5)],
     )
     w_all = lax.all_gather(w_pack, "dp", axis=0, tiled=True).reshape(dp, lines, half)
     dma = pltpu.SemaphoreType.DMA

time: 253 us -> 254 us (level)
  no operation moved by 1% of the time
where the time goes in v7:
time: 254 us; the launch traced here: 253 us
  Pallas kernels  71.7 us (28%)
  waiting for transfers between devices  63.1 us (25%)
  blocking collectives  48.6 us (19%)
  starting transfers between devices  48.2 us (19%)
  between operations  14.4 us (6%)
  other arithmetic  4.86 us (2%)
    pallas_call x20, Pallas kernels, call(): pl.pallas_call(body, out_shape=outs, in_specs=in_specs, out_specs=tuple(s...  71.7 us
    all_to_all x3, blocking collectives, exchange(): return lax.all_to_all(x, axis, split_axis=0, concat_axis=0, tiled=True)  48.6 us
    all_to_all x4, waiting for transfers between devices, exchange(): return lax.all_to_all(x, axis, split_axis=0, concat_axis=0, tiled=True)  36.3 us
    ppermute x9, starting transfers between devices, sibling(): return lax.ppermute(x, 'tensor', [(i, i ^ 1) for i in range(peers)])  18.5 us
    all_to_all x4, starting transfers between devices, exchange(): return lax.all_to_all(x, axis, split_axis=0, concat_axis=0, tiled=True)  16.4 us
    ppermute x12, starting transfers between devices, levels(): return lax.ppermute(x, 'tensor', [(i, i ^ 2 * by) for i in range(peers)])  13.2 us
    all_gather x1, waiting for transfers between devices, parts_of(): lax.all_gather(w_pack, 'dp', axis=0, tiled=True).reshape(dp, lines, half)  13.1 us
    ppermute x9, waiting for transfers between devices, sibling(): return lax.ppermute(x, 'tensor', [(i, i ^ 1) for i in range(peers)])  8.35 us
  transfers between devices with their start and end apart: 27, of which 14 were waited for; matrix products, arithmetic and copies ran while one was open for 2% of the time, Pallas kernels for 18%

profile of v7, /device:TPU:1, one launch (start us, length us, event | category | flops | bytes accessed | tf_op | source)
XLA Modules:
  0.0 252.7 jit_solution(7635779673420583557)
XLA Ops:
  7.3 2.6 %shard_map.119 = bf16[112,1024]{1,0:T(8,128)(2,1)} custom-call(s32[2]{0:T(128)S(1)} %pad_add_fusion.at_ref, bf16[96,2048]{1,0:T(8,128)(2,1)} %w_in_hbm.1, bf16[128,256]{1,0:T(8,128)(2,1)} %w_out_hbm.1), custom_call_target="tpu_custom_call" | custom-call | tf_op jit(solution)/shard_map/pallas_call | solution.py:39
  10.7 2.3 shard_map.111
  13.1 26.8 %all_to_all.35.own_hbm = bf16[16,128,256]{2,1,0:T(8,128)(2,1)S(1)} all-to-all(bf16[16,128,256]{2,1,0:T(8,128)(2,1)} %get-tuple-element.36), channel_id=1, replica_groups=mesh['dp'=16,'tensor'=8] {'dp'}, dimensions={0} | all-to-all | bytes 2097152 | tf_op jit(solution)/shard_map/all_to_all | solution.py:729
  39.9 2.7 %collective-permute-start = (bf16[16,128,256]{2,1,0:T(8,128)(2,1)S(1)}, bf16[16,128,256]{2,1,0:T(8,128)(2,1)S(1)}, u32[]{:S(2)}, u32[]{:S(2)}) collective-permute-start(bf16[16,128,256]{2,1,0:T(8,128)(2,1)S(1)} %all_to_all.35.own_hbm), channel_id=1, source_target_pairs={{0,1},{1,0},{2,3},{3,2},{4,5},{5,4},{6,7},{7,6},{8,9},{9,8},{10,11... | collective-permute-start | bytes 3145736 | tf_op jit(solution)/shard_map/ppermute | solution.py:734
  44.1 3.8 %shard_map.118.rows_hbm = bf16[256,1536]{1,0:T(8,128)(2,1)} custom-call(bf16[256,1024]{1,0:T(8,128)(2,1)S(1)} %get-tuple-element.44.sel_ref, bf16[1024,1536]{1,0:T(8,128)(2,1)} %tokens_hbm.1), custom_call_target="tpu_custom_call" | custom-call | tf_op jit(solution)/shard_map/pallas_call | solution.py:39
  47.9 7.3 %shard_map.112 = (bf16[16,1024,256]{2,1,0:T(8,128)(2,1)}, f32[16,256]{1,0:T(8,128)S(1)}, f32[16,256]{1,0:T(8,128)S(1)}) custom-call(s32[2]{0:T(128)S(1)} %pad_add_fusion.at_ref, bf16[1024,256]{1,0:T(8,128)(2,1)} %get-tuple-element.35.cols_hbm, bf16[16,128,256]{2,1,0:T(8,128)(2,1)S(1)} %all_to_all.35.own_hbm, ...), custom_call_target="tpu_custom_call" | custom-call | tf_op jit(solution)/shard_map/pallas_call | solution.py:39
  55.2 13.1 %all-gather.3.cloned.1.call-done = bf16[1792,1024]{1,0:T(8,128)(2,1)} async-done(((bf16[112,1024]{1,0:T(8,128)(2,1)}), bf16[1792,1024]{1,0:T(8,128)(2,1)}) %all-gather.3.cloned.1.call-update) | async-done | bytes 3670032 | tf_op jit(solution)/shard_map/all_gather | solution.py:810
  68.3 5.2 %shard_map.120 = (bf16[256,1024]{1,0:T(8,128)(2,1)}, f32[256,1024]{1,0:T(8,128)}, f32[256,256]{1,0:T(8,128)S(1)}, bf16[1024,256]{1,0:T(8,128)(2,1)}) custom-call(bf16[256,1536]{1,0:T(8,128)(2,1)} %shard_map.118.rows_hbm, bf16[16,112,1024]{2,1,0:T(8,128)(2,1)} %bitcast.6), custom_call_target="tpu_custom_call" | custom-call | tf_op jit(solution)/shard_map/pallas_call | solution.py:39
  78.0 2.7 %collective-permute-start.4 = (f32[16,256]{1,0:T(8,128)S(1)}, f32[16,256]{1,0:T(8,128)S(1)}, u32[]{:S(2)}, u32[]{:S(2)}) collective-permute-start(f32[16,256]{1,0:T(8,128)S(1)} %add.36.own_ref), channel_id=1, source_target_pairs={{0,6},{1,7},{2,4},{3,5},{4,2},{5,3},{6,0},{7,1},{8,14},{9,15},{10,... | collective-permute-start | bytes 49160 | tf_op jit(solution)/shard_map/ppermute | solution.py:746
  81.8 3.0 %collective-permute-done.3.far_ref = f32[16,256]{1,0:T(8,128)S(1)} collective-permute-done((f32[16,256]{1,0:T(8,128)S(1)}, f32[16,256]{1,0:T(8,128)S(1)}, u32[]{:S(2)}, u32[]{:S(2)}) %collective-permute-start.3) | collective-permute-done | bytes 16416 | tf_op jit(solution)/shard_map/ppermute | solution.py:746
  84.7 11.4 %all_to_all.36.parts_ref = bf16[16,16,256]{2,1,0:T(8,128)(2,1)S(1)} all-to-all(bf16[16,16,256]{2,1,0:T(8,128)(2,1)S(1)} %shard_map.113), channel_id=1, replica_groups=mesh['dp'=16,'tensor'=8] {'dp'}, dimensions={0} | all-to-all | bytes 262144 | tf_op jit(solution)/shard_map/all_to_all | solution.py:729
  96.1 6.0 %shard_map.114 = f32[16,256]{1,0:T(8,128)S(1)} custom-call(bf16[16,1024,256]{2,1,0:T(8,128)(2,1)} %get-tuple-element.37.expo_hbm, bf16[16,16,256]{2,1,0:T(8,128)(2,1)S(1)} %all_to_all.36.parts_ref, f32[16,256]{1,0:T(8,128)S(1)} %get-tuple-element.39.live_ref), custom_call_target="tpu_custom_call" | custom-call | tf_op jit(solution)/shard_map/pallas_call | solution.py:39
  102.1 2.9 %collective-permute-start.5 = (f32[16,256]{1,0:T(8,128)S(1)}, f32[16,256]{1,0:T(8,128)S(1)}, u32[]{:S(2)}, u32[]{:S(2)}) collective-permute-start(f32[16,256]{1,0:T(8,128)S(1)} %shard_map.114), channel_id=1, source_target_pairs={{0,1},{1,0},{2,3},{3,2},{4,5},{5,4},{6,7},{7,6},{8,9},{9,8},{10,11... | collective-permute-start | bytes 49160 | tf_op jit(solution)/shard_map/ppermute | solution.py:734
  111.1 10.4 %all_to_all.37.parts_ref = bf16[16,16,256]{2,1,0:T(8,128)(2,1)S(1)} all-to-all(bf16[16,16,256]{2,1,0:T(8,128)(2,1)S(1)} %shard_map.115), channel_id=1, replica_groups=mesh['dp'=16,'tensor'=8] {'dp'}, dimensions={0} | all-to-all | bytes 262144 | tf_op jit(solution)/shard_map/all_to_all | solution.py:729
  121.5 8.2 %shard_map.116 = (bf16[16,272,128]{2,1,0:T(8,128)(2,1)S(1)}, bf16[16,272,128]{2,1,0:T(8,128)(2,1)S(1)}, f32[1024,128]{1,0:T(8,128)}) custom-call(s32[2]{0:T(128)S(1)} %pad_add_fusion.at_ref, bf16[16,1024,256]{2,1,0:T(8,128)(2,1)} %get-tuple-element.37.expo_hbm, bf16[16,16,256]{2,1,0:T(8,128)(2,1)S(1)} %all_to_all.37.parts_ref, ...), custom_call_target="tpu_custom_call" | custom-call | tf_op jit(solution)/shard_map/pallas_call | solution.py:39
  129.8 2.7 %collective-permute-start.9 = (bf16[16,272,128]{2,1,0:T(8,128)(2,1)S(1)}, bf16[16,272,128]{2,1,0:T(8,128)(2,1)S(1)}, u32[]{:S(2)}, u32[]{:S(2)}) collective-permute-start(bf16[16,272,128]{2,1,0:T(8,128)(2,1)S(1)} %get-tuple-element.42), channel_id=1, source_target_pairs={{0,1},{1,0},{2,3},{3,2},{4,5},{5,4},{6,7},{7,6},{8,9},{9,8},{10,11... | collective-permute-start | bytes 3342344 | tf_op jit(solution)/shard_map/ppermute | solution.py:734
  132.5 2.4 collective-permute-done.9
  136.2 9.2 %shard_map.122 = (bf16[16,1024,256]{2,1,0:T(8,128)(2,1)}, bf16[16,272,128]{2,1,0:T(8,128)(2,1)S(1)}, bf16[16,272,128]{2,1,0:T(8,128)(2,1)}) custom-call(s32[2]{0:T(128)S(1)} %pad_add_fusion.at_ref, bf16[1024,256]{1,0:T(8,128)(2,1)S(1)} %copy-done.6, bf16[256,1024]{1,0:T(8,128)(2,1)S(1)} %copy-done.2, bf16[16,256,256]{2,1,0:T(8,128)(2,1)} %bitcast.8), custom_call_target="tpu_custom_call" | custom-call | tf_op jit(solution)/shard_map/pallas_call | solution.py:39
  145.8 3.7 %all-to-all-start.3 = ((bf16[16,272,128]{2,1,0:T(8,128)(2,1)}), bf16[16,272,128]{2,1,0:T(8,128)(2,1)S(1)}, u32[]{:S(2)}, u32[]{:S(2)}) async-start(bf16[16,272,128]{2,1,0:T(8,128)(2,1)} %add_convert_fusion.1), calls=%async_computation.3 | async-start | bytes 2228224 | tf_op jit(solution)/shard_map/all_to_all | solution.py:729
  149.6 2.5 %add_convert_fusion = bf16[16,272,128]{2,1,0:T(8,128)(2,1)} fusion(bf16[16,272,128]{2,1,0:T(8,128)(2,1)} %collective-permute-done.15, bf16[16,272,128]{2,1,0:T(8,128)(2,1)S(1)} %get-tuple-element.48), kind=kLoop, calls=%fused_computation | loop fusion | flops 2228224 | bytes 3342336 | tf_op jit(solution)/shard_map/convert_element_type | solution.py:756
  152.1 16.8 %all-to-all-done.3.parts_hbm = bf16[16,272,128]{2,1,0:T(8,128)(2,1)S(1)} async-done(((bf16[16,272,128]{2,1,0:T(8,128)(2,1)}), bf16[16,272,128]{2,1,0:T(8,128)(2,1)S(1)}, u32[]{:S(2)}, u32[]{:S(2)}) %all-to-all-start.3) | async-done | bytes 1114144 | tf_op jit(solution)/shard_map/all_to_all | solution.py:729
  168.9 3.7 %all-to-all-start.4 = ((bf16[16,272,128]{2,1,0:T(8,128)(2,1)}), bf16[16,272,128]{2,1,0:T(8,128)(2,1)S(1)}, u32[]{:S(2)}, u32[]{:S(2)}) async-start(bf16[16,272,128]{2,1,0:T(8,128)(2,1)} %add_convert_fusion), calls=%async_computation.4 | async-start | bytes 2228224 | tf_op jit(solution)/shard_map/all_to_all | solution.py:729
  177.0 12.3 %all-to-all-done.4.parts_hbm = bf16[16,272,128]{2,1,0:T(8,128)(2,1)S(1)} async-done(((bf16[16,272,128]{2,1,0:T(8,128)(2,1)}), bf16[16,272,128]{2,1,0:T(8,128)(2,1)S(1)}, u32[]{:S(2)}, u32[]{:S(2)}) %all-to-all-start.4) | async-done | bytes 1114144 | tf_op jit(solution)/shard_map/all_to_all | solution.py:729
  193.7 3.6 %collective-permute-start.13 = (f32[1,272,128]{2,1,0:T(8,128)S(1)}, f32[1,272,128]{2,1,0:T(8,128)S(1)}, u32[]{:S(2)}, u32[]{:S(2)}) collective-permute-start(f32[1,272,128]{2,1,0:T(8,128)S(1)} %add_add_fusion.1.pull_ref), channel_id=1, source_target_pairs={{0,1},{1,0},{2,3},{3,2},{4,5},{5,4},{6,7},{7,6},{8,9},{9,8},{10,11... | collective-permute-start | bytes 417800 | tf_op jit(solution)/shard_map/ppermute | solution.py:734
  198.2 3.9 %collective-permute-start.19 = (f32[1,272,128]{2,1,0:T(8,128)S(1)}, f32[1,272,128]{2,1,0:T(8,128)S(1)}, u32[]{:S(2)}, u32[]{:S(2)}) collective-permute-start(f32[1,272,128]{2,1,0:T(8,128)S(1)} %add_add_fusion.push_ref), channel_id=1, source_target_pairs={{0,1},{1,0},{2,3},{3,2},{4,5},{5,4},{6,7},{7,6},{8,9},{9,8},{10,11... | collective-permute-start | bytes 417800 | tf_op jit(solution)/shard_map/ppermute | solution.py:734
  203.2 4.6 %shard_map.124 = (bf16[16,128,256]{2,1,0:T(8,128)(2,1)}, bf16[256,1024]{1,0:T(8,128)(2,1)}, f32[1,4]{1,0:T(1,128)}) custom-call(s32[2]{0:T(128)S(1)} %pad_add_fusion.at_ref, f32[1,272,128]{2,1,0:T(8,128)S(1)} %add_add_fusion.1.pull_ref, f32[1,272,128]{2,1,0:T(8,128)S(1)} %collective-permute-done.13.pull_other_ref, f32[1,272,128]{2,1,0:T(8,128)S(1)} %add_add_fusion.push_ref, ...), custom_call_target="tpu_custom_call" | custom-call | tf_op jit(solution)/shard_map/pallas_call | solution.py:39
  207.8 3.8 %all-to-all-start.5 = ((bf16[16,128,256]{2,1,0:T(8,128)(2,1)}), bf16[16,128,256]{2,1,0:T(8,128)(2,1)S(1)}, u32[]{:S(2)}, u32[]{:S(2)}) async-start(bf16[16,128,256]{2,1,0:T(8,128)(2,1)} %get-tuple-element.55), calls=%async_computation.5 | async-start | bytes 2097152 | tf_op jit(solution)/shard_map/all_to_all | solution.py:729
  211.7 3.8 %shard_map.125.rows_ref = bf16[256,1536]{1,0:T(8,128)(2,1)} custom-call(bf16[256,1024]{1,0:T(8,128)(2,1)S(1)} %copy-done.3, bf16[16,112,1024]{2,1,0:T(8,128)(2,1)} %bitcast.7), custom_call_target="tpu_custom_call" | custom-call | tf_op jit(solution)/shard_map/pallas_call | solution.py:39
  215.9 2.1 collective-permute-done.20.other_ref
  221.3 7.2 %all-to-all-done.5.got_hbm = bf16[16,128,256]{2,1,0:T(8,128)(2,1)S(1)} async-done(((bf16[16,128,256]{2,1,0:T(8,128)(2,1)}), bf16[16,128,256]{2,1,0:T(8,128)(2,1)S(1)}, u32[]{:S(2)}, u32[]{:S(2)}) %all-to-all-start.5) | async-done | bytes 1048608 | tf_op jit(solution)/shard_map/all_to_all | solution.py:729
  229.9 5.2 %all-to-all-start.6 = ((bf16[8,112,256]{2,1,0:T(8,128)(2,1)}), bf16[8,112,256]{2,1,0:T(8,128)(2,1)S(1)}, u32[]{:S(2)}, u32[]{:S(2)}) async-start(bf16[8,112,256]{2,1,0:T(8,128)(2,1)} %shard_map.127), calls=%async_computation.6 | async-start | bytes 917504 | tf_op jit(solution)/shard_map/all_to_all | solution.py:729
  235.1 9.3 %shard_map.129 = f32[256,1024]{1,0:T(8,128)} custom-call(bf16[16,1024,256]{2,1,0:T(8,128)(2,1)} %get-tuple-element.37.expo_hbm, bf16[16,1024,256]{2,1,0:T(8,128)(2,1)} %get-tuple-element.61.raised_hbm, f32[1024,128]{1,0:T(8,128)} %get-tuple-element.62.scale_hbm, bf16[16,128,256]{2,1,0:T(8,128)(2,1)S(1)} %all-to-all-done.5.got_hbm, ...), custom_call_target="tpu_custom_call" | custom-call | tf_op jit(solution)/shard_map/pallas_call | solution.py:39
  (76 shorter events, 33.0 us)
Async XLA Ops:
  7.2 61.1 %all-gather.3.cloned.1.call-start = ((), (), s32[]{:S(2)}) async-start(), calls=%async_computation.7 | async-start | bytes 3899392 | tf_op jit(solution)/shard_map/all_gather | solution.py:810
  9.9 126.2 %all-gather.5.cloned.1.call-start = ((), (), s32[]{:S(2)}) async-start(), calls=%async_computation.8 | async-start | bytes 2228224 | tf_op jit(solution)/shard_map/all_gather | solution.py:870
  13.0 29.5 %copy-start.1 = (bf16[256,1024]{1,0:T(8,128)(2,1)S(1)}, bf16[256,1024]{1,0:T(8,128)(2,1)}, u32[]{:S(2)}) copy-start(bf16[256,1024]{1,0:T(8,128)(2,1)} %proto_hbm.1) | copy-start | bytes 1572868
  13.0 29.5 %copy-start.5 = (bf16[256,1024]{1,0:T(8,128)(2,1)S(1)}, bf16[256,1024]{1,0:T(8,128)(2,1)}, u32[]{:S(2)}) copy-start(bf16[256,1024]{1,0:T(8,128)(2,1)} %teacher_ref.1) | copy-start | bytes 1572868
  39.9 8.0 %collective-permute-start = (bf16[16,128,256]{2,1,0:T(8,128)(2,1)S(1)}, bf16[16,128,256]{2,1,0:T(8,128)(2,1)S(1)}, u32[]{:S(2)}, u32[]{:S(2)}) collective-permute-start(bf16[16,128,256]{2,1,0:T(8,128)(2,1)S(1)} %all_to_all.35.own_hbm), channel_id=1, source_target_pairs={{0,1},{1,0},{2,3},{3,2},{4,5},{5,4},{6,7},{7,6},{8,9},{9,8},{10,11... | collective-permute-start | bytes 3145736 | tf_op jit(solution)/shard_map/ppermute | solution.py:734
  73.5 2.4 collective-permute-start.14
  76.7 1.3 collective-permute-start.1
  78.0 3.8 %collective-permute-start.4 = (f32[16,256]{1,0:T(8,128)S(1)}, f32[16,256]{1,0:T(8,128)S(1)}, u32[]{:S(2)}, u32[]{:S(2)}) collective-permute-start(f32[16,256]{1,0:T(8,128)S(1)} %add.36.own_ref), channel_id=1, source_target_pairs={{0,6},{1,7},{2,4},{3,5},{4,2},{5,3},{6,0},{7,1},{8,14},{9,15},{10,... | collective-permute-start | bytes 49160 | tf_op jit(solution)/shard_map/ppermute | solution.py:746
  80.6 4.1 %collective-permute-start.3 = (f32[16,256]{1,0:T(8,128)S(1)}, f32[16,256]{1,0:T(8,128)S(1)}, u32[]{:S(2)}, u32[]{:S(2)}) collective-permute-start(f32[16,256]{1,0:T(8,128)S(1)} %add.36.own_ref), channel_id=1, source_target_pairs={{0,4},{1,5},{2,6},{3,7},{4,0},{5,1},{6,2},{7,3},{8,12},{9,13},{10,... | collective-permute-start | bytes 49160 | tf_op jit(solution)/shard_map/ppermute | solution.py:746
  81.0 3.7 %collective-permute-start.2 = (f32[16,256]{1,0:T(8,128)S(1)}, f32[16,256]{1,0:T(8,128)S(1)}, u32[]{:S(2)}, u32[]{:S(2)}) collective-permute-start(f32[16,256]{1,0:T(8,128)S(1)} %add.36.own_ref), channel_id=1, source_target_pairs={{0,2},{1,3},{2,0},{3,1},{4,6},{5,7},{6,4},{7,5},{8,10},{9,11},{10,... | collective-permute-start | bytes 49160 | tf_op jit(solution)/shard_map/ppermute | solution.py:746
  96.1 25.4 %copy-start.2 = (bf16[256,1024]{1,0:T(8,128)(2,1)S(1)}, bf16[256,1024]{1,0:T(8,128)(2,1)}, u32[]{:S(2)}) copy-start(bf16[256,1024]{1,0:T(8,128)(2,1)} %get-tuple-element.40.cols_ref) | copy-start | bytes 1572868
  102.1 3.8 %collective-permute-start.5 = (f32[16,256]{1,0:T(8,128)S(1)}, f32[16,256]{1,0:T(8,128)S(1)}, u32[]{:S(2)}, u32[]{:S(2)}) collective-permute-start(f32[16,256]{1,0:T(8,128)S(1)} %shard_map.114), channel_id=1, source_target_pairs={{0,1},{1,0},{2,3},{3,2},{4,5},{5,4},{6,7},{7,6},{8,9},{9,8},{10,11... | collective-permute-start | bytes 49160 | tf_op jit(solution)/shard_map/ppermute | solution.py:734
  105.9 4.2 %collective-permute-start.8 = (f32[16,256]{1,0:T(8,128)S(1)}, f32[16,256]{1,0:T(8,128)S(1)}, u32[]{:S(2)}, u32[]{:S(2)}) collective-permute-start(f32[16,256]{1,0:T(8,128)S(1)} %add.37.own_ref), channel_id=1, source_target_pairs={{0,6},{1,7},{2,4},{3,5},{4,2},{5,3},{6,0},{7,1},{8,14},{9,15},{10,... | collective-permute-start | bytes 49160 | tf_op jit(solution)/shard_map/ppermute | solution.py:746
  107.0 4.1 %collective-permute-start.7 = (f32[16,256]{1,0:T(8,128)S(1)}, f32[16,256]{1,0:T(8,128)S(1)}, u32[]{:S(2)}, u32[]{:S(2)}) collective-permute-start(f32[16,256]{1,0:T(8,128)S(1)} %add.37.own_ref), channel_id=1, source_target_pairs={{0,4},{1,5},{2,6},{3,7},{4,0},{5,1},{6,2},{7,3},{8,12},{9,13},{10,... | collective-permute-start | bytes 49160 | tf_op jit(solution)/shard_map/ppermute | solution.py:746
  107.7 3.4 %collective-permute-start.6 = (f32[16,256]{1,0:T(8,128)S(1)}, f32[16,256]{1,0:T(8,128)S(1)}, u32[]{:S(2)}, u32[]{:S(2)}) collective-permute-start(f32[16,256]{1,0:T(8,128)S(1)} %add.37.own_ref), channel_id=1, source_target_pairs={{0,2},{1,3},{2,0},{3,1},{4,6},{5,7},{6,4},{7,5},{8,10},{9,11},{10,... | collective-permute-start | bytes 49160 | tf_op jit(solution)/shard_map/ppermute | solution.py:746
  129.8 5.1 %collective-permute-start.9 = (bf16[16,272,128]{2,1,0:T(8,128)(2,1)S(1)}, bf16[16,272,128]{2,1,0:T(8,128)(2,1)S(1)}, u32[]{:S(2)}, u32[]{:S(2)}) collective-permute-start(bf16[16,272,128]{2,1,0:T(8,128)(2,1)S(1)} %get-tuple-element.42), channel_id=1, source_target_pairs={{0,1},{1,0},{2,3},{3,2},{4,5},{5,4},{6,7},{7,6},{8,9},{9,8},{10,11... | collective-permute-start | bytes 3342344 | tf_op jit(solution)/shard_map/ppermute | solution.py:734
  145.4 4.2 %collective-permute-start.15 = (bf16[16,272,128]{2,1,0:T(8,128)(2,1)}, bf16[16,272,128]{2,1,0:T(8,128)(2,1)}, u32[]{:S(2)}, u32[]{:S(2)}) collective-permute-start(bf16[16,272,128]{2,1,0:T(8,128)(2,1)} %get-tuple-element.49), channel_id=1, source_target_pairs={{0,1},{1,0},{2,3},{3,2},{4,5},{5,4},{6,7},{7,6},{8,9},{9,8},{10,11... | collective-permute-start | bytes 3342344 | tf_op jit(solution)/shard_map/ppermute | solution.py:734
  145.8 23.0 %all-to-all-start.3 = ((bf16[16,272,128]{2,1,0:T(8,128)(2,1)}), bf16[16,272,128]{2,1,0:T(8,128)(2,1)S(1)}, u32[]{:S(2)}, u32[]{:S(2)}) async-start(bf16[16,272,128]{2,1,0:T(8,128)(2,1)} %add_convert_fusion.1), calls=%async_computation.3 | async-start | bytes 2228224 | tf_op jit(solution)/shard_map/all_to_all | solution.py:729
  168.9 20.4 %all-to-all-start.4 = ((bf16[16,272,128]{2,1,0:T(8,128)(2,1)}), bf16[16,272,128]{2,1,0:T(8,128)(2,1)S(1)}, u32[]{:S(2)}, u32[]{:S(2)}) async-start(bf16[16,272,128]{2,1,0:T(8,128)(2,1)} %add_convert_fusion), calls=%async_computation.4 | async-start | bytes 2228224 | tf_op jit(solution)/shard_map/all_to_all | solution.py:729
  173.6 29.6 %copy-start.7 = (f32[8,256]{1,0:T(8,128)S(1)}, f32[8,256]{1,0:T(8,128)}, u32[]{:S(2)}) copy-start(f32[8,256]{1,0:T(8,128)} %get-tuple-element.51.member_ref) | copy-start | bytes 24580
  173.6 29.6 %copy-start.8 = (bf16[16,256]{1,0:T(8,128)(2,1)S(1)}, bf16[16,256]{1,0:T(8,128)(2,1)}, u32[]{:S(2)}) copy-start(bf16[16,256]{1,0:T(8,128)(2,1)} %get-tuple-element.50.mine_ref) | copy-start | bytes 24580
  173.7 19.4 %collective-permute-start.12 = (bf16[1,272,128]{2,1,0:T(8,128)(2,1)}, bf16[1,272,128]{2,1,0:T(8,128)(2,1)S(1)}, u32[]{:S(2)}, u32[]{:S(2)}) collective-permute-start(bf16[1,272,128]{2,1,0:T(8,128)(2,1)} %shard_map.117), channel_id=1, source_target_pairs={{0,6},{1,7},{2,4},{3,5},{4,2},{5,3},{6,0},{7,1},{8,14},{9,15},{10,... | collective-permute-start | bytes 208904 | tf_op jit(solution)/shard_map/ppermute | solution.py:746
  175.5 18.1 %collective-permute-start.11 = (bf16[1,272,128]{2,1,0:T(8,128)(2,1)}, bf16[1,272,128]{2,1,0:T(8,128)(2,1)S(1)}, u32[]{:S(2)}, u32[]{:S(2)}) collective-permute-start(bf16[1,272,128]{2,1,0:T(8,128)(2,1)} %shard_map.117), channel_id=1, source_target_pairs={{0,4},{1,5},{2,6},{3,7},{4,0},{5,1},{6,2},{7,3},{8,12},{9,13},{10,... | collective-permute-start | bytes 208904 | tf_op jit(solution)/shard_map/ppermute | solution.py:746
  176.4 17.2 %collective-permute-start.10 = (bf16[1,272,128]{2,1,0:T(8,128)(2,1)}, bf16[1,272,128]{2,1,0:T(8,128)(2,1)S(1)}, u32[]{:S(2)}, u32[]{:S(2)}) collective-permute-start(bf16[1,272,128]{2,1,0:T(8,128)(2,1)} %shard_map.117), channel_id=1, source_target_pairs={{0,2},{1,3},{2,0},{3,1},{4,6},{5,7},{6,4},{7,5},{8,10},{9,11},{10,... | collective-permute-start | bytes 208904 | tf_op jit(solution)/shard_map/ppermute | solution.py:746
  190.3 7.0 %collective-permute-start.18 = (bf16[1,272,128]{2,1,0:T(8,128)(2,1)}, bf16[1,272,128]{2,1,0:T(8,128)(2,1)S(1)}, u32[]{:S(2)}, u32[]{:S(2)}) collective-permute-start(bf16[1,272,128]{2,1,0:T(8,128)(2,1)} %shard_map.123), channel_id=1, source_target_pairs={{0,6},{1,7},{2,4},{3,5},{4,2},{5,3},{6,0},{7,1},{8,14},{9,15},{10,... | collective-permute-start | bytes 208904 | tf_op jit(solution)/shard_map/ppermute | solution.py:746
  192.2 5.1 %collective-permute-start.17 = (bf16[1,272,128]{2,1,0:T(8,128)(2,1)}, bf16[1,272,128]{2,1,0:T(8,128)(2,1)S(1)}, u32[]{:S(2)}, u32[]{:S(2)}) collective-permute-start(bf16[1,272,128]{2,1,0:T(8,128)(2,1)} %shard_map.123), channel_id=1, source_target_pairs={{0,4},{1,5},{2,6},{3,7},{4,0},{5,1},{6,2},{7,3},{8,12},{9,13},{10,... | collective-permute-start | bytes 208904 | tf_op jit(solution)/shard_map/ppermute | solution.py:746
  193.1 4.2 %collective-permute-start.16 = (bf16[1,272,128]{2,1,0:T(8,128)(2,1)}, bf16[1,272,128]{2,1,0:T(8,128)(2,1)S(1)}, u32[]{:S(2)}, u32[]{:S(2)}) collective-permute-start(bf16[1,272,128]{2,1,0:T(8,128)(2,1)} %shard_map.123), channel_id=1, source_target_pairs={{0,2},{1,3},{2,0},{3,1},{4,6},{5,7},{6,4},{7,5},{8,10},{9,11},{10,... | collective-permute-start | bytes 208904 | tf_op jit(solution)/shard_map/ppermute | solution.py:746
  193.7 8.5 %collective-permute-start.13 = (f32[1,272,128]{2,1,0:T(8,128)S(1)}, f32[1,272,128]{2,1,0:T(8,128)S(1)}, u32[]{:S(2)}, u32[]{:S(2)}) collective-permute-start(f32[1,272,128]{2,1,0:T(8,128)S(1)} %add_add_fusion.1.pull_ref), channel_id=1, source_target_pairs={{0,1},{1,0},{2,3},{3,2},{4,5},{5,4},{6,7},{7,6},{8,9},{9,8},{10,11... | collective-permute-start | bytes 417800 | tf_op jit(solution)/shard_map/ppermute | solution.py:734
  198.2 4.9 %collective-permute-start.19 = (f32[1,272,128]{2,1,0:T(8,128)S(1)}, f32[1,272,128]{2,1,0:T(8,128)S(1)}, u32[]{:S(2)}, u32[]{:S(2)}) collective-permute-start(f32[1,272,128]{2,1,0:T(8,128)S(1)} %add_add_fusion.push_ref), channel_id=1, source_target_pairs={{0,1},{1,0},{2,3},{3,2},{4,5},{5,4},{6,7},{7,6},{8,9},{9,8},{10,11... | collective-permute-start | bytes 417800 | tf_op jit(solution)/shard_map/ppermute | solution.py:734
  207.8 20.7 %all-to-all-start.5 = ((bf16[16,128,256]{2,1,0:T(8,128)(2,1)}), bf16[16,128,256]{2,1,0:T(8,128)(2,1)S(1)}, u32[]{:S(2)}, u32[]{:S(2)}) async-start(bf16[16,128,256]{2,1,0:T(8,128)(2,1)} %get-tuple-element.55), calls=%async_computation.5 | async-start | bytes 2097152 | tf_op jit(solution)/shard_map/all_to_all | solution.py:729
  215.5 2.6 %collective-permute-start.20 = (bf16[256,1536]{1,0:T(8,128)(2,1)}, bf16[256,1536]{1,0:T(8,128)(2,1)S(1)}, u32[]{:S(2)}, u32[]{:S(2)}) collective-permute-start(bf16[256,1536]{1,0:T(8,128)(2,1)} %shard_map.125.rows_ref), channel_id=1, source_target_pairs={{0,1},{1,0},{2,3},{3,2},{4,5},{5,4},{6,7},{7,6},{8,9},{9,8},{10,11... | collective-permute-start | bytes 2359304 | tf_op jit(solution)/shard_map/ppermute | solution.py:734
  229.9 14.6 %all-to-all-start.6 = ((bf16[8,112,256]{2,1,0:T(8,128)(2,1)}), bf16[8,112,256]{2,1,0:T(8,128)(2,1)S(1)}, u32[]{:S(2)}, u32[]{:S(2)}) async-start(bf16[8,112,256]{2,1,0:T(8,128)(2,1)} %shard_map.127), calls=%async_computation.6 | async-start | bytes 917504 | tf_op jit(solution)/shard_map/all_to_all | solution.py:729
  (6 other events, 29.8 us)
Sparse Core Ops, SparseCore 0:
  10.1 58.1 all-gather.2
  76.8 42.7 all-gather.4
